TPU v7x, 128 devices: a whole 4x4x4 slice. The times are simulated.
128 devices in a mesh: cand: 8 (over y, core), ctx: 16 (over x, z).
Axes of the slice: x: 4, y: 4, z: 4, core: 2. Of those that a mesh axis runs over, the one named last changes fastest.
Arguments:
- query_matrix: bfloat16 [8, 2048, 1536], P('cand', 'ctx'), as said below
- key_matrix: bfloat16 [8, 2048, 512], P('cand', 'ctx'), as said below
- value_matrix: bfloat16 [8, 2048, 512], P('cand', 'ctx'), may hold values from -6 to 6
- output_gradient: bfloat16 [8, 2048, 1536], P('cand', 'ctx'), may hold values from -6 to 6
- parent: int32 [8], replicated, may hold values from 0 to 7, as said below
- seg_depth: int32 [8], replicated, may hold values from 0 to 2, as said below
- block_mask: int32 [8, 16, 16], P('cand'), may hold values 0 or 1
Outputs:
- attended: bfloat16 [8, 2048, 1536], P('cand', 'ctx')
- query_grad: bfloat16 [8, 2048, 1536], P('cand', 'ctx')
- key_grad: bfloat16 [8, 2048, 512], P('cand', 'ctx')
- value_grad: bfloat16 [8, 2048, 512], P('cand', 'ctx')
Inputs may be any that keep to these rules, and one draw needn't show every extreme that they name: `query_matrix`: query entries lie within -9 to 9. `key_matrix`: key entries lie within -6 to 6. parent[s] is the segment that segment s continues; exactly one root segment is its own parent; a child of the root has the root as parent, every other segment has a child of the root as parent. seg_depth[s] counts the ancestors of segment s: 0 for the root only, 1 for the root's children, 2 for all others.
All inputs are finite; a program needn't handle non-finite values. No bound on the sum of `block_mask` on one device may be relied on, other than what follows from the above.
Results may differ from a plain program's by a relative error of at most 0.018.
Values may be sent and summed in bfloat16 or wider, within the bound.
No kernel may reach another device: no remote copies, remote signals or barrier semaphores. Data moves between devices by JAX's collectives and lax.ppermute only.
A program may use at most 192 MiB of HBM per device.

v0:
```python
import jax
import jax.numpy as jnp
from jax import lax
from jax.sharding import PartitionSpec as P

HEAD_SIZE = 128
BLOCK = 128
VISIBLE_SLOTS = 3


negative_big = -1e30


def block_rows(mask_member, query_pos, block_len):
    nblocks = mask_member.shape[0]
    onehot = (query_pos[:, None] // block_len == jnp.arange(nblocks)[None, :]).astype(jnp.int32)
    return jnp.sum(onehot[:, :, None] * mask_member[None, :, :], axis=1)


def visible(query_pos, key_pos, rows_member, live_member, block_len):
    nblocks = rows_member.shape[1]
    key_block = key_pos // block_len
    onehot = (key_block[:, None] == jnp.arange(nblocks)[None, :]).astype(jnp.int32)
    allowed = jnp.sum(rows_member[:, None, :] * onehot[None, :, :], axis=2)
    same_block = key_block[None, :] == (query_pos // block_len)[:, None]
    own_slot = (key_pos[None, :] <= query_pos[:, None]) & (same_block | (allowed > 0))
    far_slots = jnp.broadcast_to(
        live_member[None, 1:, None],
        (query_pos.shape[0], live_member.shape[0] - 1, key_pos.shape[0]),
    )
    return jnp.concatenate([own_slot[:, None, :], far_slots], axis=1)


def head_scores(query_head, key_head, seen_mask, scaling):
    raw_scores = (
        jnp.einsum("qgd,lkd->gqlk", query_head, key_head, preferred_element_type=jnp.float32)
        * scaling
    )
    return jnp.where(seen_mask[None], raw_scores, negative_big)


def per_device(
    query_matrix, key_matrix, value_matrix, output_gradient, parent, seg_depth, block_mask
):
    seg_dev, tok_dev, query_width = query_matrix.shape
    kv_width = key_matrix.shape[2]
    heads_kv = kv_width // HEAD_SIZE
    query_group_width = query_width // kv_width
    seg_len = tok_dev * lax.axis_size("ctx")
    scaling = HEAD_SIZE ** (-0.5)
    query_pos = lax.axis_index("ctx") * tok_dev + jnp.arange(tok_dev, dtype=jnp.int32)
    own_ids = lax.axis_index("cand") * seg_dev + jnp.arange(seg_dev, dtype=jnp.int32)
    first_up = parent[own_ids]
    lineage_table = jnp.stack([own_ids, first_up, parent[first_up]], axis=1)
    live_slots = jnp.arange(VISIBLE_SLOTS, dtype=jnp.int32)[None, :] <= seg_depth[own_ids][:, None]
    key_value = jnp.concatenate([key_matrix, value_matrix], axis=2)
    tree_rows = lax.all_gather(key_value, "cand", axis=0, tiled=True)
    picked = tree_rows[lineage_table]
    mask_rows = block_rows(block_mask[0], query_pos, BLOCK)
    head_width = query_group_width * HEAD_SIZE
    full_rows = lax.all_gather(picked, "ctx", axis=2, tiled=True)
    key_pos_all = jnp.arange(seg_len, dtype=jnp.int32)
    seen_mask = visible(query_pos, key_pos_all, mask_rows, live_slots[0], BLOCK)
    out_heads = []
    query_heads = []
    key_heads = []
    value_heads = []
    for head_index in range(heads_kv):
        query_head = query_matrix[0][
            :, head_index * head_width : (head_index + 1) * head_width
        ].reshape(tok_dev, query_group_width, HEAD_SIZE)
        cotan_head = output_gradient[0][
            :, head_index * head_width : (head_index + 1) * head_width
        ].reshape(tok_dev, query_group_width, HEAD_SIZE)
        key_head = full_rows[0][:, :, head_index * HEAD_SIZE : (head_index + 1) * HEAD_SIZE]
        value_head = full_rows[0][
            :, :, kv_width + head_index * HEAD_SIZE : kv_width + (head_index + 1) * HEAD_SIZE
        ]
        raw_scores = head_scores(query_head, key_head, seen_mask, scaling)
        row_max = jnp.max(raw_scores, axis=(2, 3))
        norm_head = row_max + jnp.log(
            jnp.sum(jnp.exp(raw_scores - row_max[:, :, None, None]), axis=(2, 3))
        )
        weights = jnp.where(seen_mask[None], jnp.exp(raw_scores - norm_head[:, :, None, None]), 0.0)
        weights_reduced = weights.astype(jnp.bfloat16)
        attended_head = jnp.einsum(
            "gqlk,lkd->qgd", weights_reduced, value_head, preferred_element_type=jnp.float32
        ).astype(jnp.bfloat16)
        row_delta = jnp.sum(
            cotan_head.astype(jnp.float32) * attended_head.astype(jnp.float32), axis=2
        ).T
        grad_weights = jnp.einsum(
            "qgd,lkd->gqlk", cotan_head, value_head, preferred_element_type=jnp.float32
        )
        grad_scores = (weights * (grad_weights - row_delta[:, :, None, None]) * scaling).astype(
            jnp.bfloat16
        )
        query_heads.append(
            jnp.einsum("gqlk,lkd->qgd", grad_scores, key_head, preferred_element_type=jnp.float32)
            .astype(jnp.bfloat16)
            .reshape(tok_dev, head_width)
        )
        key_heads.append(
            jnp.einsum("gqlk,qgd->lkd", grad_scores, query_head, preferred_element_type=jnp.float32)
        )
        value_heads.append(
            jnp.einsum(
                "gqlk,qgd->lkd", weights_reduced, cotan_head, preferred_element_type=jnp.float32
            )
        )
        out_heads.append(attended_head.reshape(tok_dev, head_width))
    attended_list = [jnp.concatenate(out_heads, axis=1)]
    query_list = [jnp.concatenate(query_heads, axis=1)]
    grads_list = [jnp.concatenate(key_heads + value_heads, axis=2)]
    slot_terms = jnp.stack(grads_list)
    slot_sums = lax.psum_scatter(
        slot_terms.astype(jnp.bfloat16), "ctx", scatter_dimension=2, tiled=True
    ).astype(jnp.float32)
    n_segments = tree_rows.shape[0]
    owner_map = (
        (lineage_table.reshape(-1)[None, :] == jnp.arange(n_segments, dtype=jnp.int32)[:, None])
        & live_slots.reshape(-1)[None, :]
    ).astype(jnp.float32)
    routed = jnp.dot(
        owner_map, slot_sums.reshape(seg_dev * VISIBLE_SLOTS, -1), precision=lax.Precision.HIGHEST
    ).reshape(n_segments, tok_dev, 2 * kv_width)
    tree_sums = lax.psum_scatter(
        routed.astype(jnp.bfloat16), "cand", scatter_dimension=0, tiled=True
    ).astype(jnp.float32)
    return (
        jnp.stack(attended_list),
        jnp.stack(query_list),
        tree_sums[:, :, :kv_width].astype(jnp.bfloat16),
        tree_sums[:, :, kv_width:].astype(jnp.bfloat16),
    )


def solution(mesh):
    in_specs = (
        P("cand", "ctx", None),
        P("cand", "ctx", None),
        P("cand", "ctx", None),
        P("cand", "ctx", None),
        P(),
        P(),
        P("cand", None, None),
    )
    out_specs = (
        P("cand", "ctx", None),
        P("cand", "ctx", None),
        P("cand", "ctx", None),
        P("cand", "ctx", None),
    )
    return jax.shard_map(
        per_device, mesh=mesh, in_specs=in_specs, out_specs=out_specs, check_vma=False
    )
```

profile of v0, /device:TPU:0, one launch (start us, length us, event | category | flops | bytes accessed | tf_op | source)
XLA Modules:
  0.0 440.4 jit_solution(17998624414436514958)
XLA Ops:
  7.2 1.7 pad_maximum_fusion
  9.0 1.3 dynamic-slice.6
  12.1 1.2 dynamic-slice.7
  13.4 1.3 fusion.76
  14.6 23.5 %all-gather.4.cloned.1.call-done = bf16[8,128,1024]{2,1,0:T(8,128)(2,1)} async-done(((bf16[1,128,1024]{2,1,0:T(8,128)(2,1)}), bf16[8,128,1024]{2,1,0:T(8,128)(2,1)}) %all-gather.4.cloned.1.call-update) | async-done | bytes 2097168 | tf_op jit(solution)/shard_map/all_gather | solution.py:57
  38.1 3.1 gather_fusion
  41.3 1.3 dynamic-slice.8
  42.7 0.8 multiply_reduce_fusion.5
  43.6 1.2 copy.156
  44.8 1.1 fusion.85
  45.9 0.1 copy.173
  46.0 0.1 copy.185
  46.1 0.1 copy.181
  46.3 0.1 copy.177
  46.4 3.1 multiply_reduce_fusion
  49.5 0.4 fusion.65
  50.0 0.4 copy.155
  50.4 0.7 iota_compare_fusion.5
  51.3 0.3 pad_add_fusion
  51.7 80.0 %all-gather.6.cloned.1.call-done = bf16[3,2048,1024]{2,1,0:T(8,128)(2,1)} async-done(((bf16[3,128,1024]{2,1,0:T(8,128)(2,1)}), bf16[3,2048,1024]{2,1,0:T(8,128)(2,1)}) %all-gather.6.cloned.1.call-update) | async-done | bytes 12582928 | tf_op jit(solution)/shard_map/all_gather | solution.py:61
  131.7 2.8 fusion.47
  134.5 6.4 %fusion.44 = f32[3,2048,128,3]{2,1,3,0:T(8,128)} fusion(bf16[128,3,128,1]{0,2,1,3:T(8,128)(2,1)S(1)} %bitcast.487, bf16[3,2048,1024]{2,1,0:T(8,128)(2,1)} %all-gather.6.cloned.1.call-done), kind=kOutput, calls=%fused_computation.80 | convolution fusion | flops 603979776 | bytes 11108352 | tf_op jit(solution)/shard_map/qgd,lkd->gqlk/dot_general | solution.py:36
  140.9 6.7 %fusion.16 = (f32[3,128]{1,0:T(4,128)S(1)}, f32[3,2048,128,3]{2,1,3,0:T(8,128)}) fusion(pred[128,3,2048]{0,2,1:T(8,128)(4,1)S(1)} %pad_add_fusion, bf16[128,3,128,1]{0,2,1,3:T(8,128)(2,1)S(1)} %bitcast.492, bf16[3,2048,1024]{2,1,0:T(8,128)(2,1)} %all-gather.6.cloned.1.call-done), kind=kOutput, calls=%fused_computation.34 | convolution fusion | flops 611057280 | bytes 11896320 | tf_op jit(solution)/shard_map/qgd,lkd->gqlk/dot_general | solution.py:36
  147.6 14.2 %exponential_reduce_fusion.3 = (f32[3,128]{1,0:T(4,128)S(1)}, f32[3,128]{1,0:T(4,128)S(1)}, f32[3,128]{1,0:T(4,128)S(1)}, f32[3,128]{1,0:T(4,128)S(1)}, f32[3,2048,128,3]{2,1,3,0:T(8,128)}) fusion(f32[3,2048,128,3]{2,1,3,0:T(8,128)} %get-tuple-element.63, f32[3,128]{1,0:T(4,128)S(1)} %get-tuple-element.62, pred[128,3,2048]{0,2,1:T(8,128)(4,1)S(1)} %pad_add_fusion, ...), kind=kOutput, calls=%fused_computation.29 | convolution fusion | flops 634649088 | bytes 40214016 | tf_op jit(solution)/shard_map/qgd,lkd->gqlk/dot_general | solution.py:36
  161.8 10.0 %exponential_reduce_fusion.2 = (f32[3,128]{1,0:T(4,128)S(1)}, f32[3,128]{1,0:T(4,128)S(1)}, f32[3,128]{1,0:T(4,128)S(1)}) fusion(f32[3,2048,128,3]{2,1,3,0:T(8,128)} %get-tuple-element.64, f32[3,128]{1,0:T(4,128)S(1)} %get-tuple-element.46, pred[128,3,2048]{0,2,1:T(8,128)(4,1)S(1)} %pad_add_fusion, f32[3,128]{1,0:T(4,128)S(1)} %get-tuple-element.47, ...), kind=kLoop, calls=%fused_computation.27 | loop fusion | flops 28310400 | bytes 29107200 | tf_op jit(solution)/shard_map/reduce_sum | solution.py:82
  171.9 4.7 %multiply_reduce_fusion.4 = (f32[128,3]{0,1:T(4,128)S(1)}, bf16[128,3,128]{2,0,1:T(8,128)(2,1)}) fusion(bf16[128,3,128]{0,2,1:T(8,128)(2,1)S(1)} %bitcast.500, f32[3,2048,128,3]{2,1,3,0:T(8,128)S(1)} %copy-done.12, f32[3,128]{1,0:T(4,128)S(1)} %log_add_fusion.3, pred[128,3,2048]{0,2,1:T(8,128)(4,1)S(1)} %pad_add_fusion, ...), kind=kOutput, calls=%fused_computation.110 | convolution fusion | flops 616021632 | bytes 11996160 | tf_op jit(solution)/shard_map/gqlk,lkd->qgd/dot_general | solution.py:86
  176.5 6.8 %fusion.11 = bf16[3,128,3,2048]{1,3,0,2:T(8,128)(2,1)} fusion(f32[3,2048,128,3]{2,1,3,0:T(8,128)S(1)} %copy-done.12, f32[3,128]{1,0:T(4,128)S(1)} %bitcast.515, f32[3,128]{1,0:T(4,128)S(1)} %log_add_fusion.3, pred[128,3,2048]{0,2,1:T(8,128)(4,1)S(1)} %pad_add_fusion, bf16[128,3,128,1]{0,2,1,3:T(8,128)(2,1)S(1)} %bitcast.501, ...), kind=kOutput, calls=%fused_computation.17 | convolution fusion | flops 622854144 | bytes 16616448 | tf_op jit(solution)/shard_map/qgd,lkd->gqlk/dot_general | solution.py:92
  183.3 5.1 %fusion.21 = bf16[1,3,2048,1024]{2,3,1,0:T(8,128)(2,1)} fusion(bf16[3,128,3,2048]{1,3,0,2:T(8,128)(2,1)} %fusion.11, bf16[128,3,128,1]{0,2,1,3:T(8,128)(2,1)S(1)} %bitcast.493), kind=kOutput, calls=%fused_computation.48 | convolution fusion | flops 604766208 | bytes 6389760 | tf_op jit(solution)/shard_map/gqlk,qgd->lkd/dot_general | solution.py:104
  188.4 7.6 %multiply_reduce_fusion.3 = (f32[128,3]{0,1:T(4,128)S(1)}, bf16[128,3,128]{2,0,1:T(8,128)(2,1)}) fusion(bf16[128,3,128]{0,2,1:T(8,128)(2,1)S(1)} %bitcast.503, f32[3,2048,128,3]{2,1,3,0:T(8,128)} %get-tuple-element.64, f32[3,128]{1,0:T(4,128)S(1)} %log_add_fusion.2, pred[128,3,2048]{0,2,1:T(8,128)(4,1)S(1)} %pad_add_fusion, ...), kind=kOutput, calls=%fused_computation.109 | convolution fusion | flops 616021632 | bytes 11996160 | tf_op jit(solution)/shard_map/gqlk,lkd->qgd/dot_general | solution.py:86
  196.0 8.2 %fusion.8 = bf16[3,128,3,2048]{1,3,0,2:T(8,128)(2,1)S(1)} fusion(f32[3,2048,128,3]{2,1,3,0:T(8,128)} %get-tuple-element.64, f32[3,128]{1,0:T(4,128)S(1)} %bitcast.516, f32[3,128]{1,0:T(4,128)S(1)} %log_add_fusion.2, pred[128,3,2048]{0,2,1:T(8,128)(4,1)} %copy-done.3, bf16[128,3,128,1]{0,2,1,3:T(8,128)(2,1)} %bitcast.504, ...), kind=kOutput, calls=%fused_computation.13 | convolution fusion | flops 622854144 | bytes 16616448 | tf_op jit(solution)/shard_map/qgd,lkd->gqlk/dot_general | solution.py:92
  204.1 2.7 fusion.23
  206.9 4.0 multiply_reduce_fusion.2
  210.9 5.8 %fusion.5 = bf16[3,128,3,2048]{1,3,0,2:T(8,128)(2,1)S(1)} fusion(f32[3,2048,128,3]{2,1,3,0:T(8,128)S(1)} %bitcast.483, f32[3,128]{1,0:T(4,128)S(1)} %bitcast.517, f32[3,128]{1,0:T(4,128)S(1)} %log_add_fusion.1, pred[128,3,2048]{0,2,1:T(8,128)(4,1)S(1)} %copy-done.4, bf16[128,3,128,1]{0,2,1,3:T(8,128)(2,1)S(1)} %bitcast.498, ...), kind=kOutput, calls=%fused_computation.9 | convolution fusion | flops 622854144 | bytes 16616448 | tf_op jit(solution)/shard_map/qgd,lkd->gqlk/dot_general | solution.py:92
  216.8 2.7 fusion.25
  219.5 4.6 %multiply_reduce_fusion.1 = (f32[128,3]{0,1:T(4,128)S(1)}, bf16[128,3,128]{2,0,1:T(8,128)(2,1)}) fusion(bf16[128,3,128]{0,2,1:T(8,128)(2,1)S(1)} %bitcast.494, f32[3,2048,128,3]{2,1,3,0:T(8,128)S(1)} %fusion.47, f32[3,128]{1,0:T(4,128)S(1)} %log_add_fusion, pred[128,3,2048]{0,2,1:T(8,128)(4,1)S(1)} %copy-done.4, ...), kind=kOutput, calls=%fused_computation.107 | convolution fusion | flops 616021632 | bytes 11996160 | tf_op jit(solution)/shard_map/gqlk,lkd->qgd/dot_general | solution.py:86
  224.1 5.5 %fusion.2 = bf16[3,128,3,2048]{1,3,0,2:T(8,128)(2,1)S(1)} fusion(f32[3,2048,128,3]{2,1,3,0:T(8,128)S(1)} %fusion.47, f32[3,128]{1,0:T(4,128)S(1)} %bitcast.518, f32[3,128]{1,0:T(4,128)S(1)} %log_add_fusion, pred[128,3,2048]{0,2,1:T(8,128)(4,1)S(1)} %copy-done.4, bf16[128,3,128,1]{0,2,1,3:T(8,128)(2,1)S(1)} %bitcast.495, ...), kind=kOutput, calls=%fused_computation.5 | convolution fusion | flops 622854144 | bytes 16616448 | tf_op jit(solution)/shard_map/qgd,lkd->gqlk/dot_general | solution.py:92
  229.6 2.7 fusion.27
  232.3 7.5 %fusion.29 = bf16[1,3,2048,1024]{2,3,1,0:T(8,128)(2,1)} fusion(bf16[1,3,2048,1024]{2,3,1,0:T(8,128)(2,1)} %fusion.27, bf16[128,3,128,1]{0,2,1,3:T(8,128)(2,1)S(1)} %bitcast.502, f32[3,2048,128,3]{2,1,3,0:T(8,128)} %get-tuple-element.63, f32[3,128]{1,0:T(4,128)S(1)} %log_add_fusion.3, pred[128,3,2048]{0,2,1:T(8,128)(4,1)S(1)} %copy-done.4), kind=kOutput, calls=%fused_computation.56 | convolution fusion | flops 616562688 | bytes 11896320 | tf_op jit(solution)/shard_map/gqlk,qgd->lkd/dot_general | solution.py:107
  239.8 7.4 %fusion.31 = bf16[1,3,2048,1024]{2,3,1,0:T(8,128)(2,1)} fusion(bf16[1,3,2048,1024]{2,3,1,0:T(8,128)(2,1)} %fusion.29, bf16[128,3,128,1]{0,2,1,3:T(8,128)(2,1)S(1)} %bitcast.505, f32[3,2048,128,3]{2,1,3,0:T(8,128)} %get-tuple-element.64, f32[3,128]{1,0:T(4,128)S(1)} %log_add_fusion.2, pred[128,3,2048]{0,2,1:T(8,128)(4,1)S(1)} %copy-done.4), kind=kOutput, calls=%fused_computation.58 | convolution fusion | flops 616562688 | bytes 11896320 | tf_op jit(solution)/shard_map/gqlk,qgd->lkd/dot_general | solution.py:107
  247.2 3.7 fusion.33
  250.9 3.9 fusion.35
  254.8 27.5 %copy.284 = bf16[1,3,2048,1024]{3,1,0,2:T(4,128)(2,1)} copy(bf16[1,3,2048,1024]{2,3,1,0:T(8,128)(2,1)} %fusion.35) | data formatting | bytes 25165824
  282.3 15.7 %copy.287 = bf16[256,8,3,1024]{3,1,2,0:T(8,128)(2,1)} copy(bf16[256,8,3,1024]{3,2,1,0:T(4,128)(2,1)} %bitcast.480) | data formatting | bytes 25165824
  298.1 0.8 iota_compare_fusion.4
  298.9 1.3 add_bitcast_fusion
  300.1 92.4 %reduce-scatter.7.cloned.1.call-done = bf16[128,3072]{1,0:T(8,128)(2,1)} async-done(((bf16[2048,3072]{1,0:T(8,128)(2,1)}), bf16[128,3072]{1,0:T(8,128)(2,1)}) %reduce-scatter.7.cloned.1.call-update) | async-done | bytes 786448
  392.5 2.7 reshape.727
  395.3 1.2 convolution_convert_fusion
  396.5 2.5 copy.203
  399.0 0.1 copy.171
  399.2 0.1 copy.170
  399.3 0.1 copy.172
  399.4 0.1 copy.169
  399.6 3.9 fusion.57
  403.4 0.1 copy.189
  403.5 3.9 fusion.63
  407.4 0.1 copy.192
  407.5 3.9 fusion.59
  411.4 0.1 copy.190
  411.5 4.0 fusion.61
  415.6 0.8 maximum_bitcast_fusion
  416.4 0.8 maximum_bitcast_fusion.1
  417.2 14.8 %reduce-scatter.5.cloned.1.call-done = bf16[1,128,1024]{2,1,0:T(8,128)(2,1)} async-done(((bf16[8,128,1024]{2,1,0:T(8,128)(2,1)}), bf16[1,128,1024]{2,1,0:T(8,128)(2,1)}) %reduce-scatter.5.cloned.1.call-update) | async-done | bytes 262160 | tf_op jit(solution)/shard_map/reduce_scatter | solution.py:127
  432.0 1.7 fusion.87
  (55 shorter events, 0.8 us)
Async XLA Ops:
  7.2 30.9 %all-gather.4.cloned.1.call-start = ((), (), s32[]{:S(2)}) async-start(), calls=%async_computation.2 | async-start | bytes 2359296 | tf_op jit(solution)/shard_map/all_gather | solution.py:57
  8.9 122.8 %all-gather.6.cloned.1.call-start = ((), (), s32[]{:S(2)}) async-start(), calls=%async_computation.4 | async-start | bytes 13369344 | tf_op jit(solution)/shard_map/all_gather | solution.py:61
  41.3 351.3 %reduce-scatter.7.cloned.1.call-start = ((), (), s32[]{:S(2)}) async-start(), calls=%async_computation.5 | async-start | bytes 13369344
  46.0 130.5 %copy-start.5 = (bf16[128,384]{0,1:T(8,128)(2,1)}, bf16[128,384]{0,1:T(8,128)(2,1)S(1)}, u32[]{:S(2)}) copy-start(bf16[128,384]{0,1:T(8,128)(2,1)S(1)} %copy.173) | copy-start | bytes 294916
  46.4 142.0 %copy-start.7 = (bf16[128,384]{0,1:T(8,128)(2,1)}, bf16[128,384]{0,1:T(8,128)(2,1)S(1)}, u32[]{:S(2)}) copy-start(bf16[128,384]{0,1:T(8,128)(2,1)S(1)} %copy.177) | copy-start | bytes 294916
  51.6 136.7 %copy-start.3 = (pred[128,3,2048]{0,2,1:T(8,128)(4,1)}, pred[128,3,2048]{0,2,1:T(8,128)(4,1)S(1)}, u32[]{:S(2)}) copy-start(pred[128,3,2048]{0,2,1:T(8,128)(4,1)S(1)} %pad_add_fusion) | copy-start | bytes 2359300
  161.8 10.0 %copy-start.12 = (f32[3,2048,128,3]{2,1,3,0:T(8,128)S(1)}, f32[3,2048,128,3]{2,1,3,0:T(8,128)}, u32[]{:S(2)}) copy-start(f32[3,2048,128,3]{2,1,3,0:T(8,128)} %get-tuple-element.63) | copy-start | bytes 28311556
  188.4 18.5 %slice-start = ((s8[9437184]{0:T(1024)(128)(4,1)}), s8[4194304]{0:T(1024)(128)(4,1)S(1)}, s32[]{:S(2)}) async-start(s8[9437184]{0:T(1024)(128)(4,1)} %bitcast.482), calls=%async_computation.6 | async-start | bytes 8388608
  188.4 18.5 %slice-start.1 = ((s8[9437184]{0:T(1024)(128)(4,1)}), s8[4194304]{0:T(1024)(128)(4,1)S(1)}, s32[]{:S(2)}) async-start(s8[9437184]{0:T(1024)(128)(4,1)} %bitcast.482), calls=%async_computation.7 | async-start | bytes 8388608
  196.0 10.9 %slice-start.2 = ((s8[9437184]{0:T(1024)(128)(4,1)}), s8[1048576]{0:T(1024)(128)(4,1)S(1)}, s32[]{:S(2)}) async-start(s8[9437184]{0:T(1024)(128)(4,1)} %bitcast.482), calls=%async_computation.8 | async-start | bytes 2097152
  196.0 10.9 %copy-start.4 = (pred[128,3,2048]{0,2,1:T(8,128)(4,1)S(1)}, pred[128,3,2048]{0,2,1:T(8,128)(4,1)}, u32[]{:S(2)}) copy-start(pred[128,3,2048]{0,2,1:T(8,128)(4,1)} %copy-done.3) | copy-start | bytes 2359300
  204.1 6.8 %copy-start = (bf16[3,128,3,2048]{1,3,0,2:T(8,128)(2,1)}, bf16[3,128,3,2048]{1,3,0,2:T(8,128)(2,1)S(1)}, u32[]{:S(2)}) copy-start(bf16[3,128,3,2048]{1,3,0,2:T(8,128)(2,1)S(1)} %fusion.8) | copy-start | bytes 14155780
  216.8 7.4 %copy-start.1 = (bf16[3,128,3,2048]{1,3,0,2:T(8,128)(2,1)}, bf16[3,128,3,2048]{1,3,0,2:T(8,128)(2,1)S(1)}, u32[]{:S(2)}) copy-start(bf16[3,128,3,2048]{1,3,0,2:T(8,128)(2,1)S(1)} %fusion.5) | copy-start | bytes 14155780
  224.1 8.2 %copy-start.6 = (bf16[128,384]{0,1:T(8,128)(2,1)S(1)}, bf16[128,384]{0,1:T(8,128)(2,1)}, u32[]{:S(2)}) copy-start(bf16[128,384]{0,1:T(8,128)(2,1)} %copy-done.5) | copy-start | bytes 294916
  229.6 10.2 %copy-start.2 = (bf16[3,128,3,2048]{1,3,0,2:T(8,128)(2,1)}, bf16[3,128,3,2048]{1,3,0,2:T(8,128)(2,1)S(1)}, u32[]{:S(2)}) copy-start(bf16[3,128,3,2048]{1,3,0,2:T(8,128)(2,1)S(1)} %fusion.2) | copy-start | bytes 14155780
  232.3 7.5 %copy-start.8 = (bf16[128,384]{0,1:T(8,128)(2,1)S(1)}, bf16[128,384]{0,1:T(8,128)(2,1)}, u32[]{:S(2)}) copy-start(bf16[128,384]{0,1:T(8,128)(2,1)} %copy-done.7) | copy-start | bytes 294916
  298.0 101.1 %copy-start.10 = (bf16[128,3,128]{2,0,1:T(8,128)(2,1)S(1)}, bf16[128,3,128]{2,0,1:T(8,128)(2,1)}, u32[]{:S(2)}) copy-start(bf16[128,3,128]{2,0,1:T(8,128)(2,1)} %get-tuple-element.70) | copy-start | bytes 294916
  298.0 101.3 %copy-start.11 = (bf16[128,3,128]{2,0,1:T(8,128)(2,1)S(1)}, bf16[128,3,128]{2,0,1:T(8,128)(2,1)}, u32[]{:S(2)}) copy-start(bf16[128,3,128]{2,0,1:T(8,128)(2,1)} %get-tuple-element.66) | copy-start | bytes 294916
  298.0 101.4 %copy-start.9 = (bf16[128,3,128]{2,0,1:T(8,128)(2,1)S(1)}, bf16[128,3,128]{2,0,1:T(8,128)(2,1)}, u32[]{:S(2)}) copy-start(bf16[128,3,128]{2,0,1:T(8,128)(2,1)} %get-tuple-element.72) | copy-start | bytes 294916
  298.0 133.9 %reduce-scatter.5.cloned.1.call-start = ((), (), s32[]{:S(2)}) async-start(), calls=%async_computation.3 | async-start | bytes 2359296 | tf_op jit(solution)/shard_map/reduce_scatter | solution.py:127
Sparse Core Ops, SparseCore 0:
  10.3 27.7 all-gather.3
  41.4 90.2 all-gather.5
  298.2 94.3 reduce-scatter.6
  399.1 32.7 reduce-scatter.4
where the time goes:
time: 449 us; the launch traced here: 440 us
  waiting for transfers between devices  211 us (47%)
  matrix products  130 us (29%)
  local copies, waits for them, and re-layouts  61.7 us (14%)
  other arithmetic  21.9 us (5%)
  between operations  16.2 us (4%)
    unnamed x5, waiting for transfers between devices  92.5 us
    all_gather x1, waiting for transfers between devices, per_device(): full_rows = lax.all_gather(picked, 'ctx', axis=2, tiled=True)  80 us
    unnamed x36, local copies, waits for them, and re-layouts  47.3 us
    dot_general x4, matrix products, head_scores(): jnp.einsum('qgd,lkd->gqlk', query_head, key_head, preferred_element_type=...  30.1 us
    dot_general x4, matrix products, per_device(): jnp.einsum('qgd,lkd->gqlk', cotan_head, value_head, preferred_element_typ...  26.2 us
    all_gather x1, waiting for transfers between devices, per_device(): tree_rows = lax.all_gather(key_value, 'cand', axis=0, tiled=True)  23.5 us
    dot_general x4, matrix products, per_device(): jnp.einsum('gqlk,qgd->lkd', weights_reduced, cotan_head, preferred_elemen...  22.4 us
    dot_general x4, matrix products, per_device(): jnp.einsum('gqlk,lkd->qgd', weights_reduced, value_head, preferred_elemen...  20.9 us
  transfers between devices with their start and end apart: 4, of which 4 were waited for; matrix products, arithmetic and copies ran while one was open for 8% of the time, Pallas kernels for 0%

commit v1 on v0

v1 whole, which is shorter than its diff:
```python
import functools
import math

import jax
import jax.numpy as jnp
from jax import lax
from jax.experimental import pallas as pl
from jax.experimental.pallas import tpu as pltpu
from jax.sharding import PartitionSpec as P

HEAD = 128
BLOCK = 128
GROUP = 3
ROWS = GROUP * BLOCK
KVW = 2 * HEAD
CHUNK = 4
NKEY = CHUNK * BLOCK
NEG = -1e30
SCALE = HEAD ** (-0.5)
LOG2E = math.log2(math.e)


def nt(a, b):
    return lax.dot_general(a, b, (((1,), (1,)), ((), ())), preferred_element_type=jnp.float32)


def nn(a, b):
    return lax.dot_general(a, b, (((1,), (0,)), ((), ())), preferred_element_type=jnp.float32)


def attend_kernel(
    nseg, nblk, tab, bias, q_in, do_in, kva, kvb,
    o_out, dq_out, own_out, oth_out,
    kv, acc, s_buf, p_buf, mx, ls, o_acc, stage, in_sem, out_sem, tseg, tgrp,
):
    loads = []
    for y in range(nseg):
        loads.append(pltpu.make_async_copy(kva.at[:, y], kv.at[y], in_sem.at[y]))
        loads.append(pltpu.make_async_copy(kvb.at[:, y], kv.at[nseg + y], in_sem.at[nseg + y]))
    for cp in loads:
        cp.start()
    pos = tab[0]
    diag = pos // CHUNK
    far_groups = nblk // CHUNK

    @pl.loop(0, 2 * nseg)
    def _(p):
        @pl.loop(0, nblk)
        def _(b):
            acc[p, b] = jnp.zeros((KVW, BLOCK), jnp.float32)

    for cp in loads:
        cp.wait()

    def keys(p, g):
        return kv[p, pl.ds(g * CHUNK, CHUNK), :, :HEAD].reshape(NKEY, HEAD)

    def values(p, g):
        return kv[p, pl.ds(g * CHUNK, CHUNK), :, HEAD:].reshape(NKEY, HEAD)

    def lanes(op, x):
        return functools.reduce(op, [x[:, i * HEAD : (i + 1) * HEAD] for i in range(CHUNK)])

    @pl.loop(0, nseg)
    def _(j):
        qm = q_in[j]
        dm = do_in[j]
        rows_of = lambda x: jnp.concatenate([x[:, g * HEAD : (g + 1) * HEAD] for g in range(GROUP)], axis=0)
        query = rows_of(qm)
        cotan = rows_of(dm)
        query_t = jnp.concatenate([qm[:, g * HEAD : (g + 1) * HEAD].T for g in range(GROUP)], axis=1)
        nfar = tab[1 + j]

        def set_own(i, _):
            tseg[i] = j
            tgrp[i] = i
            return 0

        lax.fori_loop(0, diag + 1, set_own, 0)

        def set_far(i, _):
            tseg[diag + 1 + i] = tab[5 + (i // far_groups) * nseg + j]
            tgrp[diag + 1 + i] = lax.rem(i, far_groups)
            return 0

        lax.fori_loop(0, nfar * far_groups, set_far, 0)
        total = diag + 1 + nfar * far_groups

        mx[...] = jnp.full((ROWS, HEAD), NEG, jnp.float32)
        ls[...] = jnp.zeros((ROWS, HEAD), jnp.float32)
        o_acc[...] = jnp.zeros((ROWS, HEAD), jnp.float32)

        def put(i, s):
            s_buf[i] = s
            mx[...] = jnp.maximum(mx[...], lanes(jnp.maximum, s))

        @pl.loop(0, diag)
        def _(i):
            put(i, nt(query, keys(j, i)) + bias[j, pl.ds(i, 1)])

        @pl.when(diag >= 0)
        def _():
            row = lax.broadcasted_iota(jnp.int32, (BLOCK, NKEY), 0) + pos * BLOCK
            col = lax.broadcasted_iota(jnp.int32, (BLOCK, NKEY), 1) + diag * NKEY
            low = jnp.where(col <= row, bias[j, pl.ds(diag, 1)], NEG)
            put(diag, nt(query, keys(j, diag)) + jnp.concatenate([low] * GROUP, axis=0))

        @pl.loop(diag + 1, total)
        def _(i):
            put(i, nt(query, keys(tseg[i], tgrp[i])))

        top = jnp.max(mx[...], axis=1, keepdims=True)
        mx[...] = jnp.broadcast_to(top * (SCALE * LOG2E), (ROWS, HEAD))

        @pl.loop(0, total)
        def _(i):
            m_all = jnp.concatenate([mx[...]] * CHUNK, axis=1)
            p = jnp.exp2(s_buf[i] * (SCALE * LOG2E) - m_all)
            ls[...] += lanes(jnp.add, p)
            p_low = p.astype(jnp.bfloat16)
            p_buf[i] = p_low
            o_acc[...] += nn(p_low, values(tseg[i], tgrp[i]))

        inv = 1.0 / jnp.sum(ls[...], axis=1, keepdims=True)
        out = (o_acc[...] * inv).astype(jnp.bfloat16)
        for g in range(GROUP):
            o_out[j, :, g * HEAD : (g + 1) * HEAD] = out[g * BLOCK : (g + 1) * BLOCK]
        cot_low = (cotan.astype(jnp.float32) * inv).astype(jnp.bfloat16)
        delta = jnp.sum(cot_low.astype(jnp.float32) * out.astype(jnp.float32), axis=1, keepdims=True)
        mx[...] = jnp.broadcast_to(delta, (ROWS, HEAD))
        o_acc[...] = jnp.zeros((ROWS, HEAD), jnp.float32)
        cot_t = jnp.concatenate([cot_low[g * BLOCK : (g + 1) * BLOCK].T for g in range(GROUP)], axis=1)

        @pl.loop(0, total)
        def _(i):
            seg, grp = tseg[i], tgrp[i]
            key = keys(seg, grp)
            gw = nt(cot_low, values(seg, grp))
            d_all = jnp.concatenate([mx[...]] * CHUNK, axis=1)
            p_low = p_buf[i]
            ds = (gw - d_all).astype(jnp.bfloat16) * p_low
            o_acc[...] += nn(ds, key)
            dk = nn(query_t, ds)
            dv = nn(cot_t, p_low)
            for b in range(CHUNK):
                acc[seg, grp * CHUNK + b, :HEAD] += dk[:, b * BLOCK : (b + 1) * BLOCK]
                acc[seg, grp * CHUNK + b, HEAD:] += dv[:, b * BLOCK : (b + 1) * BLOCK]

        dq = (o_acc[...] * SCALE).astype(jnp.bfloat16)
        for g in range(GROUP):
            dq_out[j, :, g * HEAD : (g + 1) * HEAD] = dq[g * BLOCK : (g + 1) * BLOCK]

    def flush(p):
        dst = own_out.at[:, p] if p < nseg else oth_out.at[:, p - nseg]
        return pltpu.make_async_copy(stage.at[p % 2], dst, out_sem.at[p % 2])

    for p in range(2 * nseg):
        if p >= 2:
            flush(p - 2).wait()

        @pl.loop(0, nblk)
        def _(b):
            stage[p % 2, b, :HEAD] = (acc[p, b, :HEAD] * SCALE).astype(jnp.bfloat16)
            stage[p % 2, b, HEAD:] = acc[p, b, HEAD:].astype(jnp.bfloat16)

        flush(p).start()
    for p in (2 * nseg - 2, 2 * nseg - 1):
        flush(p).wait()


def attend(tab, bias, q, do, kva, kvb):
    nblk, nseg = kva.shape[0], kva.shape[1]
    far = nblk // CHUNK
    groups = 3 * far
    vm = pl.BlockSpec(memory_space=pltpu.VMEM)
    hbm = pl.BlockSpec(memory_space=pl.ANY)
    bf = jnp.bfloat16
    f32 = jnp.float32
    return pl.pallas_call(
        functools.partial(attend_kernel, nseg, nblk),
        out_shape=(
            jax.ShapeDtypeStruct((nseg, BLOCK, ROWS), bf),
            jax.ShapeDtypeStruct((nseg, BLOCK, ROWS), bf),
            jax.ShapeDtypeStruct((nblk, nseg, KVW, BLOCK), bf),
            jax.ShapeDtypeStruct((nblk, nseg, KVW, BLOCK), bf),
        ),
        in_specs=[pl.BlockSpec(memory_space=pltpu.SMEM), vm, vm, vm, hbm, hbm],
        out_specs=(vm, vm, hbm, hbm),
        scratch_shapes=[
            pltpu.VMEM((2 * nseg, nblk, BLOCK, KVW), bf),
            pltpu.VMEM((2 * nseg, nblk, KVW, BLOCK), f32),
            pltpu.VMEM((groups, ROWS, NKEY), f32),
            pltpu.VMEM((groups, ROWS, NKEY), bf),
            pltpu.VMEM((ROWS, HEAD), f32),
            pltpu.VMEM((ROWS, HEAD), f32),
            pltpu.VMEM((ROWS, HEAD), f32),
            pltpu.VMEM((2, nblk, KVW, BLOCK), bf),
            pltpu.SemaphoreType.DMA((2 * nseg,)),
            pltpu.SemaphoreType.DMA((2,)),
            pltpu.SMEM((groups,), jnp.int32),
            pltpu.SMEM((groups,), jnp.int32),
        ],
        compiler_params=pltpu.CompilerParams(vmem_limit_bytes=62 * 1024 * 1024),
        cost_estimate=pl.CostEstimate(
            flops=nseg * 3 * nblk * BLOCK * ROWS * HEAD * 12,
            bytes_accessed=4 * nseg * nblk * BLOCK * KVW * 2,
            transcendentals=nseg * 3 * nblk * BLOCK * ROWS,
        ),
    )(tab, bias, q, do, kva, kvb)


def per_device(query_matrix, key_matrix, value_matrix, output_gradient, parent, seg_depth, block_mask):
    tok = query_matrix.shape[1]
    ncand = lax.axis_size("cand")
    nctx = lax.axis_size("ctx")
    nchip = ncand // 2
    heads = key_matrix.shape[2] // HEAD
    cand = lax.axis_index("cand")
    core = cand % 2
    pos = lax.axis_index("ctx")
    same_core = [[2 * y + c for y in range(nchip)] for c in range(2)]
    partner = [(i, i ^ 1) for i in range(ncand)]

    def spread(x):
        return lax.all_to_all(x, "cand", 0, 0, axis_index_groups=same_core)

    def by_head(x, width):
        return x.reshape(tok, heads, width).transpose(1, 0, 2)

    kv_own = jnp.concatenate([by_head(key_matrix[0], HEAD), by_head(value_matrix[0], HEAD)], axis=2)
    kv_mine = spread(kv_own)
    kva = lax.all_gather(kv_mine, "ctx", axis=0)
    kvb = lax.ppermute(kva, "cand", partner)

    mask_row = lax.dynamic_index_in_dim(block_mask[0], pos, 0, keepdims=False).astype(jnp.bfloat16)
    extra = jnp.zeros((heads, 16, 2 * ROWS), jnp.bfloat16).at[:, 0, :nctx].set(mask_row[None])
    both = jnp.concatenate([by_head(query_matrix[0], ROWS), by_head(output_gradient[0], ROWS)], axis=2)
    both = spread(jnp.concatenate([both, extra], axis=1))
    q = both[:, :tok, :ROWS]
    do = both[:, :tok, ROWS:]
    rows = both[:, tok, :nctx] > 0
    rows = rows | (jnp.arange(nctx)[None, :] == pos)
    bias = jnp.where(jnp.repeat(rows, BLOCK, axis=1), 0.0, NEG).astype(jnp.float32)
    bias = bias.reshape(nchip, nctx // CHUNK, NKEY)

    segs = 2 * jnp.arange(nchip, dtype=jnp.int32) + core

    def place(s):
        return jnp.where(s % 2 == core, s // 2, nchip + s // 2)

    up = parent[segs]
    tab = jnp.concatenate(
        [pos[None], seg_depth[segs], place(up), place(parent[up])]
    ).astype(jnp.int32)

    o, dq, own, oth = attend(tab, bias, q, do, kva, kvb)

    came = lax.ppermute(oth, "cand", partner)
    part = (own.astype(jnp.float32) + came.astype(jnp.float32)).astype(jnp.bfloat16)
    summed = lax.psum_scatter(part, "ctx", scatter_dimension=0)
    kv_grad = spread(summed)
    k_grad = kv_grad[:, :HEAD].transpose(2, 0, 1).reshape(1, tok, heads * HEAD)
    v_grad = kv_grad[:, HEAD:].transpose(2, 0, 1).reshape(1, tok, heads * HEAD)
    back = spread(jnp.concatenate([o, dq], axis=2))
    o_home = back[:, :, :ROWS].transpose(1, 0, 2).reshape(1, tok, heads * ROWS)
    dq_home = back[:, :, ROWS:].transpose(1, 0, 2).reshape(1, tok, heads * ROWS)
    return o_home, dq_home, k_grad, v_grad


def solution(mesh):
    split = P("cand", "ctx", None)
    return jax.shard_map(
        per_device,
        mesh=mesh,
        in_specs=(split, split, split, split, P(), P(), P("cand", None, None)),
        out_specs=(split, split, split, split),
        check_vma=False,
    )
```

time: 449 us -> 269 us (0.60); the launches traced: 440 us -> 273 us
  matrix products: 130 us -> 0 us
  waiting for transfers between devices: 211 us -> 148 us
  Pallas kernels: 0 us -> 53.3 us
  local copies, waits for them, and re-layouts: 61.7 us -> 13.5 us
  blocking collectives: 0 us -> 26.3 us
  other arithmetic: 21.9 us -> 8.26 us
  starting transfers between devices: 0.16 us -> 8.68 us
    dot_general x25 -> x0, matrix products: 130 us -> none  [the longest x4 30.1 us: head_scores(): jnp.einsum('qgd,lkd->gqlk', query_head, key_head, preferred_element_type=...]
    pallas_call x0 -> x1, Pallas kernels: none -> 53.3 us  [attend(): pl.pallas_call(functools.partial(attend_kernel, nseg, nblk), out_shape=(j...]
    all_gather x2 -> x1, waiting for transfers between devices: 104 us -> 52 us  [per_device(): kva = lax.all_gather(kv_mine, 'ctx', axis=0)]
    unnamed x36 -> x18, local copies, waits for them, and re-layouts: 47.3 us -> 8.08 us
    all_to_all x0 -> x2, blocking collectives: none -> 26.3 us  [spread(): return lax.all_to_all(x, 'cand', 0, 0, axis_index_groups=same_core)]
    unnamed x5 -> x3, waiting for transfers between devices: 92.5 us -> 73.2 us
    all_to_all x0 -> x2, waiting for transfers between devices: none -> 15.7 us  [spread(): return lax.all_to_all(x, 'cand', 0, 0, axis_index_groups=same_core)]
    reduce_scatter x1 -> x0, waiting for transfers between devices: 14.8 us -> none  [per_device(): lax.psum_scatter(routed.astype(jnp.bfloat16), 'cand', scatter_dimension=0...]
  transfers between devices with their start and end apart: 4 -> 6, of which waited for: 4 -> 5; matrix products, arithmetic and copies ran while one was open for 8% -> 4% of each run, Pallas kernels for 0% -> 0%
where the time goes in v1:
time: 269 us; the launch traced here: 273 us
  waiting for transfers between devices  148 us (55%)
  Pallas kernels  53.3 us (20%)
  blocking collectives  26.3 us (10%)
  between operations  14.2 us (5%)
  local copies, waits for them, and re-layouts  13.5 us (5%)
  starting transfers between devices  8.68 us (3%)
  other arithmetic  8.26 us (3%)
    unnamed x3, waiting for transfers between devices  73.2 us
    pallas_call x1, Pallas kernels, attend(): pl.pallas_call(functools.partial(attend_kernel, nseg, nblk), out_shape=(j...  53.3 us
    all_gather x1, waiting for transfers between devices, per_device(): kva = lax.all_gather(kv_mine, 'ctx', axis=0)  52 us
    all_to_all x2, blocking collectives, spread(): return lax.all_to_all(x, 'cand', 0, 0, axis_index_groups=same_core)  26.3 us
    all_to_all x2, waiting for transfers between devices, spread(): return lax.all_to_all(x, 'cand', 0, 0, axis_index_groups=same_core)  15.7 us
    all_to_all x2, starting transfers between devices, spread(): return lax.all_to_all(x, 'cand', 0, 0, axis_index_groups=same_core)  8.55 us
    unnamed x18, local copies, waits for them, and re-layouts  8.08 us
    ppermute x1, waiting for transfers between devices, per_device(): came = lax.ppermute(oth, 'cand', partner)  7.36 us
  transfers between devices with their start and end apart: 6, of which 5 were waited for; matrix products, arithmetic and copies ran while one was open for 4% of the time, Pallas kernels for 0%

profile of v1, /device:TPU:0, one launch (start us, length us, event | category | flops | bytes accessed | tf_op | source)
XLA Modules:
  0.0 272.5 jit_solution(4833196953836000045)
XLA Ops:
  7.2 0.0 copy-start
  7.2 0.0 copy-start.2
  7.2 0.0 all-gather.3.cloned.1.call-start
  7.2 1.1 copy.41
  8.3 1.0 copy.42
  9.4 11.1 %all_to_all.20 = bf16[4,128,256]{1,2,0:T(8,128)(2,1)S(1)} all-to-all(bf16[4,128,256]{1,2,0:T(8,128)(2,1)S(1)} %pad_maximum_fusion.2), channel_id=1, replica_groups={{0,32,64,96},{16,48,80,112},{1,33,65,97},{17,49,81,113},{2,34,66,98},{1..., dimensions={0} | all-to-all | bytes 524288 | tf_op jit(solution)/shard_map/all_to_all | solution.py:225
  20.4 0.0 copy-start.1
  20.4 0.9 copy.43
  21.3 0.0 all-gather.3.cloned.1.call-update
  21.3 52.0 %all-gather.3.cloned.1.call-done = bf16[64,128,256]{2,1,0:T(8,128)(2,1)} async-done(((bf16[4,128,256]{2,1,0:T(8,128)(2,1)}), bf16[64,128,256]{2,1,0:T(8,128)(2,1)}) %all-gather.3.cloned.1.call-update) | async-done | bytes 4194320 | tf_op jit(solution)/shard_map/all_gather | solution.py:232
  73.3 0.0 collective-permute-start
  73.3 1.2 copy.37
  74.5 0.2 copy.38
  74.8 0.0 copy-done.2
  74.8 0.2 copy.39
  75.0 0.2 copy.40
  75.3 0.7 convert_bitcast_fusion
  76.0 1.1 pad_maximum_fusion
  77.1 4.3 %all-to-all-start = ((bf16[4,144,768]{2,1,0:T(8,128)(2,1)}), bf16[4,144,768]{2,1,0:T(8,128)(2,1)S(1)}, u32[]{:S(2)}, u32[]{:S(2)}) async-start(bf16[4,144,768]{2,1,0:T(8,128)(2,1)} %pad_maximum_fusion), calls=%async_computation | async-start | bytes 1769472 | tf_op jit(solution)/shard_map/all_to_all | solution.py:225
  81.3 0.0 reduce-scatter.4.cloned.1.call-start
  81.4 0.0 copy-done
  81.4 0.6 gather_fusion.1
  82.0 0.0 copy-done.1
  82.0 0.6 gather_fusion
  82.7 0.6 gather_fusion.2
  83.3 0.6 pad_add_fusion.tab
  83.9 11.4 %all-to-all-done = bf16[4,144,768]{2,1,0:T(8,128)(2,1)S(1)} async-done(((bf16[4,144,768]{2,1,0:T(8,128)(2,1)}), bf16[4,144,768]{2,1,0:T(8,128)(2,1)S(1)}, u32[]{:S(2)}, u32[]{:S(2)}) %all-to-all-start) | async-done | bytes 884768 | tf_op jit(solution)/shard_map/all_to_all | solution.py:225
  95.4 0.1 broadcast_in_dim.26
  95.4 0.6 select_n.78.bias
  96.1 1.0 fusion.3
  97.0 0.0 collective-permute-done.kvb
  97.0 53.3 %shard_map.102 = (bf16[4,128,384]{2,1,0:T(8,128)(2,1)}, bf16[4,128,384]{2,1,0:T(8,128)(2,1)}, bf16[16,4,256,128]{3,2,1,0:T(8,128)(2,1)}, bf16[16,4,256,128]{3,2,1,0:T(8,128)(2,1)}) custom-call(s32[13]{0:T(128)} %pad_add_fusion.tab, f32[4,4,512]{2,1,0:T(4,128)} %select_n.78.bias, bf16[4,128,384]{2,1,0:T(8,128)(2,1)} %get-tuple-element.41.q_in, ...), custom_call_target="tpu_custom_call" | custom-call | flops 14495514624 | bytes 16777216 | tf_op jit(solution)/shard_map/pallas_call | solution.py:179
  150.3 0.1 collective-permute-start.1
  150.4 7.4 %collective-permute-done.1 = bf16[16,4,256,128]{3,2,1,0:T(8,128)(2,1)S(1)} collective-permute-done((bf16[16,4,256,128]{3,2,1,0:T(8,128)(2,1)}, bf16[16,4,256,128]{3,2,1,0:T(8,128)(2,1)S(1)}, u32[]{:S(2)}, u32[]{:S(2)}) %collective-permute-start.1) | collective-permute-done | bytes 4194336 | tf_op jit(solution)/shard_map/ppermute | solution.py:258
  157.8 5.8 %add_convert_fusion = bf16[16,4,256,128]{3,2,1,0:T(8,128)(2,1)} fusion(bf16[16,4,256,128]{3,2,1,0:T(8,128)(2,1)S(1)} %collective-permute-done.1, bf16[16,4,256,128]{3,2,1,0:T(8,128)(2,1)} %get-tuple-element.22), kind=kLoop, calls=%fused_computation.3 | loop fusion | flops 8388608 | bytes 12582912 | tf_op jit(solution)/shard_map/convert_element_type | solution.py:259
  163.5 0.0 copy-start.3
  163.5 0.0 copy-start.4
  163.5 0.0 reduce-scatter.4.cloned.1.call-update
  163.6 1.0 copy-done.3
  164.5 0.1 copy-done.4
  164.6 0.1 pad_maximum_fusion.1
  164.7 15.3 %all_to_all.21 = bf16[4,128,768]{2,1,0:T(8,128)(2,1)S(1)} all-to-all(bf16[4,128,768]{2,1,0:T(8,128)(2,1)S(1)} %pad_maximum_fusion.1), channel_id=1, replica_groups={{0,32,64,96},{16,48,80,112},{1,33,65,97},{17,49,81,113},{2,34,66,98},{1..., dimensions={0} | all-to-all | bytes 1572864 | tf_op jit(solution)/shard_map/all_to_all | solution.py:225
  180.0 73.2 %reduce-scatter.4.cloned.1.call-done = bf16[1,4,256,128]{3,2,1,0:T(8,128)(2,1)} async-done(((bf16[16,4,256,128]{3,2,1,0:T(8,128)(2,1)}), bf16[1,4,256,128]{3,2,1,0:T(8,128)(2,1)}) %reduce-scatter.4.cloned.1.call-update) | async-done | bytes 262160
  253.2 4.3 %all-to-all-start.3 = ((bf16[4,256,128]{2,1,0:T(8,128)(2,1)}), bf16[4,256,128]{2,1,0:T(8,128)(2,1)S(1)}, u32[]{:S(2)}, u32[]{:S(2)}) async-start(bf16[4,256,128]{2,1,0:T(8,128)(2,1)} %bitcast.48), calls=%async_computation.3 | async-start | bytes 524288 | tf_op jit(solution)/shard_map/all_to_all | solution.py:225
  257.4 0.1 slice_bitcast_fusion
  257.5 0.2 copy.45
  257.8 0.9 copy.47
  258.7 0.2 copy.44
  258.9 0.9 copy.46
  259.9 4.3 %all-to-all-done.3 = bf16[4,256,128]{2,1,0:T(8,128)(2,1)S(1)} async-done(((bf16[4,256,128]{2,1,0:T(8,128)(2,1)}), bf16[4,256,128]{2,1,0:T(8,128)(2,1)S(1)}, u32[]{:S(2)}, u32[]{:S(2)}) %all-to-all-start.3) | async-done | bytes 262176 | tf_op jit(solution)/shard_map/all_to_all | solution.py:225
  264.1 0.8 copy.49
  264.9 0.8 copy.48
  (12 shorter events, 0.1 us)
Async XLA Ops:
  7.2 74.2 %copy-start = (s32[8]{0:T(128)S(1)}, s32[8]{0:T(128)}, u32[]{:S(2)}) copy-start(s32[8]{0:T(128)} %param.13) | copy-start | bytes 100
  7.2 67.6 %copy-start.2 = (bf16[1,128,1536]{2,1,0:T(8,128)(2,1)S(1)}, bf16[1,128,1536]{2,1,0:T(8,128)(2,1)}, u32[]{:S(2)}) copy-start(bf16[1,128,1536]{2,1,0:T(8,128)(2,1)} %param.12) | copy-start | bytes 1179652
  7.2 66.1 %all-gather.3.cloned.1.call-start = ((), (), s32[]{:S(2)}) async-start(), calls=%async_computation.5 | async-start | bytes 4456448 | tf_op jit(solution)/shard_map/all_gather | solution.py:232
  20.4 61.6 %copy-start.1 = (s32[8]{0:T(128)S(1)}, s32[8]{0:T(128)}, u32[]{:S(2)}) copy-start(s32[8]{0:T(128)} %param.14) | copy-start | bytes 100
  73.3 23.7 %collective-permute-start = (bf16[16,4,128,256]{3,2,1,0:T(8,128)(2,1)}, bf16[16,4,128,256]{3,2,1,0:T(8,128)(2,1)}, u32[]{:S(2)}, u32[]{:S(2)}) collective-permute-start(bf16[16,4,128,256]{3,2,1,0:T(8,128)(2,1)} %bitcast.49), channel_id=1, source_target_pairs={{0,16},{16,0},{32,48},{48,32},{64,80},{80,64},{96,112},{112,96},{1... | collective-permute-start | bytes 12582920 | tf_op jit(solution)/shard_map/ppermute | solution.py:233
  77.1 18.3 %all-to-all-start = ((bf16[4,144,768]{2,1,0:T(8,128)(2,1)}), bf16[4,144,768]{2,1,0:T(8,128)(2,1)S(1)}, u32[]{:S(2)}, u32[]{:S(2)}) async-start(bf16[4,144,768]{2,1,0:T(8,128)(2,1)} %pad_maximum_fusion), calls=%async_computation | async-start | bytes 1769472 | tf_op jit(solution)/shard_map/all_to_all | solution.py:225
  81.3 171.8 %reduce-scatter.4.cloned.1.call-start = ((), (), s32[]{:S(2)}) async-start(), calls=%async_computation.6 | async-start | bytes 4456448
  150.3 7.4 %collective-permute-start.1 = (bf16[16,4,256,128]{3,2,1,0:T(8,128)(2,1)}, bf16[16,4,256,128]{3,2,1,0:T(8,128)(2,1)S(1)}, u32[]{:S(2)}, u32[]{:S(2)}) collective-permute-start(bf16[16,4,256,128]{3,2,1,0:T(8,128)(2,1)} %get-tuple-element.23), channel_id=1, source_target_pairs={{0,16},{16,0},{32,48},{48,32},{64,80},{80,64},{96,112},{112,96},{1... | collective-permute-start | bytes 12582920 | tf_op jit(solution)/shard_map/ppermute | solution.py:258
  163.5 1.0 copy-start.3
  163.5 1.1 copy-start.4
  253.2 11.0 %all-to-all-start.3 = ((bf16[4,256,128]{2,1,0:T(8,128)(2,1)}), bf16[4,256,128]{2,1,0:T(8,128)(2,1)S(1)}, u32[]{:S(2)}, u32[]{:S(2)}) async-start(bf16[4,256,128]{2,1,0:T(8,128)(2,1)} %bitcast.48), calls=%async_computation.3 | async-start | bytes 524288 | tf_op jit(solution)/shard_map/all_to_all | solution.py:225
Sparse Core Ops, SparseCore 0:
  21.4 51.8 all-gather.2
  163.7 89.4 reduce-scatter.3

commit v2 on v1

v2 whole, which is shorter than its diff:
```python
import functools
import math

import jax
import jax.numpy as jnp
from jax import lax
from jax.experimental import pallas as pl
from jax.experimental.pallas import tpu as pltpu
from jax.sharding import PartitionSpec as P


HEAD = 128
BLOCK = 128
GROUP = 3
ROWS = GROUP * BLOCK
KVW = 2 * HEAD
CHUNK = 8
NKEY = CHUNK * BLOCK
HALF = 4
HKEY = HALF * BLOCK
EXTRA = 16
NEG = -1e30
SCALE = HEAD ** (-0.5)
LOG2E = math.log2(math.e)
SAFE = 70.0


def nt(a, b):
    return lax.dot_general(a, b, (((1,), (1,)), ((), ())), preferred_element_type=jnp.float32)


def nn(a, b):
    return lax.dot_general(a, b, (((1,), (0,)), ((), ())), preferred_element_type=jnp.float32)


OUTER = (0, 0, 1, 1, 3, 3, 2, 2)


def spans(refs):
    return [(OUTER[k], 2 * (k % 2) + e, ref, e) for k, ref in enumerate(refs) for e in range(2)]


def attend_kernel(nseg, nblk, side, ids, parent, depth, both, *refs):
    pieces, refs = refs[:16], refs[16:]
    o_out, dq_out = refs[:2]
    parts, refs = refs[2:18], refs[18:]
    kv, acc, s_buf, p_buf, bias, mx, ls, o_acc, stage, in_sem, out_sem, tseg, tgrp = refs
    core = lax.rem(ids[0], 2)
    pos = ids[1]
    cx, cz = lax.div(pos, side), lax.rem(pos, side)

    def block_of(route, outer, inner):
        a = lax.rem(jnp.where(route == 0, cx, cz) + side - outer, side)
        b = lax.rem(jnp.where(route == 0, cz, cx) + side - inner, side)
        return jnp.where(route == 0, a * side + b, b * side + a)

    def place(s):
        return lax.div(s, 2) + jnp.where(lax.rem(s, 2) == core, 0, nseg)

    loads = []
    for w in range(2):
        route = core if w == 0 else 1 - core
        for outer, inner, ref, at in spans(pieces[8 * w : 8 * w + 8]):
            dst = kv.at[pl.ds(nseg * w, nseg), block_of(route, outer, inner)]
            loads.append(pltpu.make_async_copy(ref.at[at], dst, in_sem.at[len(loads)]))
    for cp in loads:
        cp.start()
    diag = lax.div(pos, CHUNK)
    far_groups = nblk // CHUNK

    @pl.loop(0, 2 * nseg)
    def _(p):
        @pl.loop(0, nblk // 4)
        def _(b):
            for e in range(4):
                acc[p, 4 * b + e] = jnp.zeros((KVW, BLOCK), jnp.float32)

    for cp in loads:
        cp.wait()

    def norm_step(p, top):
        k = jnp.max(jnp.abs(kv[p, :, :, :HEAD].reshape(nblk * BLOCK // 16, 16, HEAD)), axis=0).astype(jnp.float32)
        k = jnp.max(k, axis=0, keepdims=True)
        return jnp.maximum(top, jnp.sum(k * k, axis=1, keepdims=True))

    key_top = lax.fori_loop(0, 2 * nseg, norm_step, jnp.zeros((1, 1), jnp.float32))

    def keys(p, g, h):
        return kv[p, pl.ds(g * CHUNK + h * HALF, HALF), :, :HEAD].reshape(HKEY, HEAD)

    def values(p, g, h):
        return kv[p, pl.ds(g * CHUNK + h * HALF, HALF), :, HEAD:].reshape(HKEY, HEAD)

    def lanes(op, x):
        return functools.reduce(op, [x[:, i * HEAD : (i + 1) * HEAD] for i in range(HALF)])

    halves = CHUNK // HALF

    @pl.loop(0, nseg)
    def _(j):
        qm = both[j, :BLOCK, :ROWS]
        dm = both[j, :BLOCK, ROWS:]
        rows_of = lambda x: jnp.concatenate([x[:, g * HEAD : (g + 1) * HEAD] for g in range(GROUP)], axis=0)
        query = rows_of(qm)
        cotan = rows_of(dm)
        query_t = jnp.concatenate([qm[:, g * HEAD : (g + 1) * HEAD].T for g in range(GROUP)], axis=1)
        me = 2 * j + core
        nfar = depth[me]
        up = parent[me]
        far_a, far_b = place(up), place(parent[up])

        def set_own(i, _):
            tseg[i] = j
            tgrp[i] = i
            return 0

        lax.fori_loop(0, diag + 1, set_own, 0)

        def set_far(i, _):
            tseg[diag + 1 + i] = jnp.where(i < far_groups, far_a, far_b)
            tgrp[diag + 1 + i] = lax.rem(i, far_groups)
            return 0

        lax.fori_loop(0, nfar * far_groups, set_far, 0)
        total = diag + 1 + nfar * far_groups

        mask_row = both[j, BLOCK : BLOCK + EXTRA, :HEAD][:1].astype(jnp.float32)
        lane = lax.broadcasted_iota(jnp.int32, (1, HEAD), 1)
        for b in range(nblk):
            bit = jnp.sum(jnp.where(lane == b, mask_row, 0.0), axis=1, keepdims=True)
            open_ = jnp.broadcast_to(bit, (1, BLOCK)) + jnp.where(pos == b, 1.0, 0.0)
            bias[b // HALF, :, (b % HALF) * BLOCK : (b % HALF + 1) * BLOCK] = jnp.where(open_ > 0.5, 0.0, NEG)

        ls[...] = jnp.zeros((ROWS, HEAD), jnp.float32)
        o_acc[...] = jnp.zeros((ROWS, HEAD), jnp.float32)

        qf = query.astype(jnp.float32)
        q_top = jnp.max(jnp.sum(qf * qf, axis=1, keepdims=True), axis=0, keepdims=True)
        small = jnp.max(q_top * key_top * (SCALE * SCALE)) <= SAFE * SAFE

        def low_half(i, h):
            row = lax.broadcasted_iota(jnp.int32, (BLOCK, HKEY), 0) + pos * BLOCK
            col = lax.broadcasted_iota(jnp.int32, (BLOCK, HKEY), 1) + (i * NKEY + h * HKEY)
            low = jnp.where(col <= row, bias[i * halves + h], NEG)
            return jnp.concatenate([low] * GROUP, axis=0)

        def scores(i, seg, grp, h, kind):
            s = nt(query, keys(seg, grp, h))
            if kind == 1:
                s = s + bias[i * halves + h]
            if kind == 2:
                s = s + low_half(i, h)
            return s

        def finish(i, seg, grp, h, p):
            ls[...] += lanes(jnp.add, p)
            p_low = p.astype(jnp.bfloat16)
            p_buf[i, :, h * HKEY : (h + 1) * HKEY] = p_low
            o_acc[...] += nn(p_low, values(seg, grp, h))

        def sweep(body):
            @pl.loop(0, diag)
            def _(i):
                body(i, j, i, 1)

            body(diag, j, diag, 2)

            @pl.loop(diag + 1, total)
            def _(i):
                body(i, tseg[i], tgrp[i], 0)

        @pl.when(small)
        def _():
            def body(i, seg, grp, kind):
                for h in range(halves):
                    s = scores(i, seg, grp, h, kind)
                    finish(i, seg, grp, h, jnp.exp2(s * (SCALE * LOG2E)))

            sweep(body)

        @pl.when(jnp.logical_not(small))
        def _():
            mx[...] = jnp.full((ROWS, HEAD), NEG, jnp.float32)

            def body(i, seg, grp, kind):
                for h in range(halves):
                    s = scores(i, seg, grp, h, kind)
                    s_buf[i, :, h * HKEY : (h + 1) * HKEY] = s
                    mx[...] = jnp.maximum(mx[...], lanes(jnp.maximum, s))

            sweep(body)
            top = jnp.max(mx[...], axis=1, keepdims=True)
            mx[...] = jnp.broadcast_to(top, (ROWS, HEAD))

            @pl.loop(0, total)
            def _(i):
                m_all = jnp.concatenate([mx[...]] * HALF, axis=1)
                for h in range(halves):
                    s = s_buf[i, :, h * HKEY : (h + 1) * HKEY]
                    finish(i, tseg[i], tgrp[i], h, jnp.exp2((s - m_all) * (SCALE * LOG2E)))

        inv = 1.0 / jnp.sum(ls[...], axis=1, keepdims=True)
        out = (o_acc[...] * inv).astype(jnp.bfloat16)
        for g in range(GROUP):
            o_out[j, :, g * HEAD : (g + 1) * HEAD] = out[g * BLOCK : (g + 1) * BLOCK]
        cot_low = (cotan.astype(jnp.float32) * inv).astype(jnp.bfloat16)
        delta = jnp.sum(cot_low.astype(jnp.float32) * out.astype(jnp.float32), axis=1, keepdims=True)
        mx[...] = jnp.broadcast_to(delta, (ROWS, HEAD))
        o_acc[...] = jnp.zeros((ROWS, HEAD), jnp.float32)
        cot_t = jnp.concatenate([cot_low[g * BLOCK : (g + 1) * BLOCK].T for g in range(GROUP)], axis=1)

        @pl.loop(0, total)
        def _(i):
            seg, grp = tseg[i], tgrp[i]
            for h in range(halves):
                key = keys(seg, grp, h)
                gw = nt(cot_low, values(seg, grp, h))
                d_all = jnp.concatenate([mx[...]] * HALF, axis=1)
                p_low = p_buf[i, :, h * HKEY : (h + 1) * HKEY]
                ds = (gw - d_all).astype(jnp.bfloat16) * p_low
                o_acc[...] += nn(ds, key)
                dk = nn(query_t, ds)
                dv = nn(cot_t, p_low)
                for b in range(HALF):
                    at = grp * CHUNK + h * HALF + b
                    acc[seg, at, :HEAD] += dk[:, b * BLOCK : (b + 1) * BLOCK]
                    acc[seg, at, HEAD:] += dv[:, b * BLOCK : (b + 1) * BLOCK]

        dq = (o_acc[...] * SCALE).astype(jnp.bfloat16)
        for g in range(GROUP):
            dq_out[j, :, g * HEAD : (g + 1) * HEAD] = dq[g * BLOCK : (g + 1) * BLOCK]

    flushes = []
    for w in (1, 0):
        route = core if w == 0 else 1 - core
        for outer, inner, ref, at in spans(parts[8 * w : 8 * w + 8]):
            src = stage.at[w, outer * 4 + inner]
            flushes.append(pltpu.make_async_copy(src, ref.at[at], out_sem.at[len(flushes)]))

        @pl.loop(0, nblk)
        def _(t):
            b = block_of(route, lax.div(t, 4), lax.rem(t, 4))
            for e in range(nseg):
                stage[w, t, e, :HEAD] = (acc[nseg * w + e, b, :HEAD] * SCALE).astype(jnp.bfloat16)
                stage[w, t, e, HEAD:] = acc[nseg * w + e, b, HEAD:].astype(jnp.bfloat16)

        for cp in flushes[-16:]:
            cp.start()
    for cp in flushes:
        cp.wait()


def attend(ids, parent, depth, both, pieces, side):
    nseg, nblk = both.shape[0], side * side
    groups = 3 * (nblk // CHUNK)
    vm = pl.BlockSpec(memory_space=pltpu.VMEM)
    hbm = pl.BlockSpec(memory_space=pl.ANY)
    sm = pl.BlockSpec(memory_space=pltpu.SMEM)
    bf = jnp.bfloat16
    f32 = jnp.float32
    parts = [jax.ShapeDtypeStruct((2, nseg, KVW, BLOCK), bf)] * 16
    return pl.pallas_call(
        functools.partial(attend_kernel, nseg, nblk, side),
        out_shape=[jax.ShapeDtypeStruct((nseg, BLOCK, ROWS), bf)] * 2 + parts,
        in_specs=[sm, sm, sm, vm] + [hbm] * 16,
        out_specs=[vm, vm] + [hbm] * 16,
        scratch_shapes=[
            pltpu.VMEM((2 * nseg, nblk, BLOCK, KVW), bf),
            pltpu.VMEM((2 * nseg, nblk, KVW, BLOCK), f32),
            pltpu.VMEM((groups, ROWS, NKEY), f32),
            pltpu.VMEM((groups, ROWS, NKEY), bf),
            pltpu.VMEM((nblk // HALF, 1, HKEY), f32),
            pltpu.VMEM((ROWS, HEAD), f32),
            pltpu.VMEM((ROWS, HEAD), f32),
            pltpu.VMEM((ROWS, HEAD), f32),
            pltpu.VMEM((2, nblk, nseg, KVW, BLOCK), bf),
            pltpu.SemaphoreType.DMA((32,)),
            pltpu.SemaphoreType.DMA((32,)),
            pltpu.SMEM((groups,), jnp.int32),
            pltpu.SMEM((groups,), jnp.int32),
        ],
        compiler_params=pltpu.CompilerParams(vmem_limit_bytes=62 * 1024 * 1024),
        cost_estimate=pl.CostEstimate(
            flops=nseg * 3 * nblk * BLOCK * ROWS * HEAD * 12,
            bytes_accessed=4 * nseg * nblk * BLOCK * KVW * 2,
            transcendentals=nseg * 3 * nblk * BLOCK * ROWS,
        ),
    )(ids, parent, depth, both, *pieces)


BOTH_AXES = ("cand", "ctx")


def ring(ncand, side, phase, step):
    pairs = []
    for c in range(ncand):
        along_x = (c % 2 == 1) == (phase == 0)
        for x in range(side):
            for z in range(side):
                to = ((x + step) % side, z) if along_x else (x, (z + step) % side)
                pairs.append(((c * side + x) * side + z, (c * side + to[0]) * side + to[1]))
    return pairs


def add(*xs):
    return functools.reduce(jnp.add, [x.astype(jnp.float32) for x in xs]).astype(jnp.bfloat16)


def hop(x, perm):
    return lax.ppermute(x, BOTH_AXES, perm)


def gather_ring(line_lo, line_hi, up, down):
    low_a = hop(line_lo, up)
    high_b = hop(line_hi, down)
    low_b = hop(line_hi, up)
    high_a = hop(line_lo, down)
    mid_a = hop(low_a, up)
    mid_b = hop(high_b, down)
    return [line_lo, line_hi, low_a, low_b, high_a, high_b, mid_a, mid_b]


def scatter_ring(own, came, up, down):
    same_lo, same_hi, low_a, low_b, high_a, high_b, mid_a, mid_b = zip(own, came)
    far_b, far_a = add(*mid_b), add(*mid_a)
    got_b = hop(far_b, up)
    got_a = hop(far_a, down)
    free_b, free_a = add(*low_b), add(*high_a)
    from_b = hop(free_b, down)
    from_a = hop(free_a, up)
    last_a, last_b = add(*low_a, got_a), add(*high_b, got_b)
    end_a = hop(last_a, down)
    end_b = hop(last_b, up)
    return add(*same_lo, from_a, end_a), add(*same_hi, from_b, end_b)


def per_device(query_matrix, key_matrix, value_matrix, output_gradient, parent, seg_depth, block_mask):
    tok = query_matrix.shape[1]
    ncand = lax.axis_size("cand")
    nctx = lax.axis_size("ctx")
    nchip = ncand // 2
    heads = key_matrix.shape[2] // HEAD
    side = math.isqrt(nctx)
    pos = lax.axis_index("ctx")
    same_core = [[2 * y + c for y in range(nchip)] for c in range(2)]
    partner = [(i, i ^ 1) for i in range(ncand)]
    across = ring(ncand, side, 0, 2)
    rings = [(ring(ncand, side, phase, 1), ring(ncand, side, phase, -1)) for phase in range(2)]

    def spread(x):
        return lax.all_to_all(x, "cand", 0, 0, axis_index_groups=same_core)

    def cut(x, h, width):
        return x[:, h * width : (h + 1) * width]

    kv_own = jnp.stack(
        [
            jnp.concatenate([cut(key_matrix[0], h, HEAD), cut(value_matrix[0], h, HEAD)], axis=1)
            for h in range(heads)
        ]
    )
    kv_mine = spread(kv_own)
    near_low = hop(kv_mine, rings[0][0])
    near_high = hop(kv_mine, rings[0][1])
    opposite = hop(kv_mine, across)
    mine = gather_ring(jnp.stack([kv_mine, near_low]), jnp.stack([opposite, near_high]), *rings[1])
    pieces = mine + [lax.ppermute(x, "cand", partner) for x in mine]

    mask_row = lax.dynamic_index_in_dim(block_mask[0], pos, 0, keepdims=True).astype(jnp.bfloat16)
    extra = jnp.pad(mask_row, ((0, EXTRA - 1), (0, 2 * ROWS - nctx)))
    both = jnp.stack(
        [
            jnp.concatenate(
                [
                    jnp.concatenate(
                        [cut(query_matrix[0], h, ROWS), cut(output_gradient[0], h, ROWS)], axis=1
                    ),
                    extra,
                ],
                axis=0,
            )
            for h in range(heads)
        ]
    )
    both = spread(both)

    ids = jnp.stack([lax.axis_index("cand"), pos]).astype(jnp.int32)
    o, dq, *parts = attend(ids, parent, seg_depth, both, pieces, side)

    own, oth = parts[:8], parts[8:]
    came = [lax.ppermute(x, "cand", partner) for x in oth]
    line_lo, line_hi = scatter_ring(own, came, *rings[1])
    end_low = hop(line_lo[1], rings[0][1])
    end_high = hop(line_hi[1], rings[0][0])
    end_far = hop(line_hi[0], across)
    summed = add(line_lo[0], end_low, end_high, end_far)
    kv_grad = spread(summed)
    k_grad = kv_grad[:, :HEAD].transpose(2, 0, 1).reshape(1, tok, heads * HEAD)
    v_grad = kv_grad[:, HEAD:].transpose(2, 0, 1).reshape(1, tok, heads * HEAD)
    back = jnp.concatenate([o, dq], axis=2)
    back = spread(back)
    o_home = jnp.concatenate([back[h, :, :ROWS] for h in range(heads)], axis=1)[None]
    dq_home = jnp.concatenate([back[h, :, ROWS:] for h in range(heads)], axis=1)[None]
    return o_home, dq_home, k_grad, v_grad


def solution(mesh):
    split = P("cand", "ctx", None)
    return jax.shard_map(
        per_device,
        mesh=mesh,
        in_specs=(split, split, split, split, P(), P(), P("cand", None, None)),
        out_specs=(split, split, split, split),
        check_vma=False,
    )
```

time: 269 us -> 180 us (0.67); the launches traced: 273 us -> 180 us
  waiting for transfers between devices: 148 us -> 57.1 us
  starting transfers between devices: 8.68 us -> 55.8 us
  blocking collectives: 26.3 us -> 11.1 us
  between operations: 14.2 us -> 1.12 us
  Pallas kernels: 53.3 us -> 40.3 us
  local copies, waits for them, and re-layouts: 13.5 us -> 5.55 us
    unnamed x3 -> x0, waiting for transfers between devices: 73.2 us -> none
    all_gather x1 -> x0, waiting for transfers between devices: 52 us -> none  [per_device(): kva = lax.all_gather(kv_mine, 'ctx', axis=0)]
    ppermute x2 -> x34, starting transfers between devices: 0.09 us -> 44 us  [the longest x18 36.2 us: hop(): return lax.ppermute(x, BOTH_AXES, perm)]
    ppermute x2 -> x34, waiting for transfers between devices: 7.36 us -> 41 us  [the longest x18 40.9 us: hop(): return lax.ppermute(x, BOTH_AXES, perm)]
    all_to_all x2 -> x1, blocking collectives: 26.3 us -> 11.1 us  [spread(): return lax.all_to_all(x, 'cand', 0, 0, axis_index_groups=same_core)]
    pallas_call x1, Pallas kernels: 53.3 us -> 40.3 us  [attend(): pl.pallas_call(functools.partial(attend_kernel, nseg, nblk, side), out_sh...]
    unnamed x18 -> x42, local copies, waits for them, and re-layouts: 8.08 us -> 3.66 us
    convert_element_type x2 -> x10, other arithmetic: 6.45 us -> 3.07 us  [the longest x9 2.37 us: add(): functools.reduce(jnp.add, [x.astype(jnp.float32) for x in xs])]
  transfers between devices with their start and end apart: 6 -> 37, of which waited for: 5 -> 13; matrix products, arithmetic and copies ran while one was open for 4% -> 4% of each run, Pallas kernels for 0% -> 0%
where the time goes in v2:
time: 180 us
  waiting for transfers between devices  57.1 us (32%)
  starting transfers between devices  55.8 us (31%)
  Pallas kernels  40.3 us (22%)
  blocking collectives  11.1 us (6%)
  other arithmetic  8.6 us (5%)
  local copies, waits for them, and re-layouts  5.55 us (3%)
    ppermute x18, waiting for transfers between devices, hop(): return lax.ppermute(x, BOTH_AXES, perm)  40.9 us
    pallas_call x1, Pallas kernels, attend(): pl.pallas_call(functools.partial(attend_kernel, nseg, nblk, side), out_sh...  40.3 us
    ppermute x18, starting transfers between devices, hop(): return lax.ppermute(x, BOTH_AXES, perm)  36.2 us
    all_to_all x3, waiting for transfers between devices, spread(): return lax.all_to_all(x, 'cand', 0, 0, axis_index_groups=same_core)  16.1 us
    all_to_all x3, starting transfers between devices, spread(): return lax.all_to_all(x, 'cand', 0, 0, axis_index_groups=same_core)  11.8 us
    all_to_all x1, blocking collectives, spread(): return lax.all_to_all(x, 'cand', 0, 0, axis_index_groups=same_core)  11.1 us
    ppermute x8, starting transfers between devices, per_device(): came = [lax.ppermute(x, 'cand', partner) for x in oth]  6.3 us
    unnamed x42, local copies, waits for them, and re-layouts  3.66 us
  transfers between devices with their start and end apart: 37, of which 13 were waited for; matrix products, arithmetic and copies ran while one was open for 4% of the time, Pallas kernels for 0%

profile of v2, /device:TPU:0, one launch (start us, length us, event | category | flops | bytes accessed | tf_op | source)
XLA Modules:
  0.0 179.6 jit_solution(5596860019877046425)
XLA Ops:
  0.6 0.8 fusion.15
  1.5 0.8 fusion.16
  2.4 11.1 %all_to_all.20 = bf16[4,128,256]{2,1,0:T(8,128)(2,1)S(1)} all-to-all(bf16[4,128,256]{2,1,0:T(8,128)(2,1)S(1)} %pad_maximum_fusion.4), channel_id=1, replica_groups={{0,32,64,96},{16,48,80,112},{1,33,65,97},{17,49,81,113},{2,34,66,98},{1..., dimensions={0} | all-to-all | bytes 524288 | tf_op jit(solution)/shard_map/all_to_all | solution.py:351
  13.4 1.9 %collective-permute-start = (bf16[4,128,256]{2,1,0:T(8,128)(2,1)S(1)}, bf16[4,128,256]{2,1,0:T(8,128)(2,1)S(1)}, u32[]{:S(2)}, u32[]{:S(2)}) collective-permute-start(bf16[4,128,256]{2,1,0:T(8,128)(2,1)S(1)} %all_to_all.20), channel_id=1, source_target_pairs={{0,1},{1,2},{2,3},{3,0},{4,5},{5,6},{6,7},{7,4},{8,9},{9,10},{10,1... | collective-permute-start | bytes 786440 | tf_op jit(solution)/shard_map/ppermute | solution.py:310
  15.4 2.1 %collective-permute-start.2 = (bf16[4,128,256]{2,1,0:T(8,128)(2,1)S(1)}, bf16[4,128,256]{2,1,0:T(8,128)(2,1)S(1)}, u32[]{:S(2)}, u32[]{:S(2)}) collective-permute-start(bf16[4,128,256]{2,1,0:T(8,128)(2,1)S(1)} %all_to_all.20), channel_id=1, source_target_pairs={{0,3},{1,0},{2,1},{3,2},{4,7},{5,4},{6,5},{7,6},{8,11},{9,8},{10,9... | collective-permute-start | bytes 786440 | tf_op jit(solution)/shard_map/ppermute | solution.py:310
  17.5 1.9 %collective-permute-start.1 = (bf16[4,128,256]{2,1,0:T(8,128)(2,1)S(1)}, bf16[4,128,256]{2,1,0:T(8,128)(2,1)S(1)}, u32[]{:S(2)}, u32[]{:S(2)}) collective-permute-start(bf16[4,128,256]{2,1,0:T(8,128)(2,1)S(1)} %all_to_all.20), channel_id=1, source_target_pairs={{0,2},{1,3},{2,0},{3,1},{4,6},{5,7},{6,4},{7,5},{8,10},{9,11},{10,... | collective-permute-start | bytes 786440 | tf_op jit(solution)/shard_map/ppermute | solution.py:310
  19.3 2.5 %collective-permute-done = bf16[4,128,256]{2,1,0:T(8,128)(2,1)S(1)} collective-permute-done((bf16[4,128,256]{2,1,0:T(8,128)(2,1)S(1)}, bf16[4,128,256]{2,1,0:T(8,128)(2,1)S(1)}, u32[]{:S(2)}, u32[]{:S(2)}) %collective-permute-start) | collective-permute-done | bytes 262176 | tf_op jit(solution)/shard_map/ppermute | solution.py:310
  21.9 0.1 collective-permute-start.9
  22.0 2.8 %collective-permute-start.5 = (bf16[2,4,128,256]{3,2,1,0:T(8,128)(2,1)S(1)}, bf16[2,4,128,256]{3,2,1,0:T(8,128)(2,1)}, u32[]{:S(2)}, u32[]{:S(2)}) collective-permute-start(bf16[2,4,128,256]{3,2,1,0:T(8,128)(2,1)S(1)} %pad_maximum_fusion.2.refs_0_), channel_id=1, source_target_pairs={{0,12},{1,13},{2,14},{3,15},{4,0},{5,1},{6,2},{7,3},{8,4},{9,5},{1... | collective-permute-start | bytes 1572872 | tf_op jit(solution)/shard_map/ppermute | solution.py:310
  24.8 1.3 collective-permute-done.1
  26.2 2.8 %collective-permute-start.6 = (bf16[2,4,128,256]{3,2,1,0:T(8,128)(2,1)S(1)}, bf16[2,4,128,256]{3,2,1,0:T(8,128)(2,1)}, u32[]{:S(2)}, u32[]{:S(2)}) collective-permute-start(bf16[2,4,128,256]{3,2,1,0:T(8,128)(2,1)S(1)} %pad_maximum_fusion.3.refs_1_), channel_id=1, source_target_pairs={{0,12},{1,13},{2,14},{3,15},{4,0},{5,1},{6,2},{7,3},{8,4},{9,5},{1... | collective-permute-start | bytes 1572872 | tf_op jit(solution)/shard_map/ppermute | solution.py:310
  29.1 2.4 %collective-permute-done.5.refs_4_ = bf16[2,4,128,256]{3,2,1,0:T(8,128)(2,1)} collective-permute-done((bf16[2,4,128,256]{3,2,1,0:T(8,128)(2,1)S(1)}, bf16[2,4,128,256]{3,2,1,0:T(8,128)(2,1)}, u32[]{:S(2)}, u32[]{:S(2)}) %collective-permute-start.5) | collective-permute-done | bytes 524320 | tf_op jit(solution)/shard_map/ppermute | solution.py:310
  31.5 0.3 collective-permute-start.13
  31.8 3.5 %collective-permute-done.3.refs_2_ = bf16[2,4,128,256]{3,2,1,0:T(8,128)(2,1)} collective-permute-done((bf16[2,4,128,256]{3,2,1,0:T(8,128)(2,1)S(1)}, bf16[2,4,128,256]{3,2,1,0:T(8,128)(2,1)}, u32[]{:S(2)}, u32[]{:S(2)}) %collective-permute-start.3) | collective-permute-done | bytes 524320 | tf_op jit(solution)/shard_map/ppermute | solution.py:310
  35.3 1.8 %collective-permute-done.6.refs_5_ = bf16[2,4,128,256]{3,2,1,0:T(8,128)(2,1)} collective-permute-done((bf16[2,4,128,256]{3,2,1,0:T(8,128)(2,1)S(1)}, bf16[2,4,128,256]{3,2,1,0:T(8,128)(2,1)}, u32[]{:S(2)}, u32[]{:S(2)}) %collective-permute-start.6) | collective-permute-done | bytes 524320 | tf_op jit(solution)/shard_map/ppermute | solution.py:310
  37.1 3.8 %collective-permute-start.8 = (bf16[2,4,128,256]{3,2,1,0:T(8,128)(2,1)}, bf16[2,4,128,256]{3,2,1,0:T(8,128)(2,1)}, u32[]{:S(2)}, u32[]{:S(2)}) collective-permute-start(bf16[2,4,128,256]{3,2,1,0:T(8,128)(2,1)} %collective-permute-done.6.refs_5_), channel_id=1, source_target_pairs={{0,12},{1,13},{2,14},{3,15},{4,0},{5,1},{6,2},{7,3},{8,4},{9,5},{1... | collective-permute-start | bytes 1572872 | tf_op jit(solution)/shard_map/ppermute | solution.py:310
  41.0 0.7 convert_bitcast_fusion
  41.8 1.1 pad_maximum_fusion
  42.9 3.5 %all-to-all-start = ((bf16[4,144,768]{2,1,0:T(8,128)(2,1)}), bf16[4,144,768]{2,1,0:T(8,128)(2,1)S(1)}, u32[]{:S(2)}, u32[]{:S(2)}) async-start(bf16[4,144,768]{2,1,0:T(8,128)(2,1)} %pad_maximum_fusion), calls=%async_computation | async-start | bytes 1769472 | tf_op jit(solution)/shard_map/all_to_all | solution.py:351
  46.5 0.5 collective-permute-start.14
  47.0 0.1 collective-permute-start.12
  47.1 0.4 collective-permute-start.15
  47.5 0.4 collective-permute-done.8.refs_7_
  47.9 0.6 pad_add_fusion.ids
  48.5 10.2 %all-to-all-done.both = bf16[4,144,768]{2,1,0:T(8,128)(2,1)S(1)} async-done(((bf16[4,144,768]{2,1,0:T(8,128)(2,1)}), bf16[4,144,768]{2,1,0:T(8,128)(2,1)S(1)}, u32[]{:S(2)}, u32[]{:S(2)}) %all-to-all-start) | async-done | bytes 884768 | tf_op jit(solution)/shard_map/all_to_all | solution.py:351
  58.8 0.9 copy-done
  59.7 0.2 copy-done.18
  59.9 0.2 copy-done.19
  60.1 40.3 %shard_map.102 = (bf16[4,128,384]{2,1,0:T(8,128)(2,1)}, bf16[4,128,384]{2,1,0:T(8,128)(2,1)}, bf16[2,4,256,128]{3,2,1,0:T(8,128)(2,1)}, bf16[2,4,256,128]{3,2,1,...) custom-call(s32[2]{0:T(128)} %pad_add_fusion.ids, ...), custom_call_target="tpu_custom_call" | custom-call | flops 14495514624 | bytes 16777216 | tf_op jit(solution)/shard_map/pallas_call | solution.py:262
  100.5 4.8 %collective-permute-start.21 = (bf16[2,4,256,128]{3,2,1,0:T(8,128)(2,1)}, bf16[2,4,256,128]{3,2,1,0:T(8,128)(2,1)S(1)}, u32[]{:S(2)}, u32[]{:S(2)}) collective-permute-start(bf16[2,4,256,128]{3,2,1,0:T(8,128)(2,1)} %get-tuple-element.31), channel_id=1, source_target_pairs={{0,16},{16,0},{32,48},{48,32},{64,80},{80,64},{96,112},{112,96},{1... | collective-permute-start | bytes 1572872 | tf_op jit(solution)/shard_map/ppermute | solution.py:391
  105.2 0.3 collective-permute-start.18
  105.5 2.1 %pad_maximum_fusion.1 = bf16[4,128,768]{2,1,0:T(8,128)(2,1)} fusion(bf16[4,128,384]{2,1,0:T(8,128)(2,1)} %get-tuple-element.23, bf16[4,128,384]{2,1,0:T(8,128)(2,1)} %get-tuple-element.22), kind=kLoop, calls=%fused_computation.9 | loop fusion | flops 1572864 | bytes 1572864 | tf_op jit(solution)/shard_map/concatenate | solution.py:400
  107.6 3.6 %all-to-all-start.2 = ((bf16[4,128,768]{2,1,0:T(8,128)(2,1)}), bf16[4,128,768]{2,1,0:T(8,128)(2,1)S(1)}, u32[]{:S(2)}, u32[]{:S(2)}) async-start(bf16[4,128,768]{2,1,0:T(8,128)(2,1)} %pad_maximum_fusion.1), calls=%async_computation.2 | async-start | bytes 1572864 | tf_op jit(solution)/shard_map/all_to_all | solution.py:351
  111.2 0.3 collective-permute-start.17
  111.6 0.3 collective-permute-start.20
  111.8 0.2 collective-permute-start.26
  112.1 0.3 collective-permute-start.29
  112.3 0.1 add_convert_fusion.6
  112.5 12.2 %collective-permute-start.22 = (bf16[2,4,256,128]{3,2,1,0:T(8,128)(2,1)S(1)}, bf16[2,4,256,128]{3,2,1,0:T(8,128)(2,1)S(1)}, u32[]{:S(2)}, u32[]{:S(2)}) collective-permute-start(bf16[2,4,256,128]{3,2,1,0:T(8,128)(2,1)S(1)} %add_convert_fusion.6), channel_id=1, source_target_pairs={{0,12},{1,13},{2,14},{3,15},{4,0},{5,1},{6,2},{7,3},{8,4},{9,5},{1... | collective-permute-start | bytes 1572872 | tf_op jit(solution)/shard_map/ppermute | solution.py:310
  124.7 0.1 add_convert_fusion.7
  125.0 0.1 add_convert_fusion.2
  125.2 6.2 %collective-permute-done.22 = bf16[2,4,256,128]{3,2,1,0:T(8,128)(2,1)S(1)} collective-permute-done((bf16[2,4,256,128]{3,2,1,0:T(8,128)(2,1)S(1)}, bf16[2,4,256,128]{3,2,1,0:T(8,128)(2,1)S(1)}, u32[]{:S(2)}, u32[]{:S(2)}) %collective-permute-start.22) | collective-permute-done | bytes 524320 | tf_op jit(solution)/shard_map/ppermute | solution.py:310
  131.4 0.2 add_convert_fusion.5
  131.6 3.8 %collective-permute-start.23 = (bf16[2,4,256,128]{3,2,1,0:T(8,128)(2,1)S(1)}, bf16[2,4,256,128]{3,2,1,0:T(8,128)(2,1)S(1)}, u32[]{:S(2)}, u32[]{:S(2)}) collective-permute-start(bf16[2,4,256,128]{3,2,1,0:T(8,128)(2,1)S(1)} %add_convert_fusion.5), channel_id=1, source_target_pairs={{0,12},{1,13},{2,14},{3,15},{4,0},{5,1},{6,2},{7,3},{8,4},{9,5},{1... | collective-permute-start | bytes 1572872 | tf_op jit(solution)/shard_map/ppermute | solution.py:310
  135.4 0.1 add_convert_fusion.3
  135.6 0.1 collective-permute-start.25
  135.7 6.6 %collective-permute-done.30 = bf16[2,4,256,128]{3,2,1,0:T(8,128)(2,1)S(1)} collective-permute-done((bf16[2,4,256,128]{3,2,1,0:T(8,128)(2,1)S(1)}, bf16[2,4,256,128]{3,2,1,0:T(8,128)(2,1)S(1)}, u32[]{:S(2)}, u32[]{:S(2)}) %collective-permute-start.30) | collective-permute-done | bytes 524320 | tf_op jit(solution)/shard_map/ppermute | solution.py:310
  142.2 2.0 %collective-permute-start.27 = (bf16[2,4,256,128]{3,2,1,0:T(8,128)(2,1)S(1)}, bf16[2,4,256,128]{3,2,1,0:T(8,128)(2,1)S(1)}, u32[]{:S(2)}, u32[]{:S(2)}) collective-permute-start(bf16[2,4,256,128]{3,2,1,0:T(8,128)(2,1)S(1)} %add_convert_fusion.3), channel_id=1, source_target_pairs={{0,12},{1,13},{2,14},{3,15},{4,0},{5,1},{6,2},{7,3},{8,4},{9,5},{1... | collective-permute-start | bytes 1572872 | tf_op jit(solution)/shard_map/ppermute | solution.py:310
  144.3 0.2 add_convert_fusion.1
  144.6 0.7 copy-done.2
  145.3 0.3 add_convert_fusion.4
  145.7 8.3 %collective-permute-done.27 = bf16[2,4,256,128]{3,2,1,0:T(8,128)(2,1)S(1)} collective-permute-done((bf16[2,4,256,128]{3,2,1,0:T(8,128)(2,1)S(1)}, bf16[2,4,256,128]{3,2,1,0:T(8,128)(2,1)S(1)}, u32[]{:S(2)}, u32[]{:S(2)}) %collective-permute-start.27) | collective-permute-done | bytes 524320 | tf_op jit(solution)/shard_map/ppermute | solution.py:310
  154.0 1.0 collective-permute-done.31
  155.0 0.3 add_convert_fusion
  155.4 2.5 %collective-permute-start.33 = (bf16[4,256,128]{2,1,0:T(8,128)(2,1)S(1)}, bf16[4,256,128]{2,1,0:T(8,128)(2,1)S(1)}, u32[]{:S(2)}, u32[]{:S(2)}) collective-permute-start(bf16[4,256,128]{2,1,0:T(8,128)(2,1)S(1)} %get-tuple-element.53), channel_id=1, source_target_pairs={{0,2},{1,3},{2,0},{3,1},{4,6},{5,7},{6,4},{7,5},{8,10},{9,11},{10,... | collective-permute-start | bytes 786440 | tf_op jit(solution)/shard_map/ppermute | solution.py:310
  157.9 0.1 slice_bitcast_fusion.7
  158.0 0.8 maximum_bitcast_fusion.1
  158.8 7.0 %collective-permute-done.32 = bf16[4,256,128]{2,1,0:T(8,128)(2,1)S(1)} collective-permute-done((bf16[4,256,128]{2,1,0:T(8,128)(2,1)S(1)}, bf16[4,256,128]{2,1,0:T(8,128)(2,1)S(1)}, u32[]{:S(2)}, u32[]{:S(2)}) %collective-permute-start.32) | collective-permute-done | bytes 262176 | tf_op jit(solution)/shard_map/ppermute | solution.py:310
  165.8 0.8 fusion.2
  166.7 4.7 %all-to-all-start.3 = ((bf16[4,256,128]{2,1,0:T(8,128)(2,1)}), bf16[4,256,128]{2,1,0:T(8,128)(2,1)S(1)}, u32[]{:S(2)}, u32[]{:S(2)}) async-start(bf16[4,256,128]{2,1,0:T(8,128)(2,1)} %fusion.2), calls=%async_computation.3 | async-start | bytes 524288 | tf_op jit(solution)/shard_map/all_to_all | solution.py:351
  171.3 0.8 maximum_bitcast_fusion
  172.1 5.9 %all-to-all-done.3 = bf16[4,256,128]{2,1,0:T(8,128)(2,1)S(1)} async-done(((bf16[4,256,128]{2,1,0:T(8,128)(2,1)}), bf16[4,256,128]{2,1,0:T(8,128)(2,1)S(1)}, u32[]{:S(2)}, u32[]{:S(2)}) %all-to-all-start.3) | async-done | bytes 262176 | tf_op jit(solution)/shard_map/all_to_all | solution.py:351
  178.0 0.8 copy.12
  178.8 0.8 copy.11
  (82 shorter events, 1.1 us)
Async XLA Ops:
  13.4 8.4 %collective-permute-start = (bf16[4,128,256]{2,1,0:T(8,128)(2,1)S(1)}, bf16[4,128,256]{2,1,0:T(8,128)(2,1)S(1)}, u32[]{:S(2)}, u32[]{:S(2)}) collective-permute-start(bf16[4,128,256]{2,1,0:T(8,128)(2,1)S(1)} %all_to_all.20), channel_id=1, source_target_pairs={{0,1},{1,2},{2,3},{3,0},{4,5},{5,6},{6,7},{7,4},{8,9},{9,10},{10,1... | collective-permute-start | bytes 786440 | tf_op jit(solution)/shard_map/ppermute | solution.py:310
  15.4 9.5 %collective-permute-start.2 = (bf16[4,128,256]{2,1,0:T(8,128)(2,1)S(1)}, bf16[4,128,256]{2,1,0:T(8,128)(2,1)S(1)}, u32[]{:S(2)}, u32[]{:S(2)}) collective-permute-start(bf16[4,128,256]{2,1,0:T(8,128)(2,1)S(1)} %all_to_all.20), channel_id=1, source_target_pairs={{0,3},{1,0},{2,1},{3,2},{4,7},{5,4},{6,5},{7,6},{8,11},{9,8},{10,9... | collective-permute-start | bytes 786440 | tf_op jit(solution)/shard_map/ppermute | solution.py:310
  17.5 8.6 %collective-permute-start.1 = (bf16[4,128,256]{2,1,0:T(8,128)(2,1)S(1)}, bf16[4,128,256]{2,1,0:T(8,128)(2,1)S(1)}, u32[]{:S(2)}, u32[]{:S(2)}) collective-permute-start(bf16[4,128,256]{2,1,0:T(8,128)(2,1)S(1)} %all_to_all.20), channel_id=1, source_target_pairs={{0,2},{1,3},{2,0},{3,1},{4,6},{5,7},{6,4},{7,5},{8,10},{9,11},{10,... | collective-permute-start | bytes 786440 | tf_op jit(solution)/shard_map/ppermute | solution.py:310
  21.8 19.1 %copy-start.11 = (bf16[1,128,1536]{2,1,0:T(8,128)(2,1)S(1)}, bf16[1,128,1536]{2,1,0:T(8,128)(2,1)}, u32[]{:S(2)}) copy-start(bf16[1,128,1536]{2,1,0:T(8,128)(2,1)} %param.7) | copy-start | bytes 1179652
  21.8 19.1 %copy-start.12 = (bf16[1,128,1536]{2,1,0:T(8,128)(2,1)S(1)}, bf16[1,128,1536]{2,1,0:T(8,128)(2,1)}, u32[]{:S(2)}) copy-start(bf16[1,128,1536]{2,1,0:T(8,128)(2,1)} %param.10) | copy-start | bytes 1179652
  21.9 19.1 %copy-start.7 = (bf16[2,4,128,256]{3,2,1,0:T(8,128)(2,1)}, bf16[2,4,128,256]{3,2,1,0:T(8,128)(2,1)S(1)}, u32[]{:S(2)}) copy-start(bf16[2,4,128,256]{3,2,1,0:T(8,128)(2,1)S(1)} %pad_maximum_fusion.2.refs_0_) | copy-start | bytes 1572868
  21.9 7.1 %collective-permute-start.9 = (bf16[2,4,128,256]{3,2,1,0:T(8,128)(2,1)S(1)}, bf16[2,4,128,256]{3,2,1,0:T(8,128)(2,1)S(1)}, u32[]{:S(2)}, u32[]{:S(2)}) collective-permute-start(bf16[2,4,128,256]{3,2,1,0:T(8,128)(2,1)S(1)} %pad_maximum_fusion.2.refs_0_), channel_id=1, source_target_pairs={{0,16},{16,0},{32,48},{48,32},{64,80},{80,64},{96,112},{112,96},{1... | collective-permute-start | bytes 1572872 | tf_op jit(solution)/shard_map/ppermute | solution.py:367
  22.0 9.5 %collective-permute-start.5 = (bf16[2,4,128,256]{3,2,1,0:T(8,128)(2,1)S(1)}, bf16[2,4,128,256]{3,2,1,0:T(8,128)(2,1)}, u32[]{:S(2)}, u32[]{:S(2)}) collective-permute-start(bf16[2,4,128,256]{3,2,1,0:T(8,128)(2,1)S(1)} %pad_maximum_fusion.2.refs_0_), channel_id=1, source_target_pairs={{0,12},{1,13},{2,14},{3,15},{4,0},{5,1},{6,2},{7,3},{8,4},{9,5},{1... | collective-permute-start | bytes 1572872 | tf_op jit(solution)/shard_map/ppermute | solution.py:310
  24.8 10.5 %collective-permute-start.3 = (bf16[2,4,128,256]{3,2,1,0:T(8,128)(2,1)S(1)}, bf16[2,4,128,256]{3,2,1,0:T(8,128)(2,1)}, u32[]{:S(2)}, u32[]{:S(2)}) collective-permute-start(bf16[2,4,128,256]{3,2,1,0:T(8,128)(2,1)S(1)} %pad_maximum_fusion.2.refs_0_), channel_id=1, source_target_pairs={{0,4},{1,5},{2,6},{3,7},{4,8},{5,9},{6,10},{7,11},{8,12},{9,13},{1... | collective-permute-start | bytes 1572872 | tf_op jit(solution)/shard_map/ppermute | solution.py:310
  26.1 15.7 %copy-start.8 = (bf16[2,4,128,256]{3,2,1,0:T(8,128)(2,1)}, bf16[2,4,128,256]{3,2,1,0:T(8,128)(2,1)S(1)}, u32[]{:S(2)}) copy-start(bf16[2,4,128,256]{3,2,1,0:T(8,128)(2,1)S(1)} %pad_maximum_fusion.3.refs_1_) | copy-start | bytes 1572868
  26.2 11.0 %collective-permute-start.6 = (bf16[2,4,128,256]{3,2,1,0:T(8,128)(2,1)S(1)}, bf16[2,4,128,256]{3,2,1,0:T(8,128)(2,1)}, u32[]{:S(2)}, u32[]{:S(2)}) collective-permute-start(bf16[2,4,128,256]{3,2,1,0:T(8,128)(2,1)S(1)} %pad_maximum_fusion.3.refs_1_), channel_id=1, source_target_pairs={{0,12},{1,13},{2,14},{3,15},{4,0},{5,1},{6,2},{7,3},{8,4},{9,5},{1... | collective-permute-start | bytes 1572872 | tf_op jit(solution)/shard_map/ppermute | solution.py:310
  29.0 17.4 %collective-permute-start.10 = (bf16[2,4,128,256]{3,2,1,0:T(8,128)(2,1)S(1)}, bf16[2,4,128,256]{3,2,1,0:T(8,128)(2,1)}, u32[]{:S(2)}, u32[]{:S(2)}) collective-permute-start(bf16[2,4,128,256]{3,2,1,0:T(8,128)(2,1)S(1)} %pad_maximum_fusion.3.refs_1_), channel_id=1, source_target_pairs={{0,16},{16,0},{32,48},{48,32},{64,80},{80,64},{96,112},{112,96},{1... | collective-permute-start | bytes 1572872 | tf_op jit(solution)/shard_map/ppermute | solution.py:367
  29.0 11.9 %copy-start.13 = (bf16[2,4,128,256]{3,2,1,0:T(8,128)(2,1)}, bf16[2,4,128,256]{3,2,1,0:T(8,128)(2,1)S(1)}, u32[]{:S(2)}) copy-start(bf16[2,4,128,256]{3,2,1,0:T(8,128)(2,1)S(1)} %collective-permute-done.9.refs_8_) | copy-start | bytes 1572868
  29.0 17.5 %collective-permute-start.4 = (bf16[2,4,128,256]{3,2,1,0:T(8,128)(2,1)S(1)}, bf16[2,4,128,256]{3,2,1,0:T(8,128)(2,1)}, u32[]{:S(2)}, u32[]{:S(2)}) collective-permute-start(bf16[2,4,128,256]{3,2,1,0:T(8,128)(2,1)S(1)} %pad_maximum_fusion.3.refs_1_), channel_id=1, source_target_pairs={{0,4},{1,5},{2,6},{3,7},{4,8},{5,9},{6,10},{7,11},{8,12},{9,13},{1... | collective-permute-start | bytes 1572872 | tf_op jit(solution)/shard_map/ppermute | solution.py:310
  31.5 15.5 %collective-permute-start.13 = (bf16[2,4,128,256]{3,2,1,0:T(8,128)(2,1)}, bf16[2,4,128,256]{3,2,1,0:T(8,128)(2,1)}, u32[]{:S(2)}, u32[]{:S(2)}) collective-permute-start(bf16[2,4,128,256]{3,2,1,0:T(8,128)(2,1)} %collective-permute-done.5.refs_4_), channel_id=1, source_target_pairs={{0,16},{16,0},{32,48},{48,32},{64,80},{80,64},{96,112},{112,96},{1... | collective-permute-start | bytes 1572872 | tf_op jit(solution)/shard_map/ppermute | solution.py:367
  35.3 11.8 %collective-permute-start.7 = (bf16[2,4,128,256]{3,2,1,0:T(8,128)(2,1)}, bf16[2,4,128,256]{3,2,1,0:T(8,128)(2,1)}, u32[]{:S(2)}, u32[]{:S(2)}) collective-permute-start(bf16[2,4,128,256]{3,2,1,0:T(8,128)(2,1)} %collective-permute-done.3.refs_2_), channel_id=1, source_target_pairs={{0,4},{1,5},{2,6},{3,7},{4,8},{5,9},{6,10},{7,11},{8,12},{9,13},{1... | collective-permute-start | bytes 1572872 | tf_op jit(solution)/shard_map/ppermute | solution.py:310
  37.1 10.8 %collective-permute-start.8 = (bf16[2,4,128,256]{3,2,1,0:T(8,128)(2,1)}, bf16[2,4,128,256]{3,2,1,0:T(8,128)(2,1)}, u32[]{:S(2)}, u32[]{:S(2)}) collective-permute-start(bf16[2,4,128,256]{3,2,1,0:T(8,128)(2,1)} %collective-permute-done.6.refs_5_), channel_id=1, source_target_pairs={{0,12},{1,13},{2,14},{3,15},{4,0},{5,1},{6,2},{7,3},{8,4},{9,5},{1... | collective-permute-start | bytes 1572872 | tf_op jit(solution)/shard_map/ppermute | solution.py:310
  42.9 15.8 %all-to-all-start = ((bf16[4,144,768]{2,1,0:T(8,128)(2,1)}), bf16[4,144,768]{2,1,0:T(8,128)(2,1)S(1)}, u32[]{:S(2)}, u32[]{:S(2)}) async-start(bf16[4,144,768]{2,1,0:T(8,128)(2,1)} %pad_maximum_fusion), calls=%async_computation | async-start | bytes 1769472 | tf_op jit(solution)/shard_map/all_to_all | solution.py:351
  46.4 12.3 %collective-permute-start.11 = (bf16[2,4,128,256]{3,2,1,0:T(8,128)(2,1)}, bf16[2,4,128,256]{3,2,1,0:T(8,128)(2,1)S(1)}, u32[]{:S(2)}, u32[]{:S(2)}) collective-permute-start(bf16[2,4,128,256]{3,2,1,0:T(8,128)(2,1)} %collective-permute-done.3.refs_2_), channel_id=1, source_target_pairs={{0,16},{16,0},{32,48},{48,32},{64,80},{80,64},{96,112},{112,96},{1... | collective-permute-start | bytes 1572872 | tf_op jit(solution)/shard_map/ppermute | solution.py:367
  46.5 12.2 %collective-permute-start.14 = (bf16[2,4,128,256]{3,2,1,0:T(8,128)(2,1)}, bf16[2,4,128,256]{3,2,1,0:T(8,128)(2,1)S(1)}, u32[]{:S(2)}, u32[]{:S(2)}) collective-permute-start(bf16[2,4,128,256]{3,2,1,0:T(8,128)(2,1)} %collective-permute-done.6.refs_5_), channel_id=1, source_target_pairs={{0,16},{16,0},{32,48},{48,32},{64,80},{80,64},{96,112},{112,96},{1... | collective-permute-start | bytes 1572872 | tf_op jit(solution)/shard_map/ppermute | solution.py:367
  47.0 11.7 %collective-permute-start.12 = (bf16[2,4,128,256]{3,2,1,0:T(8,128)(2,1)}, bf16[2,4,128,256]{3,2,1,0:T(8,128)(2,1)}, u32[]{:S(2)}, u32[]{:S(2)}) collective-permute-start(bf16[2,4,128,256]{3,2,1,0:T(8,128)(2,1)} %collective-permute-done.4.refs_3_), channel_id=1, source_target_pairs={{0,16},{16,0},{32,48},{48,32},{64,80},{80,64},{96,112},{112,96},{1... | collective-permute-start | bytes 1572872 | tf_op jit(solution)/shard_map/ppermute | solution.py:367
  47.1 11.6 %collective-permute-start.15 = (bf16[2,4,128,256]{3,2,1,0:T(8,128)(2,1)}, bf16[2,4,128,256]{3,2,1,0:T(8,128)(2,1)}, u32[]{:S(2)}, u32[]{:S(2)}) collective-permute-start(bf16[2,4,128,256]{3,2,1,0:T(8,128)(2,1)} %collective-permute-done.7.refs_6_), channel_id=1, source_target_pairs={{0,16},{16,0},{32,48},{48,32},{64,80},{80,64},{96,112},{112,96},{1... | collective-permute-start | bytes 1572872 | tf_op jit(solution)/shard_map/ppermute | solution.py:367
  47.9 10.8 %collective-permute-start.16 = (bf16[2,4,128,256]{3,2,1,0:T(8,128)(2,1)}, bf16[2,4,128,256]{3,2,1,0:T(8,128)(2,1)}, u32[]{:S(2)}, u32[]{:S(2)}) collective-permute-start(bf16[2,4,128,256]{3,2,1,0:T(8,128)(2,1)} %collective-permute-done.8.refs_7_), channel_id=1, source_target_pairs={{0,16},{16,0},{32,48},{48,32},{64,80},{80,64},{96,112},{112,96},{1... | collective-permute-start | bytes 1572872 | tf_op jit(solution)/shard_map/ppermute | solution.py:367
  58.7 1.0 copy-start
  58.7 1.1 copy-start.18
  58.7 1.4 copy-start.19
  100.5 11.6 %collective-permute-start.21 = (bf16[2,4,256,128]{3,2,1,0:T(8,128)(2,1)}, bf16[2,4,256,128]{3,2,1,0:T(8,128)(2,1)S(1)}, u32[]{:S(2)}, u32[]{:S(2)}) collective-permute-start(bf16[2,4,256,128]{3,2,1,0:T(8,128)(2,1)} %get-tuple-element.31), channel_id=1, source_target_pairs={{0,16},{16,0},{32,48},{48,32},{64,80},{80,64},{96,112},{112,96},{1... | collective-permute-start | bytes 1572872 | tf_op jit(solution)/shard_map/ppermute | solution.py:391
  105.2 7.3 %collective-permute-start.18 = (bf16[2,4,256,128]{3,2,1,0:T(8,128)(2,1)}, bf16[2,4,256,128]{3,2,1,0:T(8,128)(2,1)S(1)}, u32[]{:S(2)}, u32[]{:S(2)}) collective-permute-start(bf16[2,4,256,128]{3,2,1,0:T(8,128)(2,1)} %get-tuple-element.27), channel_id=1, source_target_pairs={{0,16},{16,0},{32,48},{48,32},{64,80},{80,64},{96,112},{112,96},{1... | collective-permute-start | bytes 1572872 | tf_op jit(solution)/shard_map/ppermute | solution.py:391
  107.6 3.7 %copy-start.15 = (bf16[2,4,256,128]{3,2,1,0:T(8,128)(2,1)S(1)}, bf16[2,4,256,128]{3,2,1,0:T(8,128)(2,1)}, u32[]{:S(2)}) copy-start(bf16[2,4,256,128]{3,2,1,0:T(8,128)(2,1)} %get-tuple-element.25) | copy-start | bytes 1572868
  107.6 4.2 %copy-start.17 = (bf16[2,4,256,128]{3,2,1,0:T(8,128)(2,1)S(1)}, bf16[2,4,256,128]{3,2,1,0:T(8,128)(2,1)}, u32[]{:S(2)}) copy-start(bf16[2,4,256,128]{3,2,1,0:T(8,128)(2,1)} %get-tuple-element.35) | copy-start | bytes 1572868
  107.6 4.8 %copy-start.6 = (bf16[2,4,256,128]{3,2,1,0:T(8,128)(2,1)S(1)}, bf16[2,4,256,128]{3,2,1,0:T(8,128)(2,1)}, u32[]{:S(2)}) copy-start(bf16[2,4,256,128]{3,2,1,0:T(8,128)(2,1)} %get-tuple-element.30) | copy-start | bytes 1572868
  107.6 50.4 %all-to-all-start.2 = ((bf16[4,128,768]{2,1,0:T(8,128)(2,1)}), bf16[4,128,768]{2,1,0:T(8,128)(2,1)S(1)}, u32[]{:S(2)}, u32[]{:S(2)}) async-start(bf16[4,128,768]{2,1,0:T(8,128)(2,1)} %pad_maximum_fusion.1), calls=%async_computation.2 | async-start | bytes 1572864 | tf_op jit(solution)/shard_map/all_to_all | solution.py:351
  111.2 13.5 %copy-start.5 = (bf16[2,4,256,128]{3,2,1,0:T(8,128)(2,1)S(1)}, bf16[2,4,256,128]{3,2,1,0:T(8,128)(2,1)}, u32[]{:S(2)}) copy-start(bf16[2,4,256,128]{3,2,1,0:T(8,128)(2,1)} %get-tuple-element.26) | copy-start | bytes 1572868
  111.2 33.3 %collective-permute-start.17 = (bf16[2,4,256,128]{3,2,1,0:T(8,128)(2,1)S(1)}, bf16[2,4,256,128]{3,2,1,0:T(8,128)(2,1)S(1)}, u32[]{:S(2)}, u32[]{:S(2)}) collective-permute-start(bf16[2,4,256,128]{3,2,1,0:T(8,128)(2,1)S(1)} %copy-done.15), channel_id=1, source_target_pairs={{0,16},{16,0},{32,48},{48,32},{64,80},{80,64},{96,112},{112,96},{1... | collective-permute-start | bytes 1572872 | tf_op jit(solution)/shard_map/ppermute | solution.py:391
  111.6 13.6 %collective-permute-start.20 = (bf16[2,4,256,128]{3,2,1,0:T(8,128)(2,1)}, bf16[2,4,256,128]{3,2,1,0:T(8,128)(2,1)S(1)}, u32[]{:S(2)}, u32[]{:S(2)}) collective-permute-start(bf16[2,4,256,128]{3,2,1,0:T(8,128)(2,1)} %get-tuple-element.29), channel_id=1, source_target_pairs={{0,16},{16,0},{32,48},{48,32},{64,80},{80,64},{96,112},{112,96},{1... | collective-permute-start | bytes 1572872 | tf_op jit(solution)/shard_map/ppermute | solution.py:391
  111.8 19.8 %collective-permute-start.26 = (bf16[2,4,256,128]{3,2,1,0:T(8,128)(2,1)S(1)}, bf16[2,4,256,128]{3,2,1,0:T(8,128)(2,1)S(1)}, u32[]{:S(2)}, u32[]{:S(2)}) collective-permute-start(bf16[2,4,256,128]{3,2,1,0:T(8,128)(2,1)S(1)} %copy-done.17), channel_id=1, source_target_pairs={{0,16},{16,0},{32,48},{48,32},{64,80},{80,64},{96,112},{112,96},{1... | collective-permute-start | bytes 1572872 | tf_op jit(solution)/shard_map/ppermute | solution.py:391
  112.1 12.8 %collective-permute-start.29 = (bf16[2,4,256,128]{3,2,1,0:T(8,128)(2,1)}, bf16[2,4,256,128]{3,2,1,0:T(8,128)(2,1)S(1)}, u32[]{:S(2)}, u32[]{:S(2)}) collective-permute-start(bf16[2,4,256,128]{3,2,1,0:T(8,128)(2,1)} %get-tuple-element.39), channel_id=1, source_target_pairs={{0,16},{16,0},{32,48},{48,32},{64,80},{80,64},{96,112},{112,96},{1... | collective-permute-start | bytes 1572872 | tf_op jit(solution)/shard_map/ppermute | solution.py:391
  112.5 12.4 %copy-start.16 = (bf16[2,4,256,128]{3,2,1,0:T(8,128)(2,1)S(1)}, bf16[2,4,256,128]{3,2,1,0:T(8,128)(2,1)}, u32[]{:S(2)}) copy-start(bf16[2,4,256,128]{3,2,1,0:T(8,128)(2,1)} %get-tuple-element.37) | copy-start | bytes 1572868
  112.5 12.5 %copy-start.4 = (bf16[2,4,256,128]{3,2,1,0:T(8,128)(2,1)S(1)}, bf16[2,4,256,128]{3,2,1,0:T(8,128)(2,1)}, u32[]{:S(2)}) copy-start(bf16[2,4,256,128]{3,2,1,0:T(8,128)(2,1)} %get-tuple-element.38) | copy-start | bytes 1572868
  112.5 18.9 %collective-permute-start.22 = (bf16[2,4,256,128]{3,2,1,0:T(8,128)(2,1)S(1)}, bf16[2,4,256,128]{3,2,1,0:T(8,128)(2,1)S(1)}, u32[]{:S(2)}, u32[]{:S(2)}) collective-permute-start(bf16[2,4,256,128]{3,2,1,0:T(8,128)(2,1)S(1)} %add_convert_fusion.6), channel_id=1, source_target_pairs={{0,12},{1,13},{2,14},{3,15},{4,0},{5,1},{6,2},{7,3},{8,4},{9,5},{1... | collective-permute-start | bytes 1572872 | tf_op jit(solution)/shard_map/ppermute | solution.py:310
  124.8 6.6 %copy-start.10 = (bf16[2,4,256,128]{3,2,1,0:T(8,128)(2,1)S(1)}, bf16[2,4,256,128]{3,2,1,0:T(8,128)(2,1)}, u32[]{:S(2)}) copy-start(bf16[2,4,256,128]{3,2,1,0:T(8,128)(2,1)} %get-tuple-element.28) | copy-start | bytes 1572868
  124.9 10.7 %collective-permute-start.28 = (bf16[2,4,256,128]{3,2,1,0:T(8,128)(2,1)S(1)}, bf16[2,4,256,128]{3,2,1,0:T(8,128)(2,1)S(1)}, u32[]{:S(2)}, u32[]{:S(2)}) collective-permute-start(bf16[2,4,256,128]{3,2,1,0:T(8,128)(2,1)S(1)} %copy-done.16), channel_id=1, source_target_pairs={{0,16},{16,0},{32,48},{48,32},{64,80},{80,64},{96,112},{112,96},{1... | collective-permute-start | bytes 1572872 | tf_op jit(solution)/shard_map/ppermute | solution.py:391
  125.1 19.4 %collective-permute-start.19 = (bf16[2,4,256,128]{3,2,1,0:T(8,128)(2,1)S(1)}, bf16[2,4,256,128]{3,2,1,0:T(8,128)(2,1)S(1)}, u32[]{:S(2)}, u32[]{:S(2)}) collective-permute-start(bf16[2,4,256,128]{3,2,1,0:T(8,128)(2,1)S(1)} %add_convert_fusion.7), channel_id=1, source_target_pairs={{0,4},{1,5},{2,6},{3,7},{4,8},{5,9},{6,10},{7,11},{8,12},{9,13},{1... | collective-permute-start | bytes 1572872 | tf_op jit(solution)/shard_map/ppermute | solution.py:310
  131.4 10.8 %collective-permute-start.30 = (bf16[2,4,256,128]{3,2,1,0:T(8,128)(2,1)S(1)}, bf16[2,4,256,128]{3,2,1,0:T(8,128)(2,1)S(1)}, u32[]{:S(2)}, u32[]{:S(2)}) collective-permute-start(bf16[2,4,256,128]{3,2,1,0:T(8,128)(2,1)S(1)} %add_convert_fusion.2), channel_id=1, source_target_pairs={{0,4},{1,5},{2,6},{3,7},{4,8},{5,9},{6,10},{7,11},{8,12},{9,13},{1... | collective-permute-start | bytes 1572872 | tf_op jit(solution)/shard_map/ppermute | solution.py:310
  131.4 4.0 %copy-start.3 = (bf16[2,4,256,128]{3,2,1,0:T(8,128)(2,1)S(1)}, bf16[2,4,256,128]{3,2,1,0:T(8,128)(2,1)}, u32[]{:S(2)}) copy-start(bf16[2,4,256,128]{3,2,1,0:T(8,128)(2,1)} %get-tuple-element.34) | copy-start | bytes 1572868
  131.6 4.0 %copy-start.14 = (bf16[2,4,256,128]{3,2,1,0:T(8,128)(2,1)S(1)}, bf16[2,4,256,128]{3,2,1,0:T(8,128)(2,1)}, u32[]{:S(2)}) copy-start(bf16[2,4,256,128]{3,2,1,0:T(8,128)(2,1)} %get-tuple-element.33) | copy-start | bytes 1572868
  131.6 12.6 %copy-start.9 = (bf16[2,4,256,128]{3,2,1,0:T(8,128)(2,1)S(1)}, bf16[2,4,256,128]{3,2,1,0:T(8,128)(2,1)}, u32[]{:S(2)}) copy-start(bf16[2,4,256,128]{3,2,1,0:T(8,128)(2,1)} %get-tuple-element.36) | copy-start | bytes 1572868
  131.6 12.9 %collective-permute-start.23 = (bf16[2,4,256,128]{3,2,1,0:T(8,128)(2,1)S(1)}, bf16[2,4,256,128]{3,2,1,0:T(8,128)(2,1)S(1)}, u32[]{:S(2)}, u32[]{:S(2)}) collective-permute-start(bf16[2,4,256,128]{3,2,1,0:T(8,128)(2,1)S(1)} %add_convert_fusion.5), channel_id=1, source_target_pairs={{0,12},{1,13},{2,14},{3,15},{4,0},{5,1},{6,2},{7,3},{8,4},{9,5},{1... | collective-permute-start | bytes 1572872 | tf_op jit(solution)/shard_map/ppermute | solution.py:310
  135.6 10.1 %collective-permute-start.25 = (bf16[2,4,256,128]{3,2,1,0:T(8,128)(2,1)S(1)}, bf16[2,4,256,128]{3,2,1,0:T(8,128)(2,1)S(1)}, u32[]{:S(2)}, u32[]{:S(2)}) collective-permute-start(bf16[2,4,256,128]{3,2,1,0:T(8,128)(2,1)S(1)} %copy-done.14), channel_id=1, source_target_pairs={{0,16},{16,0},{32,48},{48,32},{64,80},{80,64},{96,112},{112,96},{1... | collective-permute-start | bytes 1572872 | tf_op jit(solution)/shard_map/ppermute | solution.py:391
  142.2 11.8 %collective-permute-start.27 = (bf16[2,4,256,128]{3,2,1,0:T(8,128)(2,1)S(1)}, bf16[2,4,256,128]{3,2,1,0:T(8,128)(2,1)S(1)}, u32[]{:S(2)}, u32[]{:S(2)}) collective-permute-start(bf16[2,4,256,128]{3,2,1,0:T(8,128)(2,1)S(1)} %add_convert_fusion.3), channel_id=1, source_target_pairs={{0,12},{1,13},{2,14},{3,15},{4,0},{5,1},{6,2},{7,3},{8,4},{9,5},{1... | collective-permute-start | bytes 1572872 | tf_op jit(solution)/shard_map/ppermute | solution.py:310
  144.3 1.0 copy-start.2
  144.5 10.5 %collective-permute-start.31 = (bf16[2,4,256,128]{3,2,1,0:T(8,128)(2,1)S(1)}, bf16[2,4,256,128]{3,2,1,0:T(8,128)(2,1)S(1)}, u32[]{:S(2)}, u32[]{:S(2)}) collective-permute-start(bf16[2,4,256,128]{3,2,1,0:T(8,128)(2,1)S(1)} %add_convert_fusion.1), channel_id=1, source_target_pairs={{0,4},{1,5},{2,6},{3,7},{4,8},{5,9},{6,10},{7,11},{8,12},{9,13},{1... | collective-permute-start | bytes 1572872 | tf_op jit(solution)/shard_map/ppermute | solution.py:310
  145.6 9.4 %copy-start.1 = (bf16[2,4,256,128]{3,2,1,0:T(8,128)(2,1)S(1)}, bf16[2,4,256,128]{3,2,1,0:T(8,128)(2,1)}, u32[]{:S(2)}) copy-start(bf16[2,4,256,128]{3,2,1,0:T(8,128)(2,1)} %get-tuple-element.32) | copy-start | bytes 1572868
  145.6 13.2 %collective-permute-start.24 = (bf16[4,256,128]{2,1,0:T(8,128)(2,1)S(1)}, bf16[4,256,128]{2,1,0:T(8,128)(2,1)S(1)}, u32[]{:S(2)}, u32[]{:S(2)}) collective-permute-start(bf16[4,256,128]{2,1,0:T(8,128)(2,1)S(1)} %slice_bitcast_fusion.2), channel_id=1, source_target_pairs={{0,3},{1,0},{2,1},{3,2},{4,7},{5,4},{6,5},{7,6},{8,11},{9,8},{10,9... | collective-permute-start | bytes 786440 | tf_op jit(solution)/shard_map/ppermute | solution.py:310
  155.4 10.5 %collective-permute-start.32 = (bf16[4,256,128]{2,1,0:T(8,128)(2,1)S(1)}, bf16[4,256,128]{2,1,0:T(8,128)(2,1)S(1)}, u32[]{:S(2)}, u32[]{:S(2)}) collective-permute-start(bf16[4,256,128]{2,1,0:T(8,128)(2,1)S(1)} %get-tuple-element.52), channel_id=1, source_target_pairs={{0,1},{1,2},{2,3},{3,0},{4,5},{5,6},{6,7},{7,4},{8,9},{9,10},{10,1... | collective-permute-start | bytes 786440 | tf_op jit(solution)/shard_map/ppermute | solution.py:310
  155.4 10.4 %collective-permute-start.33 = (bf16[4,256,128]{2,1,0:T(8,128)(2,1)S(1)}, bf16[4,256,128]{2,1,0:T(8,128)(2,1)S(1)}, u32[]{:S(2)}, u32[]{:S(2)}) collective-permute-start(bf16[4,256,128]{2,1,0:T(8,128)(2,1)S(1)} %get-tuple-element.53), channel_id=1, source_target_pairs={{0,2},{1,3},{2,0},{3,1},{4,6},{5,7},{6,4},{7,5},{8,10},{9,11},{10,... | collective-permute-start | bytes 786440 | tf_op jit(solution)/shard_map/ppermute | solution.py:310
  166.7 11.3 %all-to-all-start.3 = ((bf16[4,256,128]{2,1,0:T(8,128)(2,1)}), bf16[4,256,128]{2,1,0:T(8,128)(2,1)S(1)}, u32[]{:S(2)}, u32[]{:S(2)}) async-start(bf16[4,256,128]{2,1,0:T(8,128)(2,1)} %fusion.2), calls=%async_computation.3 | async-start | bytes 524288 | tf_op jit(solution)/shard_map/all_to_all | solution.py:351

commit v3 on v2

--- a/solution.py
+++ b/solution.py
@@ -14,10 +14,8 @@
 GROUP = 3
 ROWS = GROUP * BLOCK
 KVW = 2 * HEAD
-CHUNK = 8
+CHUNK = 4
 NKEY = CHUNK * BLOCK
-HALF = 4
-HKEY = HALF * BLOCK
 EXTRA = 16
 NEG = -1e30
 SCALE = HEAD ** (-0.5)
@@ -44,7 +42,7 @@
     pieces, refs = refs[:16], refs[16:]
     o_out, dq_out = refs[:2]
     parts, refs = refs[2:18], refs[18:]
-    kv, acc, s_buf, p_buf, bias, mx, ls, o_acc, stage, in_sem, out_sem, tseg, tgrp = refs
+    kv, acc, s_buf, p_buf, mx, ls, o_acc, q_rows, d_rows, q_cols, d_cols, stage, in_sem, out_sem, tseg, tblk = refs
     core = lax.rem(ids[0], 2)
     pos = ids[1]
     cx, cz = lax.div(pos, side), lax.rem(pos, side)
@@ -65,7 +63,6 @@
             loads.append(pltpu.make_async_copy(ref.at[at], dst, in_sem.at[len(loads)]))
     for cp in loads:
         cp.start()
-    diag = lax.div(pos, CHUNK)
     far_groups = nblk // CHUNK
 
     @pl.loop(0, 2 * nseg)
@@ -75,26 +72,31 @@
             for e in range(4):
                 acc[p, 4 * b + e] = jnp.zeros((KVW, BLOCK), jnp.float32)
 
-    for cp in loads:
-        cp.wait()
-
     def norm_step(p, top):
         k = jnp.max(jnp.abs(kv[p, :, :, :HEAD].reshape(nblk * BLOCK // 16, 16, HEAD)), axis=0).astype(jnp.float32)
         k = jnp.max(k, axis=0, keepdims=True)
         return jnp.maximum(top, jnp.sum(k * k, axis=1, keepdims=True))
 
-    key_top = lax.fori_loop(0, 2 * nseg, norm_step, jnp.zeros((1, 1), jnp.float32))
-
-    def keys(p, g, h):
-        return kv[p, pl.ds(g * CHUNK + h * HALF, HALF), :, :HEAD].reshape(HKEY, HEAD)
-
-    def values(p, g, h):
-        return kv[p, pl.ds(g * CHUNK + h * HALF, HALF), :, HEAD:].reshape(HKEY, HEAD)
+    key_top = jnp.zeros((1, 1), jnp.float32)
+    for w in range(2):
+        for cp in loads[nblk * w : nblk * (w + 1)]:
+            cp.wait()
+        key_top = lax.fori_loop(nseg * w, nseg * (w + 1), norm_step, key_top)
+
+    def source(i, far, lo):
+        if far:
+            return kv[tseg[i], pl.ds(tblk[CHUNK * i], CHUNK), :, lo : lo + HEAD].reshape(NKEY, HEAD)
+        at = [jnp.minimum(tblk[CHUNK * i + e], nblk - 1) for e in range(CHUNK)]
+        return jnp.concatenate([kv[tseg[i], b, :, lo : lo + HEAD] for b in at], axis=0)
+
+    def keys(i, far):
+        return source(i, far, 0)
+
+    def values(i, far):
+        return source(i, far, HEAD)
 
     def lanes(op, x):
-        return functools.reduce(op, [x[:, i * HEAD : (i + 1) * HEAD] for i in range(HALF)])
-
-    halves = CHUNK // HALF
+        return functools.reduce(op, [x[:, i * HEAD : (i + 1) * HEAD] for i in range(CHUNK)])
 
     @pl.loop(0, nseg)
     def _(j):
@@ -103,33 +105,44 @@
         rows_of = lambda x: jnp.concatenate([x[:, g * HEAD : (g + 1) * HEAD] for g in range(GROUP)], axis=0)
         query = rows_of(qm)
         cotan = rows_of(dm)
-        query_t = jnp.concatenate([qm[:, g * HEAD : (g + 1) * HEAD].T for g in range(GROUP)], axis=1)
+        q_rows[...] = query
+        q_cols[...] = jnp.concatenate([qm[:, g * HEAD : (g + 1) * HEAD].T for g in range(GROUP)], axis=1)
         me = 2 * j + core
         nfar = depth[me]
         up = parent[me]
         far_a, far_b = place(up), place(parent[up])
 
-        def set_own(i, _):
-            tseg[i] = j
-            tgrp[i] = i
-            return 0
-
-        lax.fori_loop(0, diag + 1, set_own, 0)
-
-        def set_far(i, _):
-            tseg[diag + 1 + i] = jnp.where(i < far_groups, far_a, far_b)
-            tgrp[diag + 1 + i] = lax.rem(i, far_groups)
-            return 0
-
-        lax.fori_loop(0, nfar * far_groups, set_far, 0)
-        total = diag + 1 + nfar * far_groups
-
         mask_row = both[j, BLOCK : BLOCK + EXTRA, :HEAD][:1].astype(jnp.float32)
         lane = lax.broadcasted_iota(jnp.int32, (1, HEAD), 1)
-        for b in range(nblk):
-            bit = jnp.sum(jnp.where(lane == b, mask_row, 0.0), axis=1, keepdims=True)
-            open_ = jnp.broadcast_to(bit, (1, BLOCK)) + jnp.where(pos == b, 1.0, 0.0)
-            bias[b // HALF, :, (b % HALF) * BLOCK : (b % HALF + 1) * BLOCK] = jnp.where(open_ > 0.5, 0.0, NEG)
+        bit = jnp.where((lane < nblk) & (mask_row > 0.5), jnp.left_shift(1, jnp.minimum(lane, nblk)), 0)
+        code = jnp.sum(bit.astype(jnp.float32)).astype(jnp.int32)
+
+        def add_own(b, n):
+            tblk[n] = b
+            return n + lax.rem(jnp.right_shift(code, b), 2)
+
+        seen = lax.fori_loop(0, pos, add_own, jnp.int32(0))
+        own = lax.div(seen, CHUNK) + 1
+        tail = seen - (own - 1) * CHUNK
+
+        def add_tail(n, _):
+            tblk[n] = jnp.where(n == seen, pos, nblk)
+            return 0
+
+        lax.fori_loop(seen, own * CHUNK, add_tail, 0)
+        total = own + nfar * far_groups
+
+        def add_seg(i, _):
+            tseg[i] = jnp.where(i < own, j, jnp.where(i < own + far_groups, far_a, far_b))
+            return 0
+
+        lax.fori_loop(0, total, add_seg, 0)
+
+        def add_far(n, _):
+            tblk[(own + n) * CHUNK] = lax.rem(n, far_groups) * CHUNK
+            return 0
+
+        lax.fori_loop(0, nfar * far_groups, add_far, 0)
 
         ls[...] = jnp.zeros((ROWS, HEAD), jnp.float32)
         o_acc[...] = jnp.zeros((ROWS, HEAD), jnp.float32)
@@ -138,66 +151,63 @@
         q_top = jnp.max(jnp.sum(qf * qf, axis=1, keepdims=True), axis=0, keepdims=True)
         small = jnp.max(q_top * key_top * (SCALE * SCALE)) <= SAFE * SAFE
 
-        def low_half(i, h):
-            row = lax.broadcasted_iota(jnp.int32, (BLOCK, HKEY), 0) + pos * BLOCK
-            col = lax.broadcasted_iota(jnp.int32, (BLOCK, HKEY), 1) + (i * NKEY + h * HKEY)
-            low = jnp.where(col <= row, bias[i * halves + h], NEG)
-            return jnp.concatenate([low] * GROUP, axis=0)
-
-        def scores(i, seg, grp, h, kind):
-            s = nt(query, keys(seg, grp, h))
-            if kind == 1:
-                s = s + bias[i * halves + h]
-            if kind == 2:
-                s = s + low_half(i, h)
+        def scores(i, masked, far):
+            s = nt(q_rows[...], keys(i, far))
+            if masked:
+                row = lax.broadcasted_iota(jnp.int32, (BLOCK, NKEY), 0)
+                col = lax.broadcasted_iota(jnp.int32, (BLOCK, NKEY), 1)
+                low = jnp.where(col <= row + tail * BLOCK, 0.0, NEG)
+                s = s + jnp.concatenate([low] * GROUP, axis=0)
             return s
 
-        def finish(i, seg, grp, h, p):
+        def finish(i, far, p):
             ls[...] += lanes(jnp.add, p)
             p_low = p.astype(jnp.bfloat16)
-            p_buf[i, :, h * HKEY : (h + 1) * HKEY] = p_low
-            o_acc[...] += nn(p_low, values(seg, grp, h))
+            p_buf[i] = p_low
+            o_acc[...] += nn(p_low, values(i, far))
+
+        def both_kinds(body):
+            @pl.loop(0, own)
+            def _(i):
+                body(i, False)
+
+            @pl.loop(own, total)
+            def _(i):
+                body(i, True)
 
         def sweep(body):
-            @pl.loop(0, diag)
+            body(own - 1, True, False)
+
+            @pl.loop(0, own - 1)
             def _(i):
-                body(i, j, i, 1)
-
-            body(diag, j, diag, 2)
-
-            @pl.loop(diag + 1, total)
+                body(i, False, False)
+
+            @pl.loop(own, total)
             def _(i):
-                body(i, tseg[i], tgrp[i], 0)
+                body(i, False, True)
 
         @pl.when(small)
         def _():
-            def body(i, seg, grp, kind):
-                for h in range(halves):
-                    s = scores(i, seg, grp, h, kind)
-                    finish(i, seg, grp, h, jnp.exp2(s * (SCALE * LOG2E)))
-
-            sweep(body)
+            sweep(lambda i, masked, far: finish(i, far, jnp.exp2(scores(i, masked, far) * (SCALE * LOG2E))))
 
         @pl.when(jnp.logical_not(small))
         def _():
             mx[...] = jnp.full((ROWS, HEAD), NEG, jnp.float32)
 
-            def body(i, seg, grp, kind):
-                for h in range(halves):
-                    s = scores(i, seg, grp, h, kind)
-                    s_buf[i, :, h * HKEY : (h + 1) * HKEY] = s
-                    mx[...] = jnp.maximum(mx[...], lanes(jnp.maximum, s))
+            def body(i, masked, far):
+                s = scores(i, masked, far)
+                s_buf[i] = s
+                mx[...] = jnp.maximum(mx[...], lanes(jnp.maximum, s))
 
             sweep(body)
             top = jnp.max(mx[...], axis=1, keepdims=True)
             mx[...] = jnp.broadcast_to(top, (ROWS, HEAD))
 
-            @pl.loop(0, total)
-            def _(i):
-                m_all = jnp.concatenate([mx[...]] * HALF, axis=1)
-                for h in range(halves):
-                    s = s_buf[i, :, h * HKEY : (h + 1) * HKEY]
-                    finish(i, tseg[i], tgrp[i], h, jnp.exp2((s - m_all) * (SCALE * LOG2E)))
+            def weigh(i, far):
+                m_all = jnp.concatenate([mx[...]] * CHUNK, axis=1)
+                finish(i, far, jnp.exp2((s_buf[i] - m_all) * (SCALE * LOG2E)))
+
+            both_kinds(weigh)
 
         inv = 1.0 / jnp.sum(ls[...], axis=1, keepdims=True)
         out = (o_acc[...] * inv).astype(jnp.bfloat16)
@@ -207,24 +217,25 @@
         delta = jnp.sum(cot_low.astype(jnp.float32) * out.astype(jnp.float32), axis=1, keepdims=True)
         mx[...] = jnp.broadcast_to(delta, (ROWS, HEAD))
         o_acc[...] = jnp.zeros((ROWS, HEAD), jnp.float32)
-        cot_t = jnp.concatenate([cot_low[g * BLOCK : (g + 1) * BLOCK].T for g in range(GROUP)], axis=1)
-
-        @pl.loop(0, total)
-        def _(i):
-            seg, grp = tseg[i], tgrp[i]
-            for h in range(halves):
-                key = keys(seg, grp, h)
-                gw = nt(cot_low, values(seg, grp, h))
-                d_all = jnp.concatenate([mx[...]] * HALF, axis=1)
-                p_low = p_buf[i, :, h * HKEY : (h + 1) * HKEY]
-                ds = (gw - d_all).astype(jnp.bfloat16) * p_low
-                o_acc[...] += nn(ds, key)
-                dk = nn(query_t, ds)
-                dv = nn(cot_t, p_low)
-                for b in range(HALF):
-                    at = grp * CHUNK + h * HALF + b
-                    acc[seg, at, :HEAD] += dk[:, b * BLOCK : (b + 1) * BLOCK]
-                    acc[seg, at, HEAD:] += dv[:, b * BLOCK : (b + 1) * BLOCK]
+        d_rows[...] = cot_low
+        d_cols[...] = jnp.concatenate([cot_low[g * BLOCK : (g + 1) * BLOCK].T for g in range(GROUP)], axis=1)
+
+        def grads(i, far):
+            key = keys(i, far)
+            gw = nt(d_rows[...], values(i, far))
+            d_all = jnp.concatenate([mx[...]] * CHUNK, axis=1)
+            p_low = p_buf[i]
+            ds = (gw - d_all).astype(jnp.bfloat16) * p_low
+            o_acc[...] += nn(ds, key)
+            dk = nn(q_cols[...], ds)
+            dv = nn(d_cols[...], p_low)
+            seg = tseg[i]
+            for e in range(CHUNK):
+                at = tblk[CHUNK * i] + e if far else tblk[CHUNK * i + e]
+                acc[seg, at, :HEAD] += dk[:, e * BLOCK : (e + 1) * BLOCK]
+                acc[seg, at, HEAD:] += dv[:, e * BLOCK : (e + 1) * BLOCK]
+
+        both_kinds(grads)
 
         dq = (o_acc[...] * SCALE).astype(jnp.bfloat16)
         for g in range(GROUP):
@@ -266,18 +277,21 @@
         out_specs=[vm, vm] + [hbm] * 16,
         scratch_shapes=[
             pltpu.VMEM((2 * nseg, nblk, BLOCK, KVW), bf),
-            pltpu.VMEM((2 * nseg, nblk, KVW, BLOCK), f32),
+            pltpu.VMEM((2 * nseg, nblk + 1, KVW, BLOCK), f32),
             pltpu.VMEM((groups, ROWS, NKEY), f32),
             pltpu.VMEM((groups, ROWS, NKEY), bf),
-            pltpu.VMEM((nblk // HALF, 1, HKEY), f32),
             pltpu.VMEM((ROWS, HEAD), f32),
             pltpu.VMEM((ROWS, HEAD), f32),
             pltpu.VMEM((ROWS, HEAD), f32),
+            pltpu.VMEM((ROWS, HEAD), bf),
+            pltpu.VMEM((ROWS, HEAD), bf),
+            pltpu.VMEM((HEAD, ROWS), bf),
+            pltpu.VMEM((HEAD, ROWS), bf),
             pltpu.VMEM((2, nblk, nseg, KVW, BLOCK), bf),
             pltpu.SemaphoreType.DMA((32,)),
             pltpu.SemaphoreType.DMA((32,)),
             pltpu.SMEM((groups,), jnp.int32),
-            pltpu.SMEM((groups,), jnp.int32),
+            pltpu.SMEM((groups * CHUNK,), jnp.int32),
         ],
         compiler_params=pltpu.CompilerParams(vmem_limit_bytes=62 * 1024 * 1024),
         cost_estimate=pl.CostEstimate(
@@ -331,7 +345,8 @@
     last_a, last_b = add(*low_a, got_a), add(*high_b, got_b)
     end_a = hop(last_a, down)
     end_b = hop(last_b, up)
-    return add(*same_lo, from_a, end_a), add(*same_hi, from_b, end_b)
+    lo, hi = same_lo + (from_a, end_a), same_hi + (from_b, end_b)
+    return [add(*[x[e] for x in part]) for part in (lo, hi) for e in range(2)]
 
 
 def per_device(query_matrix, key_matrix, value_matrix, output_gradient, parent, seg_depth, block_mask):
@@ -389,11 +404,11 @@
 
     own, oth = parts[:8], parts[8:]
     came = [lax.ppermute(x, "cand", partner) for x in oth]
-    line_lo, line_hi = scatter_ring(own, came, *rings[1])
-    end_low = hop(line_lo[1], rings[0][1])
-    end_high = hop(line_hi[1], rings[0][0])
-    end_far = hop(line_hi[0], across)
-    summed = add(line_lo[0], end_low, end_high, end_far)
+    to_self, to_low, to_far, to_high = scatter_ring(own, came, *rings[1])
+    end_low = hop(to_low, rings[0][1])
+    end_high = hop(to_high, rings[0][0])
+    end_far = hop(to_far, across)
+    summed = add(to_self, end_low, end_high, end_far)
     kv_grad = spread(summed)
     k_grad = kv_grad[:, :HEAD].transpose(2, 0, 1).reshape(1, tok, heads * HEAD)
     v_grad = kv_grad[:, HEAD:].transpose(2, 0, 1).reshape(1, tok, heads * HEAD)

time: 180 us -> 181 us (level)
  waiting for transfers between devices: 57.1 us -> 47.9 us
  other arithmetic: 8.6 us -> 14 us
  starting transfers between devices: 55.8 us -> 59.4 us
    ppermute x18, waiting for transfers between devices: 40.9 us -> 29.3 us  [hop(): return lax.ppermute(x, BOTH_AXES, perm)]
    convert_element_type x9 -> x7, other arithmetic: 2.37 us -> 5.74 us  [add(): functools.reduce(jnp.add, [x.astype(jnp.float32) for x in xs])]
    add x0 -> x2, other arithmetic: none -> 3.02 us  [add(): functools.reduce(jnp.add, [x.astype(jnp.float32) for x in xs])]
    ppermute x18, starting transfers between devices: 36.2 us -> 39.2 us  [hop(): return lax.ppermute(x, BOTH_AXES, perm)]
    ppermute x8, waiting for transfers between devices: 0.02 us -> 2.53 us  [per_device(): came = [lax.ppermute(x, 'cand', partner) for x in oth]]
    ppermute x8, starting transfers between devices: 6.3 us -> 8.34 us  [per_device(): came = [lax.ppermute(x, 'cand', partner) for x in oth]]
    unnamed x42 -> x40, local copies, waits for them, and re-layouts: 3.66 us -> 3.1 us
  transfers between devices with their start and end apart: 37 -> 37, of which waited for: 13 -> 15; matrix products, arithmetic and copies ran while one was open for 4% -> 7% of each run, Pallas kernels for 0% -> 0%
where the time goes in v3:
time: 181 us; the launch traced here: 180 us
  starting transfers between devices  59.4 us (33%)
  waiting for transfers between devices  47.9 us (26%)
  Pallas kernels  41.6 us (23%)
  other arithmetic  14 us (8%)
  blocking collectives  11.1 us (6%)
  local copies, waits for them, and re-layouts  4.93 us (3%)
    pallas_call x1, Pallas kernels, attend(): pl.pallas_call(functools.partial(attend_kernel, nseg, nblk, side), out_sh...  41.6 us
    ppermute x18, starting transfers between devices, hop(): return lax.ppermute(x, BOTH_AXES, perm)  39.2 us
    ppermute x18, waiting for transfers between devices, hop(): return lax.ppermute(x, BOTH_AXES, perm)  29.3 us
    all_to_all x3, waiting for transfers between devices, spread(): return lax.all_to_all(x, 'cand', 0, 0, axis_index_groups=same_core)  16 us
    all_to_all x1, blocking collectives, spread(): return lax.all_to_all(x, 'cand', 0, 0, axis_index_groups=same_core)  11.1 us
    all_to_all x3, starting transfers between devices, spread(): return lax.all_to_all(x, 'cand', 0, 0, axis_index_groups=same_core)  10.4 us
    ppermute x8, starting transfers between devices, per_device(): came = [lax.ppermute(x, 'cand', partner) for x in oth]  8.34 us
    convert_element_type x7, other arithmetic, add(): functools.reduce(jnp.add, [x.astype(jnp.float32) for x in xs])  5.74 us
  transfers between devices with their start and end apart: 37, of which 15 were waited for; matrix products, arithmetic and copies ran while one was open for 7% of the time, Pallas kernels for 0%

profile of v3, /device:TPU:0, one launch (start us, length us, event | category | flops | bytes accessed | tf_op | source)
XLA Modules:
  0.0 179.9 jit_solution(15673839173965998488)
XLA Ops:
  0.6 0.8 fusion.19
  1.5 0.8 fusion.20
  2.4 11.1 %all_to_all.20 = bf16[4,128,256]{2,1,0:T(8,128)(2,1)S(1)} all-to-all(bf16[4,128,256]{2,1,0:T(8,128)(2,1)S(1)} %pad_maximum_fusion.4), channel_id=1, replica_groups={{0,32,64,96},{16,48,80,112},{1,33,65,97},{17,49,81,113},{2,34,66,98},{1..., dimensions={0} | all-to-all | bytes 524288 | tf_op jit(solution)/shard_map/all_to_all | solution.py:366
  13.4 1.9 %collective-permute-start = (bf16[4,128,256]{2,1,0:T(8,128)(2,1)S(1)}, bf16[4,128,256]{2,1,0:T(8,128)(2,1)S(1)}, u32[]{:S(2)}, u32[]{:S(2)}) collective-permute-start(bf16[4,128,256]{2,1,0:T(8,128)(2,1)S(1)} %all_to_all.20), channel_id=1, source_target_pairs={{0,1},{1,2},{2,3},{3,0},{4,5},{5,6},{6,7},{7,4},{8,9},{9,10},{10,1... | collective-permute-start | bytes 786440 | tf_op jit(solution)/shard_map/ppermute | solution.py:324
  15.4 2.1 %collective-permute-start.2 = (bf16[4,128,256]{2,1,0:T(8,128)(2,1)S(1)}, bf16[4,128,256]{2,1,0:T(8,128)(2,1)S(1)}, u32[]{:S(2)}, u32[]{:S(2)}) collective-permute-start(bf16[4,128,256]{2,1,0:T(8,128)(2,1)S(1)} %all_to_all.20), channel_id=1, source_target_pairs={{0,3},{1,0},{2,1},{3,2},{4,7},{5,4},{6,5},{7,6},{8,11},{9,8},{10,9... | collective-permute-start | bytes 786440 | tf_op jit(solution)/shard_map/ppermute | solution.py:324
  17.5 1.9 %collective-permute-start.1 = (bf16[4,128,256]{2,1,0:T(8,128)(2,1)S(1)}, bf16[4,128,256]{2,1,0:T(8,128)(2,1)S(1)}, u32[]{:S(2)}, u32[]{:S(2)}) collective-permute-start(bf16[4,128,256]{2,1,0:T(8,128)(2,1)S(1)} %all_to_all.20), channel_id=1, source_target_pairs={{0,2},{1,3},{2,0},{3,1},{4,6},{5,7},{6,4},{7,5},{8,10},{9,11},{10,... | collective-permute-start | bytes 786440 | tf_op jit(solution)/shard_map/ppermute | solution.py:324
  19.3 2.5 %collective-permute-done = bf16[4,128,256]{2,1,0:T(8,128)(2,1)S(1)} collective-permute-done((bf16[4,128,256]{2,1,0:T(8,128)(2,1)S(1)}, bf16[4,128,256]{2,1,0:T(8,128)(2,1)S(1)}, u32[]{:S(2)}, u32[]{:S(2)}) %collective-permute-start) | collective-permute-done | bytes 262176 | tf_op jit(solution)/shard_map/ppermute | solution.py:324
  22.0 2.8 %collective-permute-start.5 = (bf16[2,4,128,256]{3,2,1,0:T(8,128)(2,1)S(1)}, bf16[2,4,128,256]{3,2,1,0:T(8,128)(2,1)S(1)}, u32[]{:S(2)}, u32[]{:S(2)}) collective-permute-start(bf16[2,4,128,256]{3,2,1,0:T(8,128)(2,1)S(1)} %pad_maximum_fusion.2.refs_0_), channel_id=1, source_target_pairs={{0,12},{1,13},{2,14},{3,15},{4,0},{5,1},{6,2},{7,3},{8,4},{9,5},{1... | collective-permute-start | bytes 1572872 | tf_op jit(solution)/shard_map/ppermute | solution.py:324
  24.8 1.3 collective-permute-done.1
  26.2 2.8 %collective-permute-start.6 = (bf16[2,4,128,256]{3,2,1,0:T(8,128)(2,1)S(1)}, bf16[2,4,128,256]{3,2,1,0:T(8,128)(2,1)}, u32[]{:S(2)}, u32[]{:S(2)}) collective-permute-start(bf16[2,4,128,256]{3,2,1,0:T(8,128)(2,1)S(1)} %pad_maximum_fusion.3.refs_1_), channel_id=1, source_target_pairs={{0,12},{1,13},{2,14},{3,15},{4,0},{5,1},{6,2},{7,3},{8,4},{9,5},{1... | collective-permute-start | bytes 1572872 | tf_op jit(solution)/shard_map/ppermute | solution.py:324
  29.1 2.4 %collective-permute-done.5.refs_4_ = bf16[2,4,128,256]{3,2,1,0:T(8,128)(2,1)S(1)} collective-permute-done((bf16[2,4,128,256]{3,2,1,0:T(8,128)(2,1)S(1)}, bf16[2,4,128,256]{3,2,1,0:T(8,128)(2,1)S(1)}, u32[]{:S(2)}, u32[]{:S(2)}) %collective-permute-start.5) | collective-permute-done | bytes 524320 | tf_op jit(solution)/shard_map/ppermute | solution.py:324
  31.5 0.3 collective-permute-start.13
  31.8 3.5 %collective-permute-done.3.refs_2_ = bf16[2,4,128,256]{3,2,1,0:T(8,128)(2,1)} collective-permute-done((bf16[2,4,128,256]{3,2,1,0:T(8,128)(2,1)S(1)}, bf16[2,4,128,256]{3,2,1,0:T(8,128)(2,1)}, u32[]{:S(2)}, u32[]{:S(2)}) %collective-permute-start.3) | collective-permute-done | bytes 524320 | tf_op jit(solution)/shard_map/ppermute | solution.py:324
  35.3 1.8 %collective-permute-done.6.refs_5_ = bf16[2,4,128,256]{3,2,1,0:T(8,128)(2,1)} collective-permute-done((bf16[2,4,128,256]{3,2,1,0:T(8,128)(2,1)S(1)}, bf16[2,4,128,256]{3,2,1,0:T(8,128)(2,1)}, u32[]{:S(2)}, u32[]{:S(2)}) %collective-permute-start.6) | collective-permute-done | bytes 524320 | tf_op jit(solution)/shard_map/ppermute | solution.py:324
  37.1 3.8 %collective-permute-start.8 = (bf16[2,4,128,256]{3,2,1,0:T(8,128)(2,1)}, bf16[2,4,128,256]{3,2,1,0:T(8,128)(2,1)}, u32[]{:S(2)}, u32[]{:S(2)}) collective-permute-start(bf16[2,4,128,256]{3,2,1,0:T(8,128)(2,1)} %collective-permute-done.6.refs_5_), channel_id=1, source_target_pairs={{0,12},{1,13},{2,14},{3,15},{4,0},{5,1},{6,2},{7,3},{8,4},{9,5},{1... | collective-permute-start | bytes 1572872 | tf_op jit(solution)/shard_map/ppermute | solution.py:324
  41.0 0.7 convert_bitcast_fusion
  41.8 1.1 pad_maximum_fusion
  42.9 3.5 %all-to-all-start = ((bf16[4,144,768]{2,1,0:T(8,128)(2,1)}), bf16[4,144,768]{2,1,0:T(8,128)(2,1)S(1)}, u32[]{:S(2)}, u32[]{:S(2)}) async-start(bf16[4,144,768]{2,1,0:T(8,128)(2,1)} %pad_maximum_fusion), calls=%async_computation | async-start | bytes 1769472 | tf_op jit(solution)/shard_map/all_to_all | solution.py:366
  46.5 0.5 collective-permute-start.14
  47.0 0.1 collective-permute-start.12
  47.1 0.4 collective-permute-start.15
  47.6 0.4 collective-permute-done.8.refs_7_
  47.9 0.7 pad_add_fusion.ids
  48.6 10.1 %all-to-all-done.both = bf16[4,144,768]{2,1,0:T(8,128)(2,1)S(1)} async-done(((bf16[4,144,768]{2,1,0:T(8,128)(2,1)}), bf16[4,144,768]{2,1,0:T(8,128)(2,1)S(1)}, u32[]{:S(2)}, u32[]{:S(2)}) %all-to-all-start) | async-done | bytes 884768 | tf_op jit(solution)/shard_map/all_to_all | solution.py:366
  58.8 0.9 copy-done
  59.7 0.2 copy-done.17
  59.9 0.3 copy-done.18
  60.2 41.6 %shard_map.102 = (bf16[4,128,384]{2,1,0:T(8,128)(2,1)}, bf16[4,128,384]{2,1,0:T(8,128)(2,1)}, bf16[2,4,256,128]{3,2,1,0:T(8,128)(2,1)}, bf16[2,4,256,128]{3,2,1,...) custom-call(s32[2]{0:T(128)} %pad_add_fusion.ids, ...), custom_call_target="tpu_custom_call" | custom-call | flops 14495514624 | bytes 16777216 | tf_op jit(solution)/shard_map/pallas_call | solution.py:273
  101.8 6.6 %collective-permute-start.18 = (bf16[2,4,256,128]{3,2,1,0:T(8,128)(2,1)}, bf16[2,4,256,128]{3,2,1,0:T(8,128)(2,1)S(1)}, u32[]{:S(2)}, u32[]{:S(2)}) collective-permute-start(bf16[2,4,256,128]{3,2,1,0:T(8,128)(2,1)} %get-tuple-element.27), channel_id=1, source_target_pairs={{0,16},{16,0},{32,48},{48,32},{64,80},{80,64},{96,112},{112,96},{1... | collective-permute-start | bytes 1572872 | tf_op jit(solution)/shard_map/ppermute | solution.py:406
  108.5 0.4 collective-permute-start.17
  108.9 0.1 collective-permute-start.20
  109.0 0.4 collective-permute-start.26
  109.4 0.7 collective-permute-done.18
  110.2 0.4 collective-permute-start.29
  110.5 1.2 add_convert_fusion.5
  111.7 0.2 collective-permute-start.28
  112.0 0.1 add_convert_fusion.4
  112.1 1.8 collective-permute-done.29
  113.9 14.3 %collective-permute-start.22 = (bf16[2,4,256,128]{3,2,1,0:T(8,128)(2,1)S(1)}, bf16[2,4,256,128]{3,2,1,0:T(8,128)(2,1)S(1)}, u32[]{:S(2)}, u32[]{:S(2)}) collective-permute-start(bf16[2,4,256,128]{3,2,1,0:T(8,128)(2,1)S(1)} %add_convert_fusion.4), channel_id=1, source_target_pairs={{0,12},{1,13},{2,14},{3,15},{4,0},{5,1},{6,2},{7,3},{8,4},{9,5},{1... | collective-permute-start | bytes 1572872 | tf_op jit(solution)/shard_map/ppermute | solution.py:324
  128.2 0.1 add_convert_fusion.1
  128.4 0.1 add_convert_fusion.2
  128.7 6.2 %collective-permute-done.22 = bf16[2,4,256,128]{3,2,1,0:T(8,128)(2,1)S(1)} collective-permute-done((bf16[2,4,256,128]{3,2,1,0:T(8,128)(2,1)S(1)}, bf16[2,4,256,128]{3,2,1,0:T(8,128)(2,1)S(1)}, u32[]{:S(2)}, u32[]{:S(2)}) %collective-permute-start.22) | collective-permute-done | bytes 524320 | tf_op jit(solution)/shard_map/ppermute | solution.py:324
  134.9 1.0 add_convert_fusion.3
  135.9 3.7 %collective-permute-start.27 = (bf16[2,4,256,128]{3,2,1,0:T(8,128)(2,1)S(1)}, bf16[2,4,256,128]{3,2,1,0:T(8,128)(2,1)S(1)}, u32[]{:S(2)}, u32[]{:S(2)}) collective-permute-start(bf16[2,4,256,128]{3,2,1,0:T(8,128)(2,1)S(1)} %add_convert_fusion.2), channel_id=1, source_target_pairs={{0,12},{1,13},{2,14},{3,15},{4,0},{5,1},{6,2},{7,3},{8,4},{9,5},{1... | collective-permute-start | bytes 1572872 | tf_op jit(solution)/shard_map/ppermute | solution.py:324
  139.6 2.0 %collective-permute-start.23 = (bf16[2,4,256,128]{3,2,1,0:T(8,128)(2,1)}, bf16[2,4,256,128]{3,2,1,0:T(8,128)(2,1)}, u32[]{:S(2)}, u32[]{:S(2)}) collective-permute-start(bf16[2,4,256,128]{3,2,1,0:T(8,128)(2,1)} %add_convert_fusion.3), channel_id=1, source_target_pairs={{0,12},{1,13},{2,14},{3,15},{4,0},{5,1},{6,2},{7,3},{8,4},{9,5},{1... | collective-permute-start | bytes 1572872 | tf_op jit(solution)/shard_map/ppermute | solution.py:324
  141.6 1.0 add_convert_fusion
  142.6 0.1 copy-done.13
  142.7 1.0 pad_maximum_fusion.1
  143.7 3.5 %all-to-all-start.2 = ((bf16[4,128,768]{2,1,0:T(8,128)(2,1)}), bf16[4,128,768]{2,1,0:T(8,128)(2,1)S(1)}, u32[]{:S(2)}, u32[]{:S(2)}) async-start(bf16[4,128,768]{2,1,0:T(8,128)(2,1)} %pad_maximum_fusion.1), calls=%async_computation.2 | async-start | bytes 1572864 | tf_op jit(solution)/shard_map/all_to_all | solution.py:366
  147.3 4.8 %collective-permute-done.23 = bf16[2,4,256,128]{3,2,1,0:T(8,128)(2,1)} collective-permute-done((bf16[2,4,256,128]{3,2,1,0:T(8,128)(2,1)}, bf16[2,4,256,128]{3,2,1,0:T(8,128)(2,1)}, u32[]{:S(2)}, u32[]{:S(2)}) %collective-permute-start.23) | collective-permute-done | bytes 524320 | tf_op jit(solution)/shard_map/ppermute | solution.py:324
  152.0 2.0 %fusion.5 = bf16[4,256,128]{2,1,0:T(8,128)(2,1)} fusion(bf16[2,4,256,128]{3,2,1,0:T(8,128)(2,1)} %collective-permute-done.23, bf16[2,4,256,128]{3,2,1,0:T(8,128)(2,1)} %collective-permute-done.19, bf16[2,4,256,128]{3,2,1,0:T(8,128)(2,1)} %collective-permute-done.17, bf16[2,4,256,128]{3,2,1,0:T(8,128)(2,1)} %get-tuple-element.24), kind=kLoop, calls=%fused_computation.23 | loop fusion | flops 1048576 | bytes 1310720 | tf_op jit(solution)/shard_map/add | solution.py:320
  154.1 1.0 fusion.6
  155.1 2.0 %collective-permute-start.32 = (bf16[4,256,128]{2,1,0:T(8,128)(2,1)}, bf16[4,256,128]{2,1,0:T(8,128)(2,1)S(1)}, u32[]{:S(2)}, u32[]{:S(2)}) collective-permute-start(bf16[4,256,128]{2,1,0:T(8,128)(2,1)} %get-tuple-element.44), channel_id=1, source_target_pairs={{0,1},{1,2},{2,3},{3,0},{4,5},{5,6},{6,7},{7,4},{8,9},{9,10},{10,1... | collective-permute-start | bytes 786440 | tf_op jit(solution)/shard_map/ppermute | solution.py:324
  157.1 1.7 collective-permute-start.33
  158.9 0.8 maximum_bitcast_fusion.1
  159.6 1.1 collective-permute-done.24
  160.7 2.1 %collective-permute-done.32 = bf16[4,256,128]{2,1,0:T(8,128)(2,1)S(1)} collective-permute-done((bf16[4,256,128]{2,1,0:T(8,128)(2,1)}, bf16[4,256,128]{2,1,0:T(8,128)(2,1)S(1)}, u32[]{:S(2)}, u32[]{:S(2)}) %collective-permute-start.32) | collective-permute-done | bytes 262176 | tf_op jit(solution)/shard_map/ppermute | solution.py:324
  162.9 3.3 %collective-permute-done.33 = bf16[4,256,128]{2,1,0:T(8,128)(2,1)S(1)} collective-permute-done((bf16[4,256,128]{2,1,0:T(8,128)(2,1)S(1)}, bf16[4,256,128]{2,1,0:T(8,128)(2,1)S(1)}, u32[]{:S(2)}, u32[]{:S(2)}) %collective-permute-start.33) | collective-permute-done | bytes 262176 | tf_op jit(solution)/shard_map/ppermute | solution.py:324
  166.1 2.1 %fusion.2 = bf16[4,256,128]{2,1,0:T(8,128)(2,1)} fusion(bf16[4,256,128]{2,1,0:T(8,128)(2,1)S(1)} %collective-permute-done.33, bf16[4,256,128]{2,1,0:T(8,128)(2,1)S(1)} %collective-permute-done.32, bf16[4,256,128]{2,1,0:T(8,128)(2,1)} %collective-permute-done.24, bf16[2,4,256,128]{3,2,1,0:T(8,128)(2,1)} %collective-permute-done.23, ...), kind=kLoop, calls=%fused_computation.13 | loop fusion | flops 2097152 | bytes 2097152 | tf_op jit(solution)/shard_map/convert_element_type | solution.py:320
  168.3 3.4 %all-to-all-start.3 = ((bf16[4,256,128]{2,1,0:T(8,128)(2,1)}), bf16[4,256,128]{2,1,0:T(8,128)(2,1)S(1)}, u32[]{:S(2)}, u32[]{:S(2)}) async-start(bf16[4,256,128]{2,1,0:T(8,128)(2,1)} %fusion.2), calls=%async_computation.3 | async-start | bytes 524288 | tf_op jit(solution)/shard_map/all_to_all | solution.py:366
  171.7 0.8 maximum_bitcast_fusion
  172.5 5.9 %all-to-all-done.3 = bf16[4,256,128]{2,1,0:T(8,128)(2,1)S(1)} async-done(((bf16[4,256,128]{2,1,0:T(8,128)(2,1)}), bf16[4,256,128]{2,1,0:T(8,128)(2,1)S(1)}, u32[]{:S(2)}, u32[]{:S(2)}) %all-to-all-start.3) | async-done | bytes 262176 | tf_op jit(solution)/shard_map/all_to_all | solution.py:366
  178.3 0.8 copy.12
  179.1 0.8 copy.11
  (78 shorter events, 1.1 us)
Async XLA Ops:
  13.4 8.4 %collective-permute-start = (bf16[4,128,256]{2,1,0:T(8,128)(2,1)S(1)}, bf16[4,128,256]{2,1,0:T(8,128)(2,1)S(1)}, u32[]{:S(2)}, u32[]{:S(2)}) collective-permute-start(bf16[4,128,256]{2,1,0:T(8,128)(2,1)S(1)} %all_to_all.20), channel_id=1, source_target_pairs={{0,1},{1,2},{2,3},{3,0},{4,5},{5,6},{6,7},{7,4},{8,9},{9,10},{10,1... | collective-permute-start | bytes 786440 | tf_op jit(solution)/shard_map/ppermute | solution.py:324
  15.4 9.5 %collective-permute-start.2 = (bf16[4,128,256]{2,1,0:T(8,128)(2,1)S(1)}, bf16[4,128,256]{2,1,0:T(8,128)(2,1)S(1)}, u32[]{:S(2)}, u32[]{:S(2)}) collective-permute-start(bf16[4,128,256]{2,1,0:T(8,128)(2,1)S(1)} %all_to_all.20), channel_id=1, source_target_pairs={{0,3},{1,0},{2,1},{3,2},{4,7},{5,4},{6,5},{7,6},{8,11},{9,8},{10,9... | collective-permute-start | bytes 786440 | tf_op jit(solution)/shard_map/ppermute | solution.py:324
  17.5 8.6 %collective-permute-start.1 = (bf16[4,128,256]{2,1,0:T(8,128)(2,1)S(1)}, bf16[4,128,256]{2,1,0:T(8,128)(2,1)S(1)}, u32[]{:S(2)}, u32[]{:S(2)}) collective-permute-start(bf16[4,128,256]{2,1,0:T(8,128)(2,1)S(1)} %all_to_all.20), channel_id=1, source_target_pairs={{0,2},{1,3},{2,0},{3,1},{4,6},{5,7},{6,4},{7,5},{8,10},{9,11},{10,... | collective-permute-start | bytes 786440 | tf_op jit(solution)/shard_map/ppermute | solution.py:324
  21.8 19.1 %copy-start.10 = (bf16[1,128,1536]{2,1,0:T(8,128)(2,1)S(1)}, bf16[1,128,1536]{2,1,0:T(8,128)(2,1)}, u32[]{:S(2)}) copy-start(bf16[1,128,1536]{2,1,0:T(8,128)(2,1)} %param.7) | copy-start | bytes 1179652
  21.8 19.1 %copy-start.11 = (bf16[1,128,1536]{2,1,0:T(8,128)(2,1)S(1)}, bf16[1,128,1536]{2,1,0:T(8,128)(2,1)}, u32[]{:S(2)}) copy-start(bf16[1,128,1536]{2,1,0:T(8,128)(2,1)} %param.10) | copy-start | bytes 1179652
  21.9 19.1 %copy-start.5 = (bf16[2,4,128,256]{3,2,1,0:T(8,128)(2,1)}, bf16[2,4,128,256]{3,2,1,0:T(8,128)(2,1)S(1)}, u32[]{:S(2)}) copy-start(bf16[2,4,128,256]{3,2,1,0:T(8,128)(2,1)S(1)} %pad_maximum_fusion.2.refs_0_) | copy-start | bytes 1572868
  21.9 7.1 %collective-permute-start.9 = (bf16[2,4,128,256]{3,2,1,0:T(8,128)(2,1)S(1)}, bf16[2,4,128,256]{3,2,1,0:T(8,128)(2,1)S(1)}, u32[]{:S(2)}, u32[]{:S(2)}) collective-permute-start(bf16[2,4,128,256]{3,2,1,0:T(8,128)(2,1)S(1)} %pad_maximum_fusion.2.refs_0_), channel_id=1, source_target_pairs={{0,16},{16,0},{32,48},{48,32},{64,80},{80,64},{96,112},{112,96},{1... | collective-permute-start | bytes 1572872 | tf_op jit(solution)/shard_map/ppermute | solution.py:382
  22.0 9.5 %collective-permute-start.5 = (bf16[2,4,128,256]{3,2,1,0:T(8,128)(2,1)S(1)}, bf16[2,4,128,256]{3,2,1,0:T(8,128)(2,1)S(1)}, u32[]{:S(2)}, u32[]{:S(2)}) collective-permute-start(bf16[2,4,128,256]{3,2,1,0:T(8,128)(2,1)S(1)} %pad_maximum_fusion.2.refs_0_), channel_id=1, source_target_pairs={{0,12},{1,13},{2,14},{3,15},{4,0},{5,1},{6,2},{7,3},{8,4},{9,5},{1... | collective-permute-start | bytes 1572872 | tf_op jit(solution)/shard_map/ppermute | solution.py:324
  24.8 10.5 %collective-permute-start.3 = (bf16[2,4,128,256]{3,2,1,0:T(8,128)(2,1)S(1)}, bf16[2,4,128,256]{3,2,1,0:T(8,128)(2,1)}, u32[]{:S(2)}, u32[]{:S(2)}) collective-permute-start(bf16[2,4,128,256]{3,2,1,0:T(8,128)(2,1)S(1)} %pad_maximum_fusion.2.refs_0_), channel_id=1, source_target_pairs={{0,4},{1,5},{2,6},{3,7},{4,8},{5,9},{6,10},{7,11},{8,12},{9,13},{1... | collective-permute-start | bytes 1572872 | tf_op jit(solution)/shard_map/ppermute | solution.py:324
  26.1 15.7 %copy-start.6 = (bf16[2,4,128,256]{3,2,1,0:T(8,128)(2,1)}, bf16[2,4,128,256]{3,2,1,0:T(8,128)(2,1)S(1)}, u32[]{:S(2)}) copy-start(bf16[2,4,128,256]{3,2,1,0:T(8,128)(2,1)S(1)} %pad_maximum_fusion.3.refs_1_) | copy-start | bytes 1572868
  26.2 11.0 %collective-permute-start.6 = (bf16[2,4,128,256]{3,2,1,0:T(8,128)(2,1)S(1)}, bf16[2,4,128,256]{3,2,1,0:T(8,128)(2,1)}, u32[]{:S(2)}, u32[]{:S(2)}) collective-permute-start(bf16[2,4,128,256]{3,2,1,0:T(8,128)(2,1)S(1)} %pad_maximum_fusion.3.refs_1_), channel_id=1, source_target_pairs={{0,12},{1,13},{2,14},{3,15},{4,0},{5,1},{6,2},{7,3},{8,4},{9,5},{1... | collective-permute-start | bytes 1572872 | tf_op jit(solution)/shard_map/ppermute | solution.py:324
  29.0 17.5 %collective-permute-start.10 = (bf16[2,4,128,256]{3,2,1,0:T(8,128)(2,1)S(1)}, bf16[2,4,128,256]{3,2,1,0:T(8,128)(2,1)}, u32[]{:S(2)}, u32[]{:S(2)}) collective-permute-start(bf16[2,4,128,256]{3,2,1,0:T(8,128)(2,1)S(1)} %pad_maximum_fusion.3.refs_1_), channel_id=1, source_target_pairs={{0,16},{16,0},{32,48},{48,32},{64,80},{80,64},{96,112},{112,96},{1... | collective-permute-start | bytes 1572872 | tf_op jit(solution)/shard_map/ppermute | solution.py:382
  29.0 12.8 %copy-start.14 = (bf16[2,4,128,256]{3,2,1,0:T(8,128)(2,1)}, bf16[2,4,128,256]{3,2,1,0:T(8,128)(2,1)S(1)}, u32[]{:S(2)}) copy-start(bf16[2,4,128,256]{3,2,1,0:T(8,128)(2,1)S(1)} %collective-permute-done.9.refs_8_) | copy-start | bytes 1572868
  29.0 17.5 %collective-permute-start.4 = (bf16[2,4,128,256]{3,2,1,0:T(8,128)(2,1)S(1)}, bf16[2,4,128,256]{3,2,1,0:T(8,128)(2,1)}, u32[]{:S(2)}, u32[]{:S(2)}) collective-permute-start(bf16[2,4,128,256]{3,2,1,0:T(8,128)(2,1)S(1)} %pad_maximum_fusion.3.refs_1_), channel_id=1, source_target_pairs={{0,4},{1,5},{2,6},{3,7},{4,8},{5,9},{6,10},{7,11},{8,12},{9,13},{1... | collective-permute-start | bytes 1572872 | tf_op jit(solution)/shard_map/ppermute | solution.py:324
  31.5 10.3 %copy-start.15 = (bf16[2,4,128,256]{3,2,1,0:T(8,128)(2,1)}, bf16[2,4,128,256]{3,2,1,0:T(8,128)(2,1)S(1)}, u32[]{:S(2)}) copy-start(bf16[2,4,128,256]{3,2,1,0:T(8,128)(2,1)S(1)} %collective-permute-done.5.refs_4_) | copy-start | bytes 1572868
  31.5 15.5 %collective-permute-start.13 = (bf16[2,4,128,256]{3,2,1,0:T(8,128)(2,1)S(1)}, bf16[2,4,128,256]{3,2,1,0:T(8,128)(2,1)}, u32[]{:S(2)}, u32[]{:S(2)}) collective-permute-start(bf16[2,4,128,256]{3,2,1,0:T(8,128)(2,1)S(1)} %collective-permute-done.5.refs_4_), channel_id=1, source_target_pairs={{0,16},{16,0},{32,48},{48,32},{64,80},{80,64},{96,112},{112,96},{1... | collective-permute-start | bytes 1572872 | tf_op jit(solution)/shard_map/ppermute | solution.py:382
  35.3 11.8 %collective-permute-start.7 = (bf16[2,4,128,256]{3,2,1,0:T(8,128)(2,1)}, bf16[2,4,128,256]{3,2,1,0:T(8,128)(2,1)}, u32[]{:S(2)}, u32[]{:S(2)}) collective-permute-start(bf16[2,4,128,256]{3,2,1,0:T(8,128)(2,1)} %collective-permute-done.3.refs_2_), channel_id=1, source_target_pairs={{0,4},{1,5},{2,6},{3,7},{4,8},{5,9},{6,10},{7,11},{8,12},{9,13},{1... | collective-permute-start | bytes 1572872 | tf_op jit(solution)/shard_map/ppermute | solution.py:324
  37.1 10.8 %collective-permute-start.8 = (bf16[2,4,128,256]{3,2,1,0:T(8,128)(2,1)}, bf16[2,4,128,256]{3,2,1,0:T(8,128)(2,1)}, u32[]{:S(2)}, u32[]{:S(2)}) collective-permute-start(bf16[2,4,128,256]{3,2,1,0:T(8,128)(2,1)} %collective-permute-done.6.refs_5_), channel_id=1, source_target_pairs={{0,12},{1,13},{2,14},{3,15},{4,0},{5,1},{6,2},{7,3},{8,4},{9,5},{1... | collective-permute-start | bytes 1572872 | tf_op jit(solution)/shard_map/ppermute | solution.py:324
  42.9 15.8 %all-to-all-start = ((bf16[4,144,768]{2,1,0:T(8,128)(2,1)}), bf16[4,144,768]{2,1,0:T(8,128)(2,1)S(1)}, u32[]{:S(2)}, u32[]{:S(2)}) async-start(bf16[4,144,768]{2,1,0:T(8,128)(2,1)} %pad_maximum_fusion), calls=%async_computation | async-start | bytes 1769472 | tf_op jit(solution)/shard_map/all_to_all | solution.py:366
  46.4 12.3 %collective-permute-start.11 = (bf16[2,4,128,256]{3,2,1,0:T(8,128)(2,1)}, bf16[2,4,128,256]{3,2,1,0:T(8,128)(2,1)S(1)}, u32[]{:S(2)}, u32[]{:S(2)}) collective-permute-start(bf16[2,4,128,256]{3,2,1,0:T(8,128)(2,1)} %collective-permute-done.3.refs_2_), channel_id=1, source_target_pairs={{0,16},{16,0},{32,48},{48,32},{64,80},{80,64},{96,112},{112,96},{1... | collective-permute-start | bytes 1572872 | tf_op jit(solution)/shard_map/ppermute | solution.py:382
  46.5 12.2 %collective-permute-start.14 = (bf16[2,4,128,256]{3,2,1,0:T(8,128)(2,1)}, bf16[2,4,128,256]{3,2,1,0:T(8,128)(2,1)}, u32[]{:S(2)}, u32[]{:S(2)}) collective-permute-start(bf16[2,4,128,256]{3,2,1,0:T(8,128)(2,1)} %collective-permute-done.6.refs_5_), channel_id=1, source_target_pairs={{0,16},{16,0},{32,48},{48,32},{64,80},{80,64},{96,112},{112,96},{1... | collective-permute-start | bytes 1572872 | tf_op jit(solution)/shard_map/ppermute | solution.py:382
  47.0 11.7 %collective-permute-start.12 = (bf16[2,4,128,256]{3,2,1,0:T(8,128)(2,1)}, bf16[2,4,128,256]{3,2,1,0:T(8,128)(2,1)S(1)}, u32[]{:S(2)}, u32[]{:S(2)}) collective-permute-start(bf16[2,4,128,256]{3,2,1,0:T(8,128)(2,1)} %collective-permute-done.4.refs_3_), channel_id=1, source_target_pairs={{0,16},{16,0},{32,48},{48,32},{64,80},{80,64},{96,112},{112,96},{1... | collective-permute-start | bytes 1572872 | tf_op jit(solution)/shard_map/ppermute | solution.py:382
  47.1 11.6 %collective-permute-start.15 = (bf16[2,4,128,256]{3,2,1,0:T(8,128)(2,1)}, bf16[2,4,128,256]{3,2,1,0:T(8,128)(2,1)}, u32[]{:S(2)}, u32[]{:S(2)}) collective-permute-start(bf16[2,4,128,256]{3,2,1,0:T(8,128)(2,1)} %collective-permute-done.7.refs_6_), channel_id=1, source_target_pairs={{0,16},{16,0},{32,48},{48,32},{64,80},{80,64},{96,112},{112,96},{1... | collective-permute-start | bytes 1572872 | tf_op jit(solution)/shard_map/ppermute | solution.py:382
  47.9 10.8 %collective-permute-start.16 = (bf16[2,4,128,256]{3,2,1,0:T(8,128)(2,1)}, bf16[2,4,128,256]{3,2,1,0:T(8,128)(2,1)}, u32[]{:S(2)}, u32[]{:S(2)}) collective-permute-start(bf16[2,4,128,256]{3,2,1,0:T(8,128)(2,1)} %collective-permute-done.8.refs_7_), channel_id=1, source_target_pairs={{0,16},{16,0},{32,48},{48,32},{64,80},{80,64},{96,112},{112,96},{1... | collective-permute-start | bytes 1572872 | tf_op jit(solution)/shard_map/ppermute | solution.py:382
  58.7 1.0 copy-start
  58.7 1.2 copy-start.17
  58.8 1.4 copy-start.18
  101.7 10.0 %copy-start.16 = (bf16[2,4,256,128]{3,2,1,0:T(8,128)(2,1)S(1)}, bf16[2,4,256,128]{3,2,1,0:T(8,128)(2,1)}, u32[]{:S(2)}) copy-start(bf16[2,4,256,128]{3,2,1,0:T(8,128)(2,1)} %get-tuple-element.37) | copy-start | bytes 1572868
  101.8 10.2 %copy-start.4 = (bf16[2,4,256,128]{3,2,1,0:T(8,128)(2,1)S(1)}, bf16[2,4,256,128]{3,2,1,0:T(8,128)(2,1)}, u32[]{:S(2)}) copy-start(bf16[2,4,256,128]{3,2,1,0:T(8,128)(2,1)} %get-tuple-element.30) | copy-start | bytes 1572868
  101.8 8.4 %collective-permute-start.18 = (bf16[2,4,256,128]{3,2,1,0:T(8,128)(2,1)}, bf16[2,4,256,128]{3,2,1,0:T(8,128)(2,1)S(1)}, u32[]{:S(2)}, u32[]{:S(2)}) collective-permute-start(bf16[2,4,256,128]{3,2,1,0:T(8,128)(2,1)} %get-tuple-element.27), channel_id=1, source_target_pairs={{0,16},{16,0},{32,48},{48,32},{64,80},{80,64},{96,112},{112,96},{1... | collective-permute-start | bytes 1572872 | tf_op jit(solution)/shard_map/ppermute | solution.py:406
  108.4 3.3 %collective-permute-start.21 = (bf16[2,4,256,128]{3,2,1,0:T(8,128)(2,1)}, bf16[2,4,256,128]{3,2,1,0:T(8,128)(2,1)S(1)}, u32[]{:S(2)}, u32[]{:S(2)}) collective-permute-start(bf16[2,4,256,128]{3,2,1,0:T(8,128)(2,1)} %get-tuple-element.31), channel_id=1, source_target_pairs={{0,16},{16,0},{32,48},{48,32},{64,80},{80,64},{96,112},{112,96},{1... | collective-permute-start | bytes 1572872 | tf_op jit(solution)/shard_map/ppermute | solution.py:406
  108.5 34.1 %collective-permute-start.17 = (bf16[2,4,256,128]{3,2,1,0:T(8,128)(2,1)}, bf16[2,4,256,128]{3,2,1,0:T(8,128)(2,1)}, u32[]{:S(2)}, u32[]{:S(2)}) collective-permute-start(bf16[2,4,256,128]{3,2,1,0:T(8,128)(2,1)} %get-tuple-element.25), channel_id=1, source_target_pairs={{0,16},{16,0},{32,48},{48,32},{64,80},{80,64},{96,112},{112,96},{1... | collective-permute-start | bytes 1572872 | tf_op jit(solution)/shard_map/ppermute | solution.py:406
  108.9 19.7 %collective-permute-start.20 = (bf16[2,4,256,128]{3,2,1,0:T(8,128)(2,1)}, bf16[2,4,256,128]{3,2,1,0:T(8,128)(2,1)S(1)}, u32[]{:S(2)}, u32[]{:S(2)}) collective-permute-start(bf16[2,4,256,128]{3,2,1,0:T(8,128)(2,1)} %get-tuple-element.29), channel_id=1, source_target_pairs={{0,16},{16,0},{32,48},{48,32},{64,80},{80,64},{96,112},{112,96},{1... | collective-permute-start | bytes 1572872 | tf_op jit(solution)/shard_map/ppermute | solution.py:406
  109.0 19.3 %collective-permute-start.26 = (bf16[2,4,256,128]{3,2,1,0:T(8,128)(2,1)}, bf16[2,4,256,128]{3,2,1,0:T(8,128)(2,1)S(1)}, u32[]{:S(2)}, u32[]{:S(2)}) collective-permute-start(bf16[2,4,256,128]{3,2,1,0:T(8,128)(2,1)} %get-tuple-element.35), channel_id=1, source_target_pairs={{0,16},{16,0},{32,48},{48,32},{64,80},{80,64},{96,112},{112,96},{1... | collective-permute-start | bytes 1572872 | tf_op jit(solution)/shard_map/ppermute | solution.py:406
  110.2 3.7 %collective-permute-start.29 = (bf16[2,4,256,128]{3,2,1,0:T(8,128)(2,1)}, bf16[2,4,256,128]{3,2,1,0:T(8,128)(2,1)S(1)}, u32[]{:S(2)}, u32[]{:S(2)}) collective-permute-start(bf16[2,4,256,128]{3,2,1,0:T(8,128)(2,1)} %get-tuple-element.39), channel_id=1, source_target_pairs={{0,16},{16,0},{32,48},{48,32},{64,80},{80,64},{96,112},{112,96},{1... | collective-permute-start | bytes 1572872 | tf_op jit(solution)/shard_map/ppermute | solution.py:406
  111.7 16.4 %copy-start.3 = (bf16[2,4,256,128]{3,2,1,0:T(8,128)(2,1)S(1)}, bf16[2,4,256,128]{3,2,1,0:T(8,128)(2,1)}, u32[]{:S(2)}) copy-start(bf16[2,4,256,128]{3,2,1,0:T(8,128)(2,1)} %get-tuple-element.38) | copy-start | bytes 1572868
  111.7 24.1 %collective-permute-start.28 = (bf16[2,4,256,128]{3,2,1,0:T(8,128)(2,1)S(1)}, bf16[2,4,256,128]{3,2,1,0:T(8,128)(2,1)S(1)}, u32[]{:S(2)}, u32[]{:S(2)}) collective-permute-start(bf16[2,4,256,128]{3,2,1,0:T(8,128)(2,1)S(1)} %copy-done.16), channel_id=1, source_target_pairs={{0,16},{16,0},{32,48},{48,32},{64,80},{80,64},{96,112},{112,96},{1... | collective-permute-start | bytes 1572872 | tf_op jit(solution)/shard_map/ppermute | solution.py:406
  112.1 16.3 %copy-start.2 = (bf16[2,4,256,128]{3,2,1,0:T(8,128)(2,1)S(1)}, bf16[2,4,256,128]{3,2,1,0:T(8,128)(2,1)}, u32[]{:S(2)}) copy-start(bf16[2,4,256,128]{3,2,1,0:T(8,128)(2,1)} %get-tuple-element.34) | copy-start | bytes 1572868
  113.9 21.0 %collective-permute-start.22 = (bf16[2,4,256,128]{3,2,1,0:T(8,128)(2,1)S(1)}, bf16[2,4,256,128]{3,2,1,0:T(8,128)(2,1)S(1)}, u32[]{:S(2)}, u32[]{:S(2)}) collective-permute-start(bf16[2,4,256,128]{3,2,1,0:T(8,128)(2,1)S(1)} %add_convert_fusion.4), channel_id=1, source_target_pairs={{0,12},{1,13},{2,14},{3,15},{4,0},{5,1},{6,2},{7,3},{8,4},{9,5},{1... | collective-permute-start | bytes 1572872 | tf_op jit(solution)/shard_map/ppermute | solution.py:324
  128.3 6.6 %copy-start.9 = (bf16[2,4,256,128]{3,2,1,0:T(8,128)(2,1)S(1)}, bf16[2,4,256,128]{3,2,1,0:T(8,128)(2,1)}, u32[]{:S(2)}) copy-start(bf16[2,4,256,128]{3,2,1,0:T(8,128)(2,1)} %get-tuple-element.28) | copy-start | bytes 1572868
  128.3 11.3 %collective-permute-start.30 = (bf16[2,4,256,128]{3,2,1,0:T(8,128)(2,1)S(1)}, bf16[2,4,256,128]{3,2,1,0:T(8,128)(2,1)S(1)}, u32[]{:S(2)}, u32[]{:S(2)}) collective-permute-start(bf16[2,4,256,128]{3,2,1,0:T(8,128)(2,1)S(1)} %add_convert_fusion.1), channel_id=1, source_target_pairs={{0,4},{1,5},{2,6},{3,7},{4,8},{5,9},{6,10},{7,11},{8,12},{9,13},{1... | collective-permute-start | bytes 1572872 | tf_op jit(solution)/shard_map/ppermute | solution.py:324
  128.6 25.5 %collective-permute-start.25 = (bf16[2,4,256,128]{3,2,1,0:T(8,128)(2,1)}, bf16[2,4,256,128]{3,2,1,0:T(8,128)(2,1)S(1)}, u32[]{:S(2)}, u32[]{:S(2)}) collective-permute-start(bf16[2,4,256,128]{3,2,1,0:T(8,128)(2,1)} %get-tuple-element.33), channel_id=1, source_target_pairs={{0,16},{16,0},{32,48},{48,32},{64,80},{80,64},{96,112},{112,96},{1... | collective-permute-start | bytes 1572872 | tf_op jit(solution)/shard_map/ppermute | solution.py:406
  134.9 12.4 %collective-permute-start.19 = (bf16[2,4,256,128]{3,2,1,0:T(8,128)(2,1)S(1)}, bf16[2,4,256,128]{3,2,1,0:T(8,128)(2,1)}, u32[]{:S(2)}, u32[]{:S(2)}) collective-permute-start(bf16[2,4,256,128]{3,2,1,0:T(8,128)(2,1)S(1)} %add_convert_fusion.5), channel_id=1, source_target_pairs={{0,4},{1,5},{2,6},{3,7},{4,8},{5,9},{6,10},{7,11},{8,12},{9,13},{1... | collective-permute-start | bytes 1572872 | tf_op jit(solution)/shard_map/ppermute | solution.py:324
  134.9 6.7 %copy-start.8 = (bf16[2,4,256,128]{3,2,1,0:T(8,128)(2,1)S(1)}, bf16[2,4,256,128]{3,2,1,0:T(8,128)(2,1)}, u32[]{:S(2)}) copy-start(bf16[2,4,256,128]{3,2,1,0:T(8,128)(2,1)} %get-tuple-element.36) | copy-start | bytes 1572868
  135.9 18.2 %collective-permute-start.27 = (bf16[2,4,256,128]{3,2,1,0:T(8,128)(2,1)S(1)}, bf16[2,4,256,128]{3,2,1,0:T(8,128)(2,1)S(1)}, u32[]{:S(2)}, u32[]{:S(2)}) collective-permute-start(bf16[2,4,256,128]{3,2,1,0:T(8,128)(2,1)S(1)} %add_convert_fusion.2), channel_id=1, source_target_pairs={{0,12},{1,13},{2,14},{3,15},{4,0},{5,1},{6,2},{7,3},{8,4},{9,5},{1... | collective-permute-start | bytes 1572872 | tf_op jit(solution)/shard_map/ppermute | solution.py:324
  139.6 12.4 %collective-permute-start.23 = (bf16[2,4,256,128]{3,2,1,0:T(8,128)(2,1)}, bf16[2,4,256,128]{3,2,1,0:T(8,128)(2,1)}, u32[]{:S(2)}, u32[]{:S(2)}) collective-permute-start(bf16[2,4,256,128]{3,2,1,0:T(8,128)(2,1)} %add_convert_fusion.3), channel_id=1, source_target_pairs={{0,12},{1,13},{2,14},{3,15},{4,0},{5,1},{6,2},{7,3},{8,4},{9,5},{1... | collective-permute-start | bytes 1572872 | tf_op jit(solution)/shard_map/ppermute | solution.py:324
  141.6 1.0 copy-start.12
  141.6 1.1 copy-start.13
  142.6 11.5 %collective-permute-start.31 = (bf16[2,4,256,128]{3,2,1,0:T(8,128)(2,1)}, bf16[2,4,256,128]{3,2,1,0:T(8,128)(2,1)S(1)}, u32[]{:S(2)}, u32[]{:S(2)}) collective-permute-start(bf16[2,4,256,128]{3,2,1,0:T(8,128)(2,1)} %add_convert_fusion), channel_id=1, source_target_pairs={{0,4},{1,5},{2,6},{3,7},{4,8},{5,9},{6,10},{7,11},{8,12},{9,13},{1... | collective-permute-start | bytes 1572872 | tf_op jit(solution)/shard_map/ppermute | solution.py:324
  143.7 15.0 %all-to-all-start.2 = ((bf16[4,128,768]{2,1,0:T(8,128)(2,1)}), bf16[4,128,768]{2,1,0:T(8,128)(2,1)S(1)}, u32[]{:S(2)}, u32[]{:S(2)}) async-start(bf16[4,128,768]{2,1,0:T(8,128)(2,1)} %pad_maximum_fusion.1), calls=%async_computation.2 | async-start | bytes 1572864 | tf_op jit(solution)/shard_map/all_to_all | solution.py:366
  147.2 6.8 %copy-start.1 = (bf16[2,4,256,128]{3,2,1,0:T(8,128)(2,1)S(1)}, bf16[2,4,256,128]{3,2,1,0:T(8,128)(2,1)}, u32[]{:S(2)}) copy-start(bf16[2,4,256,128]{3,2,1,0:T(8,128)(2,1)} %get-tuple-element.32) | copy-start | bytes 1572868
  154.0 6.7 %collective-permute-start.24 = (bf16[4,256,128]{2,1,0:T(8,128)(2,1)}, bf16[4,256,128]{2,1,0:T(8,128)(2,1)}, u32[]{:S(2)}, u32[]{:S(2)}) collective-permute-start(bf16[4,256,128]{2,1,0:T(8,128)(2,1)} %fusion.5), channel_id=1, source_target_pairs={{0,3},{1,0},{2,1},{3,2},{4,7},{5,4},{6,5},{7,6},{8,11},{9,8},{10,9... | collective-permute-start | bytes 786440 | tf_op jit(solution)/shard_map/ppermute | solution.py:324
  155.1 7.8 %collective-permute-start.32 = (bf16[4,256,128]{2,1,0:T(8,128)(2,1)}, bf16[4,256,128]{2,1,0:T(8,128)(2,1)S(1)}, u32[]{:S(2)}, u32[]{:S(2)}) collective-permute-start(bf16[4,256,128]{2,1,0:T(8,128)(2,1)} %get-tuple-element.44), channel_id=1, source_target_pairs={{0,1},{1,2},{2,3},{3,0},{4,5},{5,6},{6,7},{7,4},{8,9},{9,10},{10,1... | collective-permute-start | bytes 786440 | tf_op jit(solution)/shard_map/ppermute | solution.py:324
  157.1 9.0 %copy-start.7 = (bf16[2,4,256,128]{3,2,1,0:T(8,128)(2,1)S(1)}, bf16[2,4,256,128]{3,2,1,0:T(8,128)(2,1)}, u32[]{:S(2)}) copy-start(bf16[2,4,256,128]{3,2,1,0:T(8,128)(2,1)} %get-tuple-element.24) | copy-start | bytes 1572868
  157.1 9.0 %collective-permute-start.33 = (bf16[4,256,128]{2,1,0:T(8,128)(2,1)S(1)}, bf16[4,256,128]{2,1,0:T(8,128)(2,1)S(1)}, u32[]{:S(2)}, u32[]{:S(2)}) collective-permute-start(bf16[4,256,128]{2,1,0:T(8,128)(2,1)S(1)} %get-tuple-element.45), channel_id=1, source_target_pairs={{0,2},{1,3},{2,0},{3,1},{4,6},{5,7},{6,4},{7,5},{8,10},{9,11},{10,... | collective-permute-start | bytes 786440 | tf_op jit(solution)/shard_map/ppermute | solution.py:324
  168.3 10.1 %all-to-all-start.3 = ((bf16[4,256,128]{2,1,0:T(8,128)(2,1)}), bf16[4,256,128]{2,1,0:T(8,128)(2,1)S(1)}, u32[]{:S(2)}, u32[]{:S(2)}) async-start(bf16[4,256,128]{2,1,0:T(8,128)(2,1)} %fusion.2), calls=%async_computation.3 | async-start | bytes 524288 | tf_op jit(solution)/shard_map/all_to_all | solution.py:366

commit v4 on v3

--- a/solution.py
+++ b/solution.py
@@ -38,13 +38,13 @@
     return [(OUTER[k], 2 * (k % 2) + e, ref, e) for k, ref in enumerate(refs) for e in range(2)]
 
 
-def attend_kernel(nseg, nblk, side, ids, parent, depth, both, *refs):
+def attend_kernel(nseg, nblk, side, parent, depth, both, *refs):
     pieces, refs = refs[:16], refs[16:]
     o_out, dq_out = refs[:2]
     parts, refs = refs[2:18], refs[18:]
-    kv, acc, s_buf, p_buf, mx, ls, o_acc, q_rows, d_rows, q_cols, d_cols, stage, in_sem, out_sem, tseg, tblk = refs
-    core = lax.rem(ids[0], 2)
-    pos = ids[1]
+    kv, acc, s_buf, p_buf, mx, ls, o_acc, q_rows, d_rows, q_cols, d_cols, stage, in_sem, out_sem, tseg, tblk, tsrc = refs
+    core = lax.rem(lax.axis_index("cand"), 2)
+    pos = lax.axis_index("ctx")
     cx, cz = lax.div(pos, side), lax.rem(pos, side)
 
     def block_of(route, outer, inner):
@@ -73,7 +73,10 @@
                 acc[p, 4 * b + e] = jnp.zeros((KVW, BLOCK), jnp.float32)
 
     def norm_step(p, top):
-        k = jnp.max(jnp.abs(kv[p, :, :, :HEAD].reshape(nblk * BLOCK // 16, 16, HEAD)), axis=0).astype(jnp.float32)
+        tops = [jnp.abs(kv[p, b, :, :HEAD]) for b in range(nblk)]
+        while len(tops) > 1:
+            tops = [jnp.maximum(x, y) for x, y in zip(tops[::2], tops[1::2])]
+        k = tops[0].astype(jnp.float32)
         k = jnp.max(k, axis=0, keepdims=True)
         return jnp.maximum(top, jnp.sum(k * k, axis=1, keepdims=True))
 
@@ -86,7 +89,7 @@
     def source(i, far, lo):
         if far:
             return kv[tseg[i], pl.ds(tblk[CHUNK * i], CHUNK), :, lo : lo + HEAD].reshape(NKEY, HEAD)
-        at = [jnp.minimum(tblk[CHUNK * i + e], nblk - 1) for e in range(CHUNK)]
+        at = [tsrc[CHUNK * i + e] for e in range(CHUNK)]
         return jnp.concatenate([kv[tseg[i], b, :, lo : lo + HEAD] for b in at], axis=0)
 
     def keys(i, far):
@@ -119,6 +122,7 @@
 
         def add_own(b, n):
             tblk[n] = b
+            tsrc[n] = b
             return n + lax.rem(jnp.right_shift(code, b), 2)
 
         seen = lax.fori_loop(0, pos, add_own, jnp.int32(0))
@@ -127,6 +131,7 @@
 
         def add_tail(n, _):
             tblk[n] = jnp.where(n == seen, pos, nblk)
+            tsrc[n] = pos
             return 0
 
         lax.fori_loop(seen, own * CHUNK, add_tail, 0)
@@ -244,24 +249,25 @@
     flushes = []
     for w in (1, 0):
         route = core if w == 0 else 1 - core
-        for outer, inner, ref, at in spans(parts[8 * w : 8 * w + 8]):
-            src = stage.at[w, outer * 4 + inner]
-            flushes.append(pltpu.make_async_copy(src, ref.at[at], out_sem.at[len(flushes)]))
-
-        @pl.loop(0, nblk)
-        def _(t):
-            b = block_of(route, lax.div(t, 4), lax.rem(t, 4))
-            for e in range(nseg):
-                stage[w, t, e, :HEAD] = (acc[nseg * w + e, b, :HEAD] * SCALE).astype(jnp.bfloat16)
-                stage[w, t, e, HEAD:] = acc[nseg * w + e, b, HEAD:].astype(jnp.bfloat16)
-
-        for cp in flushes[-16:]:
-            cp.start()
+        found = spans(parts[8 * w : 8 * w + 8])
+        for outer in (2, 1, 3, 0):
+            for inner in range(4):
+                b = block_of(route, outer, inner)
+                t = outer * 4 + inner
+                for e in range(nseg):
+                    stage[w, t, e, :HEAD] = (acc[nseg * w + e, b, :HEAD] * SCALE).astype(jnp.bfloat16)
+                    stage[w, t, e, HEAD:] = acc[nseg * w + e, b, HEAD:].astype(jnp.bfloat16)
+            for o, inner, ref, at in found:
+                if o == outer:
+                    src = stage.at[w, outer * 4 + inner]
+                    cp = pltpu.make_async_copy(src, ref.at[at], out_sem.at[len(flushes)])
+                    cp.start()
+                    flushes.append(cp)
     for cp in flushes:
         cp.wait()
 
 
-def attend(ids, parent, depth, both, pieces, side):
+def attend(parent, depth, both, pieces, side):
     nseg, nblk = both.shape[0], side * side
     groups = 3 * (nblk // CHUNK)
     vm = pl.BlockSpec(memory_space=pltpu.VMEM)
@@ -273,7 +279,7 @@
     return pl.pallas_call(
         functools.partial(attend_kernel, nseg, nblk, side),
         out_shape=[jax.ShapeDtypeStruct((nseg, BLOCK, ROWS), bf)] * 2 + parts,
-        in_specs=[sm, sm, sm, vm] + [hbm] * 16,
+        in_specs=[sm, sm, vm] + [hbm] * 16,
         out_specs=[vm, vm] + [hbm] * 16,
         scratch_shapes=[
             pltpu.VMEM((2 * nseg, nblk, BLOCK, KVW), bf),
@@ -292,6 +298,7 @@
             pltpu.SemaphoreType.DMA((32,)),
             pltpu.SMEM((groups,), jnp.int32),
             pltpu.SMEM((groups * CHUNK,), jnp.int32),
+            pltpu.SMEM((groups * CHUNK,), jnp.int32),
         ],
         compiler_params=pltpu.CompilerParams(vmem_limit_bytes=62 * 1024 * 1024),
         cost_estimate=pl.CostEstimate(
@@ -299,7 +306,7 @@
             bytes_accessed=4 * nseg * nblk * BLOCK * KVW * 2,
             transcendentals=nseg * 3 * nblk * BLOCK * ROWS,
         ),
-    )(ids, parent, depth, both, *pieces)
+    )(parent, depth, both, *pieces)
 
 
 BOTH_AXES = ("cand", "ctx")
@@ -399,8 +406,7 @@
     )
     both = spread(both)
 
-    ids = jnp.stack([lax.axis_index("cand"), pos]).astype(jnp.int32)
-    o, dq, *parts = attend(ids, parent, seg_depth, both, pieces, side)
+    o, dq, *parts = attend(parent, seg_depth, both, pieces, side)
 
     own, oth = parts[:8], parts[8:]
     came = [lax.ppermute(x, "cand", partner) for x in oth]

time: 181 us -> 181 us (level)
  transfers between devices with their start and end apart: 37 -> 37, of which waited for: 15 -> 15; matrix products, arithmetic and copies ran while one was open for 7% -> 6% of each run, Pallas kernels for 0% -> 0%
where the time goes in v4:
time: 181 us; the launch traced here: 179 us
  starting transfers between devices  59.6 us (33%)
  waiting for transfers between devices  48.5 us (27%)
  Pallas kernels  40.7 us (22%)
  other arithmetic  13.3 us (7%)
  blocking collectives  11.1 us (6%)
  local copies, waits for them, and re-layouts  4.93 us (3%)
    pallas_call x1, Pallas kernels, attend(): pl.pallas_call(functools.partial(attend_kernel, nseg, nblk, side), out_sh...  40.7 us
    ppermute x18, starting transfers between devices, hop(): return lax.ppermute(x, BOTH_AXES, perm)  39.4 us
    ppermute x18, waiting for transfers between devices, hop(): return lax.ppermute(x, BOTH_AXES, perm)  29.3 us
    all_to_all x3, waiting for transfers between devices, spread(): return lax.all_to_all(x, 'cand', 0, 0, axis_index_groups=same_core)  16.7 us
    all_to_all x1, blocking collectives, spread(): return lax.all_to_all(x, 'cand', 0, 0, axis_index_groups=same_core)  11.1 us
    all_to_all x3, starting transfers between devices, spread(): return lax.all_to_all(x, 'cand', 0, 0, axis_index_groups=same_core)  10.4 us
    ppermute x8, starting transfers between devices, per_device(): came = [lax.ppermute(x, 'cand', partner) for x in oth]  8.31 us
    convert_element_type x7, other arithmetic, add(): functools.reduce(jnp.add, [x.astype(jnp.float32) for x in xs])  5.74 us
  transfers between devices with their start and end apart: 37, of which 15 were waited for; matrix products, arithmetic and copies ran while one was open for 6% of the time, Pallas kernels for 0%

profile of v4, /device:TPU:0, one launch (start us, length us, event | category | flops | bytes accessed | tf_op | source)
XLA Modules:
  0.0 179.1 jit_solution(11178825131074671605)
XLA Ops:
  0.6 0.8 fusion.19
  1.5 0.8 fusion.20
  2.4 11.1 %all_to_all.20 = bf16[4,128,256]{2,1,0:T(8,128)(2,1)S(1)} all-to-all(bf16[4,128,256]{2,1,0:T(8,128)(2,1)S(1)} %pad_maximum_fusion.4), channel_id=1, replica_groups={{0,32,64,96},{16,48,80,112},{1,33,65,97},{17,49,81,113},{2,34,66,98},{1..., dimensions={0} | all-to-all | bytes 524288 | tf_op jit(solution)/shard_map/all_to_all | solution.py:373
  13.4 1.9 %collective-permute-start = (bf16[4,128,256]{2,1,0:T(8,128)(2,1)S(1)}, bf16[4,128,256]{2,1,0:T(8,128)(2,1)S(1)}, u32[]{:S(2)}, u32[]{:S(2)}) collective-permute-start(bf16[4,128,256]{2,1,0:T(8,128)(2,1)S(1)} %all_to_all.20), channel_id=1, source_target_pairs={{0,1},{1,2},{2,3},{3,0},{4,5},{5,6},{6,7},{7,4},{8,9},{9,10},{10,1... | collective-permute-start | bytes 786440 | tf_op jit(solution)/shard_map/ppermute | solution.py:331
  15.4 2.1 %collective-permute-start.2 = (bf16[4,128,256]{2,1,0:T(8,128)(2,1)S(1)}, bf16[4,128,256]{2,1,0:T(8,128)(2,1)S(1)}, u32[]{:S(2)}, u32[]{:S(2)}) collective-permute-start(bf16[4,128,256]{2,1,0:T(8,128)(2,1)S(1)} %all_to_all.20), channel_id=1, source_target_pairs={{0,3},{1,0},{2,1},{3,2},{4,7},{5,4},{6,5},{7,6},{8,11},{9,8},{10,9... | collective-permute-start | bytes 786440 | tf_op jit(solution)/shard_map/ppermute | solution.py:331
  17.5 1.9 %collective-permute-start.1 = (bf16[4,128,256]{2,1,0:T(8,128)(2,1)S(1)}, bf16[4,128,256]{2,1,0:T(8,128)(2,1)S(1)}, u32[]{:S(2)}, u32[]{:S(2)}) collective-permute-start(bf16[4,128,256]{2,1,0:T(8,128)(2,1)S(1)} %all_to_all.20), channel_id=1, source_target_pairs={{0,2},{1,3},{2,0},{3,1},{4,6},{5,7},{6,4},{7,5},{8,10},{9,11},{10,... | collective-permute-start | bytes 786440 | tf_op jit(solution)/shard_map/ppermute | solution.py:331
  19.3 2.5 %collective-permute-done = bf16[4,128,256]{2,1,0:T(8,128)(2,1)S(1)} collective-permute-done((bf16[4,128,256]{2,1,0:T(8,128)(2,1)S(1)}, bf16[4,128,256]{2,1,0:T(8,128)(2,1)S(1)}, u32[]{:S(2)}, u32[]{:S(2)}) %collective-permute-start) | collective-permute-done | bytes 262176 | tf_op jit(solution)/shard_map/ppermute | solution.py:331
  22.0 2.8 %collective-permute-start.5 = (bf16[2,4,128,256]{3,2,1,0:T(8,128)(2,1)S(1)}, bf16[2,4,128,256]{3,2,1,0:T(8,128)(2,1)S(1)}, u32[]{:S(2)}, u32[]{:S(2)}) collective-permute-start(bf16[2,4,128,256]{3,2,1,0:T(8,128)(2,1)S(1)} %pad_maximum_fusion.2.refs_0_), channel_id=1, source_target_pairs={{0,12},{1,13},{2,14},{3,15},{4,0},{5,1},{6,2},{7,3},{8,4},{9,5},{1... | collective-permute-start | bytes 1572872 | tf_op jit(solution)/shard_map/ppermute | solution.py:331
  24.8 1.3 collective-permute-done.1
  26.2 2.8 %collective-permute-start.6 = (bf16[2,4,128,256]{3,2,1,0:T(8,128)(2,1)S(1)}, bf16[2,4,128,256]{3,2,1,0:T(8,128)(2,1)}, u32[]{:S(2)}, u32[]{:S(2)}) collective-permute-start(bf16[2,4,128,256]{3,2,1,0:T(8,128)(2,1)S(1)} %pad_maximum_fusion.3.refs_1_), channel_id=1, source_target_pairs={{0,12},{1,13},{2,14},{3,15},{4,0},{5,1},{6,2},{7,3},{8,4},{9,5},{1... | collective-permute-start | bytes 1572872 | tf_op jit(solution)/shard_map/ppermute | solution.py:331
  29.1 2.4 %collective-permute-done.5.refs_4_ = bf16[2,4,128,256]{3,2,1,0:T(8,128)(2,1)S(1)} collective-permute-done((bf16[2,4,128,256]{3,2,1,0:T(8,128)(2,1)S(1)}, bf16[2,4,128,256]{3,2,1,0:T(8,128)(2,1)S(1)}, u32[]{:S(2)}, u32[]{:S(2)}) %collective-permute-start.5) | collective-permute-done | bytes 524320 | tf_op jit(solution)/shard_map/ppermute | solution.py:331
  31.5 0.3 collective-permute-start.13
  31.8 3.5 %collective-permute-done.3.refs_2_ = bf16[2,4,128,256]{3,2,1,0:T(8,128)(2,1)} collective-permute-done((bf16[2,4,128,256]{3,2,1,0:T(8,128)(2,1)S(1)}, bf16[2,4,128,256]{3,2,1,0:T(8,128)(2,1)}, u32[]{:S(2)}, u32[]{:S(2)}) %collective-permute-start.3) | collective-permute-done | bytes 524320 | tf_op jit(solution)/shard_map/ppermute | solution.py:331
  35.3 1.8 %collective-permute-done.6.refs_5_ = bf16[2,4,128,256]{3,2,1,0:T(8,128)(2,1)} collective-permute-done((bf16[2,4,128,256]{3,2,1,0:T(8,128)(2,1)S(1)}, bf16[2,4,128,256]{3,2,1,0:T(8,128)(2,1)}, u32[]{:S(2)}, u32[]{:S(2)}) %collective-permute-start.6) | collective-permute-done | bytes 524320 | tf_op jit(solution)/shard_map/ppermute | solution.py:331
  37.1 3.8 %collective-permute-start.8 = (bf16[2,4,128,256]{3,2,1,0:T(8,128)(2,1)}, bf16[2,4,128,256]{3,2,1,0:T(8,128)(2,1)}, u32[]{:S(2)}, u32[]{:S(2)}) collective-permute-start(bf16[2,4,128,256]{3,2,1,0:T(8,128)(2,1)} %collective-permute-done.6.refs_5_), channel_id=1, source_target_pairs={{0,12},{1,13},{2,14},{3,15},{4,0},{5,1},{6,2},{7,3},{8,4},{9,5},{1... | collective-permute-start | bytes 1572872 | tf_op jit(solution)/shard_map/ppermute | solution.py:331
  41.0 0.7 convert_bitcast_fusion
  41.8 1.1 pad_maximum_fusion
  42.9 3.5 %all-to-all-start = ((bf16[4,144,768]{2,1,0:T(8,128)(2,1)}), bf16[4,144,768]{2,1,0:T(8,128)(2,1)S(1)}, u32[]{:S(2)}, u32[]{:S(2)}) async-start(bf16[4,144,768]{2,1,0:T(8,128)(2,1)} %pad_maximum_fusion), calls=%async_computation | async-start | bytes 1769472 | tf_op jit(solution)/shard_map/all_to_all | solution.py:373
  46.5 0.5 collective-permute-start.14
  47.0 0.1 collective-permute-start.12
  47.1 0.4 collective-permute-start.15
  47.6 0.4 collective-permute-done.8.refs_7_
  47.9 10.8 %all-to-all-done.both = bf16[4,144,768]{2,1,0:T(8,128)(2,1)S(1)} async-done(((bf16[4,144,768]{2,1,0:T(8,128)(2,1)}), bf16[4,144,768]{2,1,0:T(8,128)(2,1)S(1)}, u32[]{:S(2)}, u32[]{:S(2)}) %all-to-all-start) | async-done | bytes 884768 | tf_op jit(solution)/shard_map/all_to_all | solution.py:373
  58.8 0.9 copy-done
  59.7 0.2 copy-done.17
  59.9 0.3 copy-done.18
  60.2 40.7 %shard_map.102 = (bf16[4,128,384]{2,1,0:T(8,128)(2,1)}, bf16[4,128,384]{2,1,0:T(8,128)(2,1)}, bf16[2,4,256,128]{3,2,1,0:T(8,128)(2,1)}, bf16[2,4,256,128]{3,2,1,...) custom-call(s32[8]{0:T(128)} %parent.1, s32[8]{0:T(128)} %depth.1, ...), custom_call_target="tpu_custom_call" | custom-call | flops 14495514624 | bytes 16777216 | tf_op jit(solution)/shard_map/pallas_call | solution.py:279
  100.8 6.6 %collective-permute-start.18 = (bf16[2,4,256,128]{3,2,1,0:T(8,128)(2,1)}, bf16[2,4,256,128]{3,2,1,0:T(8,128)(2,1)S(1)}, u32[]{:S(2)}, u32[]{:S(2)}) collective-permute-start(bf16[2,4,256,128]{3,2,1,0:T(8,128)(2,1)} %get-tuple-element.27), channel_id=1, source_target_pairs={{0,16},{16,0},{32,48},{48,32},{64,80},{80,64},{96,112},{112,96},{1... | collective-permute-start | bytes 1572872 | tf_op jit(solution)/shard_map/ppermute | solution.py:412
  107.5 0.3 collective-permute-start.21
  107.7 0.2 collective-permute-start.17
  108.0 0.3 collective-permute-start.20
  108.2 0.2 collective-permute-start.26
  108.5 0.7 collective-permute-done.18
  109.2 0.4 collective-permute-start.29
  109.6 1.2 add_convert_fusion.5
  110.8 0.2 collective-permute-start.28
  111.0 0.1 add_convert_fusion.4
  111.2 1.8 collective-permute-done.29
  112.9 14.4 %collective-permute-start.22 = (bf16[2,4,256,128]{3,2,1,0:T(8,128)(2,1)S(1)}, bf16[2,4,256,128]{3,2,1,0:T(8,128)(2,1)S(1)}, u32[]{:S(2)}, u32[]{:S(2)}) collective-permute-start(bf16[2,4,256,128]{3,2,1,0:T(8,128)(2,1)S(1)} %add_convert_fusion.4), channel_id=1, source_target_pairs={{0,12},{1,13},{2,14},{3,15},{4,0},{5,1},{6,2},{7,3},{8,4},{9,5},{1... | collective-permute-start | bytes 1572872 | tf_op jit(solution)/shard_map/ppermute | solution.py:331
  127.3 0.1 add_convert_fusion.1
  127.6 0.1 add_convert_fusion.2
  127.9 6.2 %collective-permute-done.22 = bf16[2,4,256,128]{3,2,1,0:T(8,128)(2,1)S(1)} collective-permute-done((bf16[2,4,256,128]{3,2,1,0:T(8,128)(2,1)S(1)}, bf16[2,4,256,128]{3,2,1,0:T(8,128)(2,1)S(1)}, u32[]{:S(2)}, u32[]{:S(2)}) %collective-permute-start.22) | collective-permute-done | bytes 524320 | tf_op jit(solution)/shard_map/ppermute | solution.py:331
  134.1 1.0 add_convert_fusion.3
  135.1 3.7 %collective-permute-start.27 = (bf16[2,4,256,128]{3,2,1,0:T(8,128)(2,1)S(1)}, bf16[2,4,256,128]{3,2,1,0:T(8,128)(2,1)S(1)}, u32[]{:S(2)}, u32[]{:S(2)}) collective-permute-start(bf16[2,4,256,128]{3,2,1,0:T(8,128)(2,1)S(1)} %add_convert_fusion.2), channel_id=1, source_target_pairs={{0,12},{1,13},{2,14},{3,15},{4,0},{5,1},{6,2},{7,3},{8,4},{9,5},{1... | collective-permute-start | bytes 1572872 | tf_op jit(solution)/shard_map/ppermute | solution.py:331
  138.8 2.0 %collective-permute-start.23 = (bf16[2,4,256,128]{3,2,1,0:T(8,128)(2,1)}, bf16[2,4,256,128]{3,2,1,0:T(8,128)(2,1)}, u32[]{:S(2)}, u32[]{:S(2)}) collective-permute-start(bf16[2,4,256,128]{3,2,1,0:T(8,128)(2,1)} %add_convert_fusion.3), channel_id=1, source_target_pairs={{0,12},{1,13},{2,14},{3,15},{4,0},{5,1},{6,2},{7,3},{8,4},{9,5},{1... | collective-permute-start | bytes 1572872 | tf_op jit(solution)/shard_map/ppermute | solution.py:331
  140.8 1.0 add_convert_fusion
  141.8 0.1 copy-done.13
  141.9 1.0 pad_maximum_fusion.1
  142.9 3.5 %all-to-all-start.2 = ((bf16[4,128,768]{2,1,0:T(8,128)(2,1)}), bf16[4,128,768]{2,1,0:T(8,128)(2,1)S(1)}, u32[]{:S(2)}, u32[]{:S(2)}) async-start(bf16[4,128,768]{2,1,0:T(8,128)(2,1)} %pad_maximum_fusion.1), calls=%async_computation.2 | async-start | bytes 1572864 | tf_op jit(solution)/shard_map/all_to_all | solution.py:373
  146.4 4.8 %collective-permute-done.23 = bf16[2,4,256,128]{3,2,1,0:T(8,128)(2,1)} collective-permute-done((bf16[2,4,256,128]{3,2,1,0:T(8,128)(2,1)}, bf16[2,4,256,128]{3,2,1,0:T(8,128)(2,1)}, u32[]{:S(2)}, u32[]{:S(2)}) %collective-permute-start.23) | collective-permute-done | bytes 524320 | tf_op jit(solution)/shard_map/ppermute | solution.py:331
  151.2 2.0 %fusion.5 = bf16[4,256,128]{2,1,0:T(8,128)(2,1)} fusion(bf16[2,4,256,128]{3,2,1,0:T(8,128)(2,1)} %collective-permute-done.23, bf16[2,4,256,128]{3,2,1,0:T(8,128)(2,1)} %collective-permute-done.19, bf16[2,4,256,128]{3,2,1,0:T(8,128)(2,1)} %collective-permute-done.17, bf16[2,4,256,128]{3,2,1,0:T(8,128)(2,1)} %get-tuple-element.24), kind=kLoop, calls=%fused_computation.23 | loop fusion | flops 1048576 | bytes 1310720 | tf_op jit(solution)/shard_map/add | solution.py:327
  153.3 1.0 fusion.6
  154.2 2.0 %collective-permute-start.32 = (bf16[4,256,128]{2,1,0:T(8,128)(2,1)}, bf16[4,256,128]{2,1,0:T(8,128)(2,1)S(1)}, u32[]{:S(2)}, u32[]{:S(2)}) collective-permute-start(bf16[4,256,128]{2,1,0:T(8,128)(2,1)} %get-tuple-element.44), channel_id=1, source_target_pairs={{0,1},{1,2},{2,3},{3,0},{4,5},{5,6},{6,7},{7,4},{8,9},{9,10},{10,1... | collective-permute-start | bytes 786440 | tf_op jit(solution)/shard_map/ppermute | solution.py:331
  156.3 1.7 collective-permute-start.33
  158.1 0.8 maximum_bitcast_fusion.1
  158.9 1.0 collective-permute-done.24
  159.9 2.1 %collective-permute-done.32 = bf16[4,256,128]{2,1,0:T(8,128)(2,1)S(1)} collective-permute-done((bf16[4,256,128]{2,1,0:T(8,128)(2,1)}, bf16[4,256,128]{2,1,0:T(8,128)(2,1)S(1)}, u32[]{:S(2)}, u32[]{:S(2)}) %collective-permute-start.32) | collective-permute-done | bytes 262176 | tf_op jit(solution)/shard_map/ppermute | solution.py:331
  162.0 3.3 %collective-permute-done.33 = bf16[4,256,128]{2,1,0:T(8,128)(2,1)S(1)} collective-permute-done((bf16[4,256,128]{2,1,0:T(8,128)(2,1)S(1)}, bf16[4,256,128]{2,1,0:T(8,128)(2,1)S(1)}, u32[]{:S(2)}, u32[]{:S(2)}) %collective-permute-start.33) | collective-permute-done | bytes 262176 | tf_op jit(solution)/shard_map/ppermute | solution.py:331
  165.4 2.1 %fusion.2 = bf16[4,256,128]{2,1,0:T(8,128)(2,1)} fusion(bf16[4,256,128]{2,1,0:T(8,128)(2,1)S(1)} %collective-permute-done.33, bf16[4,256,128]{2,1,0:T(8,128)(2,1)S(1)} %collective-permute-done.32, bf16[4,256,128]{2,1,0:T(8,128)(2,1)} %collective-permute-done.24, bf16[2,4,256,128]{3,2,1,0:T(8,128)(2,1)} %collective-permute-done.23, ...), kind=kLoop, calls=%fused_computation.13 | loop fusion | flops 2097152 | bytes 2097152 | tf_op jit(solution)/shard_map/convert_element_type | solution.py:327
  167.5 3.4 %all-to-all-start.3 = ((bf16[4,256,128]{2,1,0:T(8,128)(2,1)}), bf16[4,256,128]{2,1,0:T(8,128)(2,1)S(1)}, u32[]{:S(2)}, u32[]{:S(2)}) async-start(bf16[4,256,128]{2,1,0:T(8,128)(2,1)} %fusion.2), calls=%async_computation.3 | async-start | bytes 524288 | tf_op jit(solution)/shard_map/all_to_all | solution.py:373
  170.9 0.8 maximum_bitcast_fusion
  171.7 5.9 %all-to-all-done.3 = bf16[4,256,128]{2,1,0:T(8,128)(2,1)S(1)} async-done(((bf16[4,256,128]{2,1,0:T(8,128)(2,1)}), bf16[4,256,128]{2,1,0:T(8,128)(2,1)S(1)}, u32[]{:S(2)}, u32[]{:S(2)}) %all-to-all-start.3) | async-done | bytes 262176 | tf_op jit(solution)/shard_map/all_to_all | solution.py:373
  177.6 0.8 copy.12
  178.4 0.8 copy.11
  (77 shorter events, 1.0 us)
Async XLA Ops:
  13.4 8.4 %collective-permute-start = (bf16[4,128,256]{2,1,0:T(8,128)(2,1)S(1)}, bf16[4,128,256]{2,1,0:T(8,128)(2,1)S(1)}, u32[]{:S(2)}, u32[]{:S(2)}) collective-permute-start(bf16[4,128,256]{2,1,0:T(8,128)(2,1)S(1)} %all_to_all.20), channel_id=1, source_target_pairs={{0,1},{1,2},{2,3},{3,0},{4,5},{5,6},{6,7},{7,4},{8,9},{9,10},{10,1... | collective-permute-start | bytes 786440 | tf_op jit(solution)/shard_map/ppermute | solution.py:331
  15.4 9.5 %collective-permute-start.2 = (bf16[4,128,256]{2,1,0:T(8,128)(2,1)S(1)}, bf16[4,128,256]{2,1,0:T(8,128)(2,1)S(1)}, u32[]{:S(2)}, u32[]{:S(2)}) collective-permute-start(bf16[4,128,256]{2,1,0:T(8,128)(2,1)S(1)} %all_to_all.20), channel_id=1, source_target_pairs={{0,3},{1,0},{2,1},{3,2},{4,7},{5,4},{6,5},{7,6},{8,11},{9,8},{10,9... | collective-permute-start | bytes 786440 | tf_op jit(solution)/shard_map/ppermute | solution.py:331
  17.5 8.6 %collective-permute-start.1 = (bf16[4,128,256]{2,1,0:T(8,128)(2,1)S(1)}, bf16[4,128,256]{2,1,0:T(8,128)(2,1)S(1)}, u32[]{:S(2)}, u32[]{:S(2)}) collective-permute-start(bf16[4,128,256]{2,1,0:T(8,128)(2,1)S(1)} %all_to_all.20), channel_id=1, source_target_pairs={{0,2},{1,3},{2,0},{3,1},{4,6},{5,7},{6,4},{7,5},{8,10},{9,11},{10,... | collective-permute-start | bytes 786440 | tf_op jit(solution)/shard_map/ppermute | solution.py:331
  21.8 19.1 %copy-start.10 = (bf16[1,128,1536]{2,1,0:T(8,128)(2,1)S(1)}, bf16[1,128,1536]{2,1,0:T(8,128)(2,1)}, u32[]{:S(2)}) copy-start(bf16[1,128,1536]{2,1,0:T(8,128)(2,1)} %param.7) | copy-start | bytes 1179652
  21.8 19.1 %copy-start.11 = (bf16[1,128,1536]{2,1,0:T(8,128)(2,1)S(1)}, bf16[1,128,1536]{2,1,0:T(8,128)(2,1)}, u32[]{:S(2)}) copy-start(bf16[1,128,1536]{2,1,0:T(8,128)(2,1)} %param.10) | copy-start | bytes 1179652
  21.9 19.1 %copy-start.5 = (bf16[2,4,128,256]{3,2,1,0:T(8,128)(2,1)}, bf16[2,4,128,256]{3,2,1,0:T(8,128)(2,1)S(1)}, u32[]{:S(2)}) copy-start(bf16[2,4,128,256]{3,2,1,0:T(8,128)(2,1)S(1)} %pad_maximum_fusion.2.refs_0_) | copy-start | bytes 1572868
  21.9 7.1 %collective-permute-start.9 = (bf16[2,4,128,256]{3,2,1,0:T(8,128)(2,1)S(1)}, bf16[2,4,128,256]{3,2,1,0:T(8,128)(2,1)S(1)}, u32[]{:S(2)}, u32[]{:S(2)}) collective-permute-start(bf16[2,4,128,256]{3,2,1,0:T(8,128)(2,1)S(1)} %pad_maximum_fusion.2.refs_0_), channel_id=1, source_target_pairs={{0,16},{16,0},{32,48},{48,32},{64,80},{80,64},{96,112},{112,96},{1... | collective-permute-start | bytes 1572872 | tf_op jit(solution)/shard_map/ppermute | solution.py:389
  22.0 9.5 %collective-permute-start.5 = (bf16[2,4,128,256]{3,2,1,0:T(8,128)(2,1)S(1)}, bf16[2,4,128,256]{3,2,1,0:T(8,128)(2,1)S(1)}, u32[]{:S(2)}, u32[]{:S(2)}) collective-permute-start(bf16[2,4,128,256]{3,2,1,0:T(8,128)(2,1)S(1)} %pad_maximum_fusion.2.refs_0_), channel_id=1, source_target_pairs={{0,12},{1,13},{2,14},{3,15},{4,0},{5,1},{6,2},{7,3},{8,4},{9,5},{1... | collective-permute-start | bytes 1572872 | tf_op jit(solution)/shard_map/ppermute | solution.py:331
  24.8 10.5 %collective-permute-start.3 = (bf16[2,4,128,256]{3,2,1,0:T(8,128)(2,1)S(1)}, bf16[2,4,128,256]{3,2,1,0:T(8,128)(2,1)}, u32[]{:S(2)}, u32[]{:S(2)}) collective-permute-start(bf16[2,4,128,256]{3,2,1,0:T(8,128)(2,1)S(1)} %pad_maximum_fusion.2.refs_0_), channel_id=1, source_target_pairs={{0,4},{1,5},{2,6},{3,7},{4,8},{5,9},{6,10},{7,11},{8,12},{9,13},{1... | collective-permute-start | bytes 1572872 | tf_op jit(solution)/shard_map/ppermute | solution.py:331
  26.1 15.7 %copy-start.6 = (bf16[2,4,128,256]{3,2,1,0:T(8,128)(2,1)}, bf16[2,4,128,256]{3,2,1,0:T(8,128)(2,1)S(1)}, u32[]{:S(2)}) copy-start(bf16[2,4,128,256]{3,2,1,0:T(8,128)(2,1)S(1)} %pad_maximum_fusion.3.refs_1_) | copy-start | bytes 1572868
  26.2 11.0 %collective-permute-start.6 = (bf16[2,4,128,256]{3,2,1,0:T(8,128)(2,1)S(1)}, bf16[2,4,128,256]{3,2,1,0:T(8,128)(2,1)}, u32[]{:S(2)}, u32[]{:S(2)}) collective-permute-start(bf16[2,4,128,256]{3,2,1,0:T(8,128)(2,1)S(1)} %pad_maximum_fusion.3.refs_1_), channel_id=1, source_target_pairs={{0,12},{1,13},{2,14},{3,15},{4,0},{5,1},{6,2},{7,3},{8,4},{9,5},{1... | collective-permute-start | bytes 1572872 | tf_op jit(solution)/shard_map/ppermute | solution.py:331
  29.0 17.5 %collective-permute-start.10 = (bf16[2,4,128,256]{3,2,1,0:T(8,128)(2,1)S(1)}, bf16[2,4,128,256]{3,2,1,0:T(8,128)(2,1)}, u32[]{:S(2)}, u32[]{:S(2)}) collective-permute-start(bf16[2,4,128,256]{3,2,1,0:T(8,128)(2,1)S(1)} %pad_maximum_fusion.3.refs_1_), channel_id=1, source_target_pairs={{0,16},{16,0},{32,48},{48,32},{64,80},{80,64},{96,112},{112,96},{1... | collective-permute-start | bytes 1572872 | tf_op jit(solution)/shard_map/ppermute | solution.py:389
  29.0 12.8 %copy-start.14 = (bf16[2,4,128,256]{3,2,1,0:T(8,128)(2,1)}, bf16[2,4,128,256]{3,2,1,0:T(8,128)(2,1)S(1)}, u32[]{:S(2)}) copy-start(bf16[2,4,128,256]{3,2,1,0:T(8,128)(2,1)S(1)} %collective-permute-done.9.refs_8_) | copy-start | bytes 1572868
  29.0 17.5 %collective-permute-start.4 = (bf16[2,4,128,256]{3,2,1,0:T(8,128)(2,1)S(1)}, bf16[2,4,128,256]{3,2,1,0:T(8,128)(2,1)}, u32[]{:S(2)}, u32[]{:S(2)}) collective-permute-start(bf16[2,4,128,256]{3,2,1,0:T(8,128)(2,1)S(1)} %pad_maximum_fusion.3.refs_1_), channel_id=1, source_target_pairs={{0,4},{1,5},{2,6},{3,7},{4,8},{5,9},{6,10},{7,11},{8,12},{9,13},{1... | collective-permute-start | bytes 1572872 | tf_op jit(solution)/shard_map/ppermute | solution.py:331
  31.5 10.3 %copy-start.15 = (bf16[2,4,128,256]{3,2,1,0:T(8,128)(2,1)}, bf16[2,4,128,256]{3,2,1,0:T(8,128)(2,1)S(1)}, u32[]{:S(2)}) copy-start(bf16[2,4,128,256]{3,2,1,0:T(8,128)(2,1)S(1)} %collective-permute-done.5.refs_4_) | copy-start | bytes 1572868
  31.5 15.5 %collective-permute-start.13 = (bf16[2,4,128,256]{3,2,1,0:T(8,128)(2,1)S(1)}, bf16[2,4,128,256]{3,2,1,0:T(8,128)(2,1)}, u32[]{:S(2)}, u32[]{:S(2)}) collective-permute-start(bf16[2,4,128,256]{3,2,1,0:T(8,128)(2,1)S(1)} %collective-permute-done.5.refs_4_), channel_id=1, source_target_pairs={{0,16},{16,0},{32,48},{48,32},{64,80},{80,64},{96,112},{112,96},{1... | collective-permute-start | bytes 1572872 | tf_op jit(solution)/shard_map/ppermute | solution.py:389
  35.3 11.8 %collective-permute-start.7 = (bf16[2,4,128,256]{3,2,1,0:T(8,128)(2,1)}, bf16[2,4,128,256]{3,2,1,0:T(8,128)(2,1)}, u32[]{:S(2)}, u32[]{:S(2)}) collective-permute-start(bf16[2,4,128,256]{3,2,1,0:T(8,128)(2,1)} %collective-permute-done.3.refs_2_), channel_id=1, source_target_pairs={{0,4},{1,5},{2,6},{3,7},{4,8},{5,9},{6,10},{7,11},{8,12},{9,13},{1... | collective-permute-start | bytes 1572872 | tf_op jit(solution)/shard_map/ppermute | solution.py:331
  37.1 10.8 %collective-permute-start.8 = (bf16[2,4,128,256]{3,2,1,0:T(8,128)(2,1)}, bf16[2,4,128,256]{3,2,1,0:T(8,128)(2,1)}, u32[]{:S(2)}, u32[]{:S(2)}) collective-permute-start(bf16[2,4,128,256]{3,2,1,0:T(8,128)(2,1)} %collective-permute-done.6.refs_5_), channel_id=1, source_target_pairs={{0,12},{1,13},{2,14},{3,15},{4,0},{5,1},{6,2},{7,3},{8,4},{9,5},{1... | collective-permute-start | bytes 1572872 | tf_op jit(solution)/shard_map/ppermute | solution.py:331
  42.9 15.8 %all-to-all-start = ((bf16[4,144,768]{2,1,0:T(8,128)(2,1)}), bf16[4,144,768]{2,1,0:T(8,128)(2,1)S(1)}, u32[]{:S(2)}, u32[]{:S(2)}) async-start(bf16[4,144,768]{2,1,0:T(8,128)(2,1)} %pad_maximum_fusion), calls=%async_computation | async-start | bytes 1769472 | tf_op jit(solution)/shard_map/all_to_all | solution.py:373
  46.4 12.3 %collective-permute-start.11 = (bf16[2,4,128,256]{3,2,1,0:T(8,128)(2,1)}, bf16[2,4,128,256]{3,2,1,0:T(8,128)(2,1)S(1)}, u32[]{:S(2)}, u32[]{:S(2)}) collective-permute-start(bf16[2,4,128,256]{3,2,1,0:T(8,128)(2,1)} %collective-permute-done.3.refs_2_), channel_id=1, source_target_pairs={{0,16},{16,0},{32,48},{48,32},{64,80},{80,64},{96,112},{112,96},{1... | collective-permute-start | bytes 1572872 | tf_op jit(solution)/shard_map/ppermute | solution.py:389
  46.5 12.2 %collective-permute-start.14 = (bf16[2,4,128,256]{3,2,1,0:T(8,128)(2,1)}, bf16[2,4,128,256]{3,2,1,0:T(8,128)(2,1)}, u32[]{:S(2)}, u32[]{:S(2)}) collective-permute-start(bf16[2,4,128,256]{3,2,1,0:T(8,128)(2,1)} %collective-permute-done.6.refs_5_), channel_id=1, source_target_pairs={{0,16},{16,0},{32,48},{48,32},{64,80},{80,64},{96,112},{112,96},{1... | collective-permute-start | bytes 1572872 | tf_op jit(solution)/shard_map/ppermute | solution.py:389
  47.0 11.7 %collective-permute-start.12 = (bf16[2,4,128,256]{3,2,1,0:T(8,128)(2,1)}, bf16[2,4,128,256]{3,2,1,0:T(8,128)(2,1)S(1)}, u32[]{:S(2)}, u32[]{:S(2)}) collective-permute-start(bf16[2,4,128,256]{3,2,1,0:T(8,128)(2,1)} %collective-permute-done.4.refs_3_), channel_id=1, source_target_pairs={{0,16},{16,0},{32,48},{48,32},{64,80},{80,64},{96,112},{112,96},{1... | collective-permute-start | bytes 1572872 | tf_op jit(solution)/shard_map/ppermute | solution.py:389
  47.1 11.6 %collective-permute-start.15 = (bf16[2,4,128,256]{3,2,1,0:T(8,128)(2,1)}, bf16[2,4,128,256]{3,2,1,0:T(8,128)(2,1)}, u32[]{:S(2)}, u32[]{:S(2)}) collective-permute-start(bf16[2,4,128,256]{3,2,1,0:T(8,128)(2,1)} %collective-permute-done.7.refs_6_), channel_id=1, source_target_pairs={{0,16},{16,0},{32,48},{48,32},{64,80},{80,64},{96,112},{112,96},{1... | collective-permute-start | bytes 1572872 | tf_op jit(solution)/shard_map/ppermute | solution.py:389
  47.9 10.8 %collective-permute-start.16 = (bf16[2,4,128,256]{3,2,1,0:T(8,128)(2,1)}, bf16[2,4,128,256]{3,2,1,0:T(8,128)(2,1)}, u32[]{:S(2)}, u32[]{:S(2)}) collective-permute-start(bf16[2,4,128,256]{3,2,1,0:T(8,128)(2,1)} %collective-permute-done.8.refs_7_), channel_id=1, source_target_pairs={{0,16},{16,0},{32,48},{48,32},{64,80},{80,64},{96,112},{112,96},{1... | collective-permute-start | bytes 1572872 | tf_op jit(solution)/shard_map/ppermute | solution.py:389
  58.7 1.0 copy-start
  58.7 1.2 copy-start.17
  58.8 1.4 copy-start.18
  100.8 10.0 %copy-start.16 = (bf16[2,4,256,128]{3,2,1,0:T(8,128)(2,1)S(1)}, bf16[2,4,256,128]{3,2,1,0:T(8,128)(2,1)}, u32[]{:S(2)}) copy-start(bf16[2,4,256,128]{3,2,1,0:T(8,128)(2,1)} %get-tuple-element.37) | copy-start | bytes 1572868
  100.8 10.2 %copy-start.4 = (bf16[2,4,256,128]{3,2,1,0:T(8,128)(2,1)S(1)}, bf16[2,4,256,128]{3,2,1,0:T(8,128)(2,1)}, u32[]{:S(2)}) copy-start(bf16[2,4,256,128]{3,2,1,0:T(8,128)(2,1)} %get-tuple-element.30) | copy-start | bytes 1572868
  100.8 8.4 %collective-permute-start.18 = (bf16[2,4,256,128]{3,2,1,0:T(8,128)(2,1)}, bf16[2,4,256,128]{3,2,1,0:T(8,128)(2,1)S(1)}, u32[]{:S(2)}, u32[]{:S(2)}) collective-permute-start(bf16[2,4,256,128]{3,2,1,0:T(8,128)(2,1)} %get-tuple-element.27), channel_id=1, source_target_pairs={{0,16},{16,0},{32,48},{48,32},{64,80},{80,64},{96,112},{112,96},{1... | collective-permute-start | bytes 1572872 | tf_op jit(solution)/shard_map/ppermute | solution.py:412
  107.5 3.3 %collective-permute-start.21 = (bf16[2,4,256,128]{3,2,1,0:T(8,128)(2,1)}, bf16[2,4,256,128]{3,2,1,0:T(8,128)(2,1)S(1)}, u32[]{:S(2)}, u32[]{:S(2)}) collective-permute-start(bf16[2,4,256,128]{3,2,1,0:T(8,128)(2,1)} %get-tuple-element.31), channel_id=1, source_target_pairs={{0,16},{16,0},{32,48},{48,32},{64,80},{80,64},{96,112},{112,96},{1... | collective-permute-start | bytes 1572872 | tf_op jit(solution)/shard_map/ppermute | solution.py:412
  107.7 34.1 %collective-permute-start.17 = (bf16[2,4,256,128]{3,2,1,0:T(8,128)(2,1)}, bf16[2,4,256,128]{3,2,1,0:T(8,128)(2,1)}, u32[]{:S(2)}, u32[]{:S(2)}) collective-permute-start(bf16[2,4,256,128]{3,2,1,0:T(8,128)(2,1)} %get-tuple-element.25), channel_id=1, source_target_pairs={{0,16},{16,0},{32,48},{48,32},{64,80},{80,64},{96,112},{112,96},{1... | collective-permute-start | bytes 1572872 | tf_op jit(solution)/shard_map/ppermute | solution.py:412
  108.0 19.8 %collective-permute-start.20 = (bf16[2,4,256,128]{3,2,1,0:T(8,128)(2,1)}, bf16[2,4,256,128]{3,2,1,0:T(8,128)(2,1)S(1)}, u32[]{:S(2)}, u32[]{:S(2)}) collective-permute-start(bf16[2,4,256,128]{3,2,1,0:T(8,128)(2,1)} %get-tuple-element.29), channel_id=1, source_target_pairs={{0,16},{16,0},{32,48},{48,32},{64,80},{80,64},{96,112},{112,96},{1... | collective-permute-start | bytes 1572872 | tf_op jit(solution)/shard_map/ppermute | solution.py:412
  108.2 19.3 %collective-permute-start.26 = (bf16[2,4,256,128]{3,2,1,0:T(8,128)(2,1)}, bf16[2,4,256,128]{3,2,1,0:T(8,128)(2,1)S(1)}, u32[]{:S(2)}, u32[]{:S(2)}) collective-permute-start(bf16[2,4,256,128]{3,2,1,0:T(8,128)(2,1)} %get-tuple-element.35), channel_id=1, source_target_pairs={{0,16},{16,0},{32,48},{48,32},{64,80},{80,64},{96,112},{112,96},{1... | collective-permute-start | bytes 1572872 | tf_op jit(solution)/shard_map/ppermute | solution.py:412
  109.2 3.7 %collective-permute-start.29 = (bf16[2,4,256,128]{3,2,1,0:T(8,128)(2,1)}, bf16[2,4,256,128]{3,2,1,0:T(8,128)(2,1)S(1)}, u32[]{:S(2)}, u32[]{:S(2)}) collective-permute-start(bf16[2,4,256,128]{3,2,1,0:T(8,128)(2,1)} %get-tuple-element.39), channel_id=1, source_target_pairs={{0,16},{16,0},{32,48},{48,32},{64,80},{80,64},{96,112},{112,96},{1... | collective-permute-start | bytes 1572872 | tf_op jit(solution)/shard_map/ppermute | solution.py:412
  110.8 16.6 %copy-start.3 = (bf16[2,4,256,128]{3,2,1,0:T(8,128)(2,1)S(1)}, bf16[2,4,256,128]{3,2,1,0:T(8,128)(2,1)}, u32[]{:S(2)}) copy-start(bf16[2,4,256,128]{3,2,1,0:T(8,128)(2,1)} %get-tuple-element.38) | copy-start | bytes 1572868
  110.8 24.3 %collective-permute-start.28 = (bf16[2,4,256,128]{3,2,1,0:T(8,128)(2,1)S(1)}, bf16[2,4,256,128]{3,2,1,0:T(8,128)(2,1)S(1)}, u32[]{:S(2)}, u32[]{:S(2)}) collective-permute-start(bf16[2,4,256,128]{3,2,1,0:T(8,128)(2,1)S(1)} %copy-done.16), channel_id=1, source_target_pairs={{0,16},{16,0},{32,48},{48,32},{64,80},{80,64},{96,112},{112,96},{1... | collective-permute-start | bytes 1572872 | tf_op jit(solution)/shard_map/ppermute | solution.py:412
  111.1 16.4 %copy-start.2 = (bf16[2,4,256,128]{3,2,1,0:T(8,128)(2,1)S(1)}, bf16[2,4,256,128]{3,2,1,0:T(8,128)(2,1)}, u32[]{:S(2)}) copy-start(bf16[2,4,256,128]{3,2,1,0:T(8,128)(2,1)} %get-tuple-element.34) | copy-start | bytes 1572868
  112.9 21.1 %collective-permute-start.22 = (bf16[2,4,256,128]{3,2,1,0:T(8,128)(2,1)S(1)}, bf16[2,4,256,128]{3,2,1,0:T(8,128)(2,1)S(1)}, u32[]{:S(2)}, u32[]{:S(2)}) collective-permute-start(bf16[2,4,256,128]{3,2,1,0:T(8,128)(2,1)S(1)} %add_convert_fusion.4), channel_id=1, source_target_pairs={{0,12},{1,13},{2,14},{3,15},{4,0},{5,1},{6,2},{7,3},{8,4},{9,5},{1... | collective-permute-start | bytes 1572872 | tf_op jit(solution)/shard_map/ppermute | solution.py:331
  127.5 6.6 %copy-start.9 = (bf16[2,4,256,128]{3,2,1,0:T(8,128)(2,1)S(1)}, bf16[2,4,256,128]{3,2,1,0:T(8,128)(2,1)}, u32[]{:S(2)}) copy-start(bf16[2,4,256,128]{3,2,1,0:T(8,128)(2,1)} %get-tuple-element.28) | copy-start | bytes 1572868
  127.5 11.3 %collective-permute-start.30 = (bf16[2,4,256,128]{3,2,1,0:T(8,128)(2,1)S(1)}, bf16[2,4,256,128]{3,2,1,0:T(8,128)(2,1)S(1)}, u32[]{:S(2)}, u32[]{:S(2)}) collective-permute-start(bf16[2,4,256,128]{3,2,1,0:T(8,128)(2,1)S(1)} %add_convert_fusion.1), channel_id=1, source_target_pairs={{0,4},{1,5},{2,6},{3,7},{4,8},{5,9},{6,10},{7,11},{8,12},{9,13},{1... | collective-permute-start | bytes 1572872 | tf_op jit(solution)/shard_map/ppermute | solution.py:331
  127.8 25.5 %collective-permute-start.25 = (bf16[2,4,256,128]{3,2,1,0:T(8,128)(2,1)}, bf16[2,4,256,128]{3,2,1,0:T(8,128)(2,1)S(1)}, u32[]{:S(2)}, u32[]{:S(2)}) collective-permute-start(bf16[2,4,256,128]{3,2,1,0:T(8,128)(2,1)} %get-tuple-element.33), channel_id=1, source_target_pairs={{0,16},{16,0},{32,48},{48,32},{64,80},{80,64},{96,112},{112,96},{1... | collective-permute-start | bytes 1572872 | tf_op jit(solution)/shard_map/ppermute | solution.py:412
  134.0 12.4 %collective-permute-start.19 = (bf16[2,4,256,128]{3,2,1,0:T(8,128)(2,1)S(1)}, bf16[2,4,256,128]{3,2,1,0:T(8,128)(2,1)}, u32[]{:S(2)}, u32[]{:S(2)}) collective-permute-start(bf16[2,4,256,128]{3,2,1,0:T(8,128)(2,1)S(1)} %add_convert_fusion.5), channel_id=1, source_target_pairs={{0,4},{1,5},{2,6},{3,7},{4,8},{5,9},{6,10},{7,11},{8,12},{9,13},{1... | collective-permute-start | bytes 1572872 | tf_op jit(solution)/shard_map/ppermute | solution.py:331
  134.1 6.7 %copy-start.8 = (bf16[2,4,256,128]{3,2,1,0:T(8,128)(2,1)S(1)}, bf16[2,4,256,128]{3,2,1,0:T(8,128)(2,1)}, u32[]{:S(2)}) copy-start(bf16[2,4,256,128]{3,2,1,0:T(8,128)(2,1)} %get-tuple-element.36) | copy-start | bytes 1572868
  135.1 18.2 %collective-permute-start.27 = (bf16[2,4,256,128]{3,2,1,0:T(8,128)(2,1)S(1)}, bf16[2,4,256,128]{3,2,1,0:T(8,128)(2,1)S(1)}, u32[]{:S(2)}, u32[]{:S(2)}) collective-permute-start(bf16[2,4,256,128]{3,2,1,0:T(8,128)(2,1)S(1)} %add_convert_fusion.2), channel_id=1, source_target_pairs={{0,12},{1,13},{2,14},{3,15},{4,0},{5,1},{6,2},{7,3},{8,4},{9,5},{1... | collective-permute-start | bytes 1572872 | tf_op jit(solution)/shard_map/ppermute | solution.py:331
  138.8 12.4 %collective-permute-start.23 = (bf16[2,4,256,128]{3,2,1,0:T(8,128)(2,1)}, bf16[2,4,256,128]{3,2,1,0:T(8,128)(2,1)}, u32[]{:S(2)}, u32[]{:S(2)}) collective-permute-start(bf16[2,4,256,128]{3,2,1,0:T(8,128)(2,1)} %add_convert_fusion.3), channel_id=1, source_target_pairs={{0,12},{1,13},{2,14},{3,15},{4,0},{5,1},{6,2},{7,3},{8,4},{9,5},{1... | collective-permute-start | bytes 1572872 | tf_op jit(solution)/shard_map/ppermute | solution.py:331
  140.8 1.0 copy-start.12
  140.8 1.1 copy-start.13
  141.8 11.5 %collective-permute-start.31 = (bf16[2,4,256,128]{3,2,1,0:T(8,128)(2,1)}, bf16[2,4,256,128]{3,2,1,0:T(8,128)(2,1)S(1)}, u32[]{:S(2)}, u32[]{:S(2)}) collective-permute-start(bf16[2,4,256,128]{3,2,1,0:T(8,128)(2,1)} %add_convert_fusion), channel_id=1, source_target_pairs={{0,4},{1,5},{2,6},{3,7},{4,8},{5,9},{6,10},{7,11},{8,12},{9,13},{1... | collective-permute-start | bytes 1572872 | tf_op jit(solution)/shard_map/ppermute | solution.py:331
  142.9 15.1 %all-to-all-start.2 = ((bf16[4,128,768]{2,1,0:T(8,128)(2,1)}), bf16[4,128,768]{2,1,0:T(8,128)(2,1)S(1)}, u32[]{:S(2)}, u32[]{:S(2)}) async-start(bf16[4,128,768]{2,1,0:T(8,128)(2,1)} %pad_maximum_fusion.1), calls=%async_computation.2 | async-start | bytes 1572864 | tf_op jit(solution)/shard_map/all_to_all | solution.py:373
  146.4 6.8 %copy-start.1 = (bf16[2,4,256,128]{3,2,1,0:T(8,128)(2,1)S(1)}, bf16[2,4,256,128]{3,2,1,0:T(8,128)(2,1)}, u32[]{:S(2)}) copy-start(bf16[2,4,256,128]{3,2,1,0:T(8,128)(2,1)} %get-tuple-element.32) | copy-start | bytes 1572868
  153.2 6.7 %collective-permute-start.24 = (bf16[4,256,128]{2,1,0:T(8,128)(2,1)}, bf16[4,256,128]{2,1,0:T(8,128)(2,1)}, u32[]{:S(2)}, u32[]{:S(2)}) collective-permute-start(bf16[4,256,128]{2,1,0:T(8,128)(2,1)} %fusion.5), channel_id=1, source_target_pairs={{0,3},{1,0},{2,1},{3,2},{4,7},{5,4},{6,5},{7,6},{8,11},{9,8},{10,9... | collective-permute-start | bytes 786440 | tf_op jit(solution)/shard_map/ppermute | solution.py:331
  154.2 7.8 %collective-permute-start.32 = (bf16[4,256,128]{2,1,0:T(8,128)(2,1)}, bf16[4,256,128]{2,1,0:T(8,128)(2,1)S(1)}, u32[]{:S(2)}, u32[]{:S(2)}) collective-permute-start(bf16[4,256,128]{2,1,0:T(8,128)(2,1)} %get-tuple-element.44), channel_id=1, source_target_pairs={{0,1},{1,2},{2,3},{3,0},{4,5},{5,6},{6,7},{7,4},{8,9},{9,10},{10,1... | collective-permute-start | bytes 786440 | tf_op jit(solution)/shard_map/ppermute | solution.py:331
  156.3 9.1 %copy-start.7 = (bf16[2,4,256,128]{3,2,1,0:T(8,128)(2,1)S(1)}, bf16[2,4,256,128]{3,2,1,0:T(8,128)(2,1)}, u32[]{:S(2)}) copy-start(bf16[2,4,256,128]{3,2,1,0:T(8,128)(2,1)} %get-tuple-element.24) | copy-start | bytes 1572868
  156.3 9.1 %collective-permute-start.33 = (bf16[4,256,128]{2,1,0:T(8,128)(2,1)S(1)}, bf16[4,256,128]{2,1,0:T(8,128)(2,1)S(1)}, u32[]{:S(2)}, u32[]{:S(2)}) collective-permute-start(bf16[4,256,128]{2,1,0:T(8,128)(2,1)S(1)} %get-tuple-element.45), channel_id=1, source_target_pairs={{0,2},{1,3},{2,0},{3,1},{4,6},{5,7},{6,4},{7,5},{8,10},{9,11},{10,... | collective-permute-start | bytes 786440 | tf_op jit(solution)/shard_map/ppermute | solution.py:331
  167.5 10.1 %all-to-all-start.3 = ((bf16[4,256,128]{2,1,0:T(8,128)(2,1)}), bf16[4,256,128]{2,1,0:T(8,128)(2,1)S(1)}, u32[]{:S(2)}, u32[]{:S(2)}) async-start(bf16[4,256,128]{2,1,0:T(8,128)(2,1)} %fusion.2), calls=%async_computation.3 | async-start | bytes 524288 | tf_op jit(solution)/shard_map/all_to_all | solution.py:373

commit v5 on v4

--- a/solution.py
+++ b/solution.py
@@ -176,9 +176,10 @@
             def _(i):
                 body(i, False)
 
-            @pl.loop(own, total)
-            def _(i):
-                body(i, True)
+            @pl.loop(0, lax.div(total - own, 2))
+            def _(n):
+                body(own + 2 * n, True)
+                body(own + 2 * n + 1, True)
 
         def sweep(body):
             body(own - 1, True, False)
@@ -187,9 +188,10 @@
             def _(i):
                 body(i, False, False)
 
-            @pl.loop(own, total)
-            def _(i):
-                body(i, False, True)
+            @pl.loop(0, lax.div(total - own, 2))
+            def _(n):
+                body(own + 2 * n, False, True)
+                body(own + 2 * n + 1, False, True)
 
         @pl.when(small)
         def _():

time: 181 us -> 175 us (0.967)
  Pallas kernels: 40.7 us -> 36.4 us
    pallas_call x1, Pallas kernels: 40.7 us -> 36.4 us  [attend(): pl.pallas_call(functools.partial(attend_kernel, nseg, nblk, side), out_sh...]
  transfers between devices with their start and end apart: 37 -> 37, of which waited for: 15 -> 15; matrix products, arithmetic and copies ran while one was open for 6% -> 7% of each run, Pallas kernels for 0% -> 0%
where the time goes in v5:
time: 175 us; the launch traced here: 173 us
  starting transfers between devices  57.9 us (33%)
  waiting for transfers between devices  48.5 us (28%)
  Pallas kernels  36.4 us (21%)
  other arithmetic  13.3 us (8%)
  blocking collectives  11.1 us (6%)
  local copies, waits for them, and re-layouts  4.93 us (3%)
    ppermute x18, starting transfers between devices, hop(): return lax.ppermute(x, BOTH_AXES, perm)  39.4 us
    pallas_call x1, Pallas kernels, attend(): pl.pallas_call(functools.partial(attend_kernel, nseg, nblk, side), out_sh...  36.4 us
    ppermute x18, waiting for transfers between devices, hop(): return lax.ppermute(x, BOTH_AXES, perm)  29.3 us
    all_to_all x3, waiting for transfers between devices, spread(): return lax.all_to_all(x, 'cand', 0, 0, axis_index_groups=same_core)  16.7 us
    all_to_all x1, blocking collectives, spread(): return lax.all_to_all(x, 'cand', 0, 0, axis_index_groups=same_core)  11.1 us
    all_to_all x3, starting transfers between devices, spread(): return lax.all_to_all(x, 'cand', 0, 0, axis_index_groups=same_core)  10.4 us
    ppermute x8, starting transfers between devices, per_device(): came = [lax.ppermute(x, 'cand', partner) for x in oth]  6.6 us
    convert_element_type x7, other arithmetic, add(): functools.reduce(jnp.add, [x.astype(jnp.float32) for x in xs])  5.74 us
  transfers between devices with their start and end apart: 37, of which 15 were waited for; matrix products, arithmetic and copies ran while one was open for 7% of the time, Pallas kernels for 0%

profile of v5, /device:TPU:0, one launch (start us, length us, event | category | flops | bytes accessed | tf_op | source)
XLA Modules:
  0.0 173.1 jit_solution(9510005540772351053)
XLA Ops:
  0.6 0.8 fusion.19
  1.5 0.8 fusion.20
  2.4 11.1 %all_to_all.20 = bf16[4,128,256]{2,1,0:T(8,128)(2,1)S(1)} all-to-all(bf16[4,128,256]{2,1,0:T(8,128)(2,1)S(1)} %pad_maximum_fusion.4), channel_id=1, replica_groups={{0,32,64,96},{16,48,80,112},{1,33,65,97},{17,49,81,113},{2,34,66,98},{1..., dimensions={0} | all-to-all | bytes 524288 | tf_op jit(solution)/shard_map/all_to_all | solution.py:375
  13.4 1.9 %collective-permute-start = (bf16[4,128,256]{2,1,0:T(8,128)(2,1)S(1)}, bf16[4,128,256]{2,1,0:T(8,128)(2,1)S(1)}, u32[]{:S(2)}, u32[]{:S(2)}) collective-permute-start(bf16[4,128,256]{2,1,0:T(8,128)(2,1)S(1)} %all_to_all.20), channel_id=1, source_target_pairs={{0,1},{1,2},{2,3},{3,0},{4,5},{5,6},{6,7},{7,4},{8,9},{9,10},{10,1... | collective-permute-start | bytes 786440 | tf_op jit(solution)/shard_map/ppermute | solution.py:333
  15.4 2.1 %collective-permute-start.2 = (bf16[4,128,256]{2,1,0:T(8,128)(2,1)S(1)}, bf16[4,128,256]{2,1,0:T(8,128)(2,1)S(1)}, u32[]{:S(2)}, u32[]{:S(2)}) collective-permute-start(bf16[4,128,256]{2,1,0:T(8,128)(2,1)S(1)} %all_to_all.20), channel_id=1, source_target_pairs={{0,3},{1,0},{2,1},{3,2},{4,7},{5,4},{6,5},{7,6},{8,11},{9,8},{10,9... | collective-permute-start | bytes 786440 | tf_op jit(solution)/shard_map/ppermute | solution.py:333
  17.5 1.9 %collective-permute-start.1 = (bf16[4,128,256]{2,1,0:T(8,128)(2,1)S(1)}, bf16[4,128,256]{2,1,0:T(8,128)(2,1)S(1)}, u32[]{:S(2)}, u32[]{:S(2)}) collective-permute-start(bf16[4,128,256]{2,1,0:T(8,128)(2,1)S(1)} %all_to_all.20), channel_id=1, source_target_pairs={{0,2},{1,3},{2,0},{3,1},{4,6},{5,7},{6,4},{7,5},{8,10},{9,11},{10,... | collective-permute-start | bytes 786440 | tf_op jit(solution)/shard_map/ppermute | solution.py:333
  19.3 2.5 %collective-permute-done = bf16[4,128,256]{2,1,0:T(8,128)(2,1)S(1)} collective-permute-done((bf16[4,128,256]{2,1,0:T(8,128)(2,1)S(1)}, bf16[4,128,256]{2,1,0:T(8,128)(2,1)S(1)}, u32[]{:S(2)}, u32[]{:S(2)}) %collective-permute-start) | collective-permute-done | bytes 262176 | tf_op jit(solution)/shard_map/ppermute | solution.py:333
  22.0 2.8 %collective-permute-start.5 = (bf16[2,4,128,256]{3,2,1,0:T(8,128)(2,1)S(1)}, bf16[2,4,128,256]{3,2,1,0:T(8,128)(2,1)S(1)}, u32[]{:S(2)}, u32[]{:S(2)}) collective-permute-start(bf16[2,4,128,256]{3,2,1,0:T(8,128)(2,1)S(1)} %pad_maximum_fusion.2.refs_0_), channel_id=1, source_target_pairs={{0,12},{1,13},{2,14},{3,15},{4,0},{5,1},{6,2},{7,3},{8,4},{9,5},{1... | collective-permute-start | bytes 1572872 | tf_op jit(solution)/shard_map/ppermute | solution.py:333
  24.8 1.3 collective-permute-done.1
  26.2 2.8 %collective-permute-start.6 = (bf16[2,4,128,256]{3,2,1,0:T(8,128)(2,1)S(1)}, bf16[2,4,128,256]{3,2,1,0:T(8,128)(2,1)}, u32[]{:S(2)}, u32[]{:S(2)}) collective-permute-start(bf16[2,4,128,256]{3,2,1,0:T(8,128)(2,1)S(1)} %pad_maximum_fusion.3.refs_1_), channel_id=1, source_target_pairs={{0,12},{1,13},{2,14},{3,15},{4,0},{5,1},{6,2},{7,3},{8,4},{9,5},{1... | collective-permute-start | bytes 1572872 | tf_op jit(solution)/shard_map/ppermute | solution.py:333
  29.1 2.4 %collective-permute-done.5.refs_4_ = bf16[2,4,128,256]{3,2,1,0:T(8,128)(2,1)S(1)} collective-permute-done((bf16[2,4,128,256]{3,2,1,0:T(8,128)(2,1)S(1)}, bf16[2,4,128,256]{3,2,1,0:T(8,128)(2,1)S(1)}, u32[]{:S(2)}, u32[]{:S(2)}) %collective-permute-start.5) | collective-permute-done | bytes 524320 | tf_op jit(solution)/shard_map/ppermute | solution.py:333
  31.5 0.3 collective-permute-start.13
  31.8 3.5 %collective-permute-done.3.refs_2_ = bf16[2,4,128,256]{3,2,1,0:T(8,128)(2,1)} collective-permute-done((bf16[2,4,128,256]{3,2,1,0:T(8,128)(2,1)S(1)}, bf16[2,4,128,256]{3,2,1,0:T(8,128)(2,1)}, u32[]{:S(2)}, u32[]{:S(2)}) %collective-permute-start.3) | collective-permute-done | bytes 524320 | tf_op jit(solution)/shard_map/ppermute | solution.py:333
  35.3 1.8 %collective-permute-done.6.refs_5_ = bf16[2,4,128,256]{3,2,1,0:T(8,128)(2,1)} collective-permute-done((bf16[2,4,128,256]{3,2,1,0:T(8,128)(2,1)S(1)}, bf16[2,4,128,256]{3,2,1,0:T(8,128)(2,1)}, u32[]{:S(2)}, u32[]{:S(2)}) %collective-permute-start.6) | collective-permute-done | bytes 524320 | tf_op jit(solution)/shard_map/ppermute | solution.py:333
  37.1 3.8 %collective-permute-start.8 = (bf16[2,4,128,256]{3,2,1,0:T(8,128)(2,1)}, bf16[2,4,128,256]{3,2,1,0:T(8,128)(2,1)}, u32[]{:S(2)}, u32[]{:S(2)}) collective-permute-start(bf16[2,4,128,256]{3,2,1,0:T(8,128)(2,1)} %collective-permute-done.6.refs_5_), channel_id=1, source_target_pairs={{0,12},{1,13},{2,14},{3,15},{4,0},{5,1},{6,2},{7,3},{8,4},{9,5},{1... | collective-permute-start | bytes 1572872 | tf_op jit(solution)/shard_map/ppermute | solution.py:333
  41.0 0.7 convert_bitcast_fusion
  41.8 1.1 pad_maximum_fusion
  42.9 3.5 %all-to-all-start = ((bf16[4,144,768]{2,1,0:T(8,128)(2,1)}), bf16[4,144,768]{2,1,0:T(8,128)(2,1)S(1)}, u32[]{:S(2)}, u32[]{:S(2)}) async-start(bf16[4,144,768]{2,1,0:T(8,128)(2,1)} %pad_maximum_fusion), calls=%async_computation | async-start | bytes 1769472 | tf_op jit(solution)/shard_map/all_to_all | solution.py:375
  46.5 0.5 collective-permute-start.14
  47.0 0.1 collective-permute-start.12
  47.1 0.4 collective-permute-start.15
  47.6 0.4 collective-permute-done.8.refs_7_
  47.9 10.8 %all-to-all-done.both = bf16[4,144,768]{2,1,0:T(8,128)(2,1)S(1)} async-done(((bf16[4,144,768]{2,1,0:T(8,128)(2,1)}), bf16[4,144,768]{2,1,0:T(8,128)(2,1)S(1)}, u32[]{:S(2)}, u32[]{:S(2)}) %all-to-all-start) | async-done | bytes 884768 | tf_op jit(solution)/shard_map/all_to_all | solution.py:375
  58.8 0.9 copy-done
  59.7 0.2 copy-done.17
  59.9 0.3 copy-done.18
  60.2 36.4 %shard_map.102 = (bf16[4,128,384]{2,1,0:T(8,128)(2,1)}, bf16[4,128,384]{2,1,0:T(8,128)(2,1)}, bf16[2,4,256,128]{3,2,1,0:T(8,128)(2,1)}, bf16[2,4,256,128]{3,2,1,...) custom-call(s32[8]{0:T(128)} %parent.1, s32[8]{0:T(128)} %depth.1, ...), custom_call_target="tpu_custom_call" | custom-call | flops 14495514624 | bytes 16777216 | tf_op jit(solution)/shard_map/pallas_call | solution.py:281
  96.6 4.9 %collective-permute-start.18 = (bf16[2,4,256,128]{3,2,1,0:T(8,128)(2,1)}, bf16[2,4,256,128]{3,2,1,0:T(8,128)(2,1)S(1)}, u32[]{:S(2)}, u32[]{:S(2)}) collective-permute-start(bf16[2,4,256,128]{3,2,1,0:T(8,128)(2,1)} %get-tuple-element.27), channel_id=1, source_target_pairs={{0,16},{16,0},{32,48},{48,32},{64,80},{80,64},{96,112},{112,96},{1... | collective-permute-start | bytes 1572872 | tf_op jit(solution)/shard_map/ppermute | solution.py:414
  101.5 0.1 collective-permute-start.21
  101.6 0.4 collective-permute-start.17
  102.0 0.1 collective-permute-start.20
  102.1 0.4 collective-permute-start.26
  102.5 0.7 collective-permute-done.18
  103.2 0.4 collective-permute-start.29
  103.6 1.2 add_convert_fusion.5
  104.8 0.2 collective-permute-start.28
  105.0 0.1 add_convert_fusion.4
  105.2 1.8 %collective-permute-done.29 = bf16[2,4,256,128]{3,2,1,0:T(8,128)(2,1)S(1)} collective-permute-done((bf16[2,4,256,128]{3,2,1,0:T(8,128)(2,1)}, bf16[2,4,256,128]{3,2,1,0:T(8,128)(2,1)S(1)}, u32[]{:S(2)}, u32[]{:S(2)}) %collective-permute-start.29) | collective-permute-done | bytes 524320 | tf_op jit(solution)/shard_map/ppermute | solution.py:414
  107.0 14.4 %collective-permute-start.22 = (bf16[2,4,256,128]{3,2,1,0:T(8,128)(2,1)S(1)}, bf16[2,4,256,128]{3,2,1,0:T(8,128)(2,1)S(1)}, u32[]{:S(2)}, u32[]{:S(2)}) collective-permute-start(bf16[2,4,256,128]{3,2,1,0:T(8,128)(2,1)S(1)} %add_convert_fusion.4), channel_id=1, source_target_pairs={{0,12},{1,13},{2,14},{3,15},{4,0},{5,1},{6,2},{7,3},{8,4},{9,5},{1... | collective-permute-start | bytes 1572872 | tf_op jit(solution)/shard_map/ppermute | solution.py:333
  121.4 0.1 add_convert_fusion.1
  121.6 0.1 add_convert_fusion.2
  121.9 6.2 %collective-permute-done.22 = bf16[2,4,256,128]{3,2,1,0:T(8,128)(2,1)S(1)} collective-permute-done((bf16[2,4,256,128]{3,2,1,0:T(8,128)(2,1)S(1)}, bf16[2,4,256,128]{3,2,1,0:T(8,128)(2,1)S(1)}, u32[]{:S(2)}, u32[]{:S(2)}) %collective-permute-start.22) | collective-permute-done | bytes 524320 | tf_op jit(solution)/shard_map/ppermute | solution.py:333
  128.1 1.0 add_convert_fusion.3
  129.1 3.7 %collective-permute-start.27 = (bf16[2,4,256,128]{3,2,1,0:T(8,128)(2,1)S(1)}, bf16[2,4,256,128]{3,2,1,0:T(8,128)(2,1)S(1)}, u32[]{:S(2)}, u32[]{:S(2)}) collective-permute-start(bf16[2,4,256,128]{3,2,1,0:T(8,128)(2,1)S(1)} %add_convert_fusion.2), channel_id=1, source_target_pairs={{0,12},{1,13},{2,14},{3,15},{4,0},{5,1},{6,2},{7,3},{8,4},{9,5},{1... | collective-permute-start | bytes 1572872 | tf_op jit(solution)/shard_map/ppermute | solution.py:333
  132.8 2.0 %collective-permute-start.23 = (bf16[2,4,256,128]{3,2,1,0:T(8,128)(2,1)}, bf16[2,4,256,128]{3,2,1,0:T(8,128)(2,1)}, u32[]{:S(2)}, u32[]{:S(2)}) collective-permute-start(bf16[2,4,256,128]{3,2,1,0:T(8,128)(2,1)} %add_convert_fusion.3), channel_id=1, source_target_pairs={{0,12},{1,13},{2,14},{3,15},{4,0},{5,1},{6,2},{7,3},{8,4},{9,5},{1... | collective-permute-start | bytes 1572872 | tf_op jit(solution)/shard_map/ppermute | solution.py:333
  134.8 1.0 add_convert_fusion
  135.8 0.1 copy-done.13
  136.0 1.0 pad_maximum_fusion.1
  136.9 3.5 %all-to-all-start.2 = ((bf16[4,128,768]{2,1,0:T(8,128)(2,1)}), bf16[4,128,768]{2,1,0:T(8,128)(2,1)S(1)}, u32[]{:S(2)}, u32[]{:S(2)}) async-start(bf16[4,128,768]{2,1,0:T(8,128)(2,1)} %pad_maximum_fusion.1), calls=%async_computation.2 | async-start | bytes 1572864 | tf_op jit(solution)/shard_map/all_to_all | solution.py:375
  140.5 4.8 %collective-permute-done.23 = bf16[2,4,256,128]{3,2,1,0:T(8,128)(2,1)} collective-permute-done((bf16[2,4,256,128]{3,2,1,0:T(8,128)(2,1)}, bf16[2,4,256,128]{3,2,1,0:T(8,128)(2,1)}, u32[]{:S(2)}, u32[]{:S(2)}) %collective-permute-start.23) | collective-permute-done | bytes 524320 | tf_op jit(solution)/shard_map/ppermute | solution.py:333
  145.2 2.0 %fusion.5 = bf16[4,256,128]{2,1,0:T(8,128)(2,1)} fusion(bf16[2,4,256,128]{3,2,1,0:T(8,128)(2,1)} %collective-permute-done.23, bf16[2,4,256,128]{3,2,1,0:T(8,128)(2,1)} %collective-permute-done.19, bf16[2,4,256,128]{3,2,1,0:T(8,128)(2,1)} %collective-permute-done.17, bf16[2,4,256,128]{3,2,1,0:T(8,128)(2,1)} %get-tuple-element.24), kind=kLoop, calls=%fused_computation.23 | loop fusion | flops 1048576 | bytes 1310720 | tf_op jit(solution)/shard_map/add | solution.py:329
  147.3 1.0 fusion.6
  148.3 2.0 %collective-permute-start.32 = (bf16[4,256,128]{2,1,0:T(8,128)(2,1)}, bf16[4,256,128]{2,1,0:T(8,128)(2,1)S(1)}, u32[]{:S(2)}, u32[]{:S(2)}) collective-permute-start(bf16[4,256,128]{2,1,0:T(8,128)(2,1)} %get-tuple-element.44), channel_id=1, source_target_pairs={{0,1},{1,2},{2,3},{3,0},{4,5},{5,6},{6,7},{7,4},{8,9},{9,10},{10,1... | collective-permute-start | bytes 786440 | tf_op jit(solution)/shard_map/ppermute | solution.py:333
  150.3 1.7 collective-permute-start.33
  152.1 0.8 maximum_bitcast_fusion.1
  152.9 1.1 collective-permute-done.24
  153.9 2.1 %collective-permute-done.32 = bf16[4,256,128]{2,1,0:T(8,128)(2,1)S(1)} collective-permute-done((bf16[4,256,128]{2,1,0:T(8,128)(2,1)}, bf16[4,256,128]{2,1,0:T(8,128)(2,1)S(1)}, u32[]{:S(2)}, u32[]{:S(2)}) %collective-permute-start.32) | collective-permute-done | bytes 262176 | tf_op jit(solution)/shard_map/ppermute | solution.py:333
  156.1 3.3 %collective-permute-done.33 = bf16[4,256,128]{2,1,0:T(8,128)(2,1)S(1)} collective-permute-done((bf16[4,256,128]{2,1,0:T(8,128)(2,1)S(1)}, bf16[4,256,128]{2,1,0:T(8,128)(2,1)S(1)}, u32[]{:S(2)}, u32[]{:S(2)}) %collective-permute-start.33) | collective-permute-done | bytes 262176 | tf_op jit(solution)/shard_map/ppermute | solution.py:333
  159.4 2.1 %fusion.2 = bf16[4,256,128]{2,1,0:T(8,128)(2,1)} fusion(bf16[4,256,128]{2,1,0:T(8,128)(2,1)S(1)} %collective-permute-done.33, bf16[4,256,128]{2,1,0:T(8,128)(2,1)S(1)} %collective-permute-done.32, bf16[4,256,128]{2,1,0:T(8,128)(2,1)} %collective-permute-done.24, bf16[2,4,256,128]{3,2,1,0:T(8,128)(2,1)} %collective-permute-done.23, ...), kind=kLoop, calls=%fused_computation.13 | loop fusion | flops 2097152 | bytes 2097152 | tf_op jit(solution)/shard_map/convert_element_type | solution.py:329
  161.5 3.4 %all-to-all-start.3 = ((bf16[4,256,128]{2,1,0:T(8,128)(2,1)}), bf16[4,256,128]{2,1,0:T(8,128)(2,1)S(1)}, u32[]{:S(2)}, u32[]{:S(2)}) async-start(bf16[4,256,128]{2,1,0:T(8,128)(2,1)} %fusion.2), calls=%async_computation.3 | async-start | bytes 524288 | tf_op jit(solution)/shard_map/all_to_all | solution.py:375
  164.9 0.8 maximum_bitcast_fusion
  165.7 5.9 %all-to-all-done.3 = bf16[4,256,128]{2,1,0:T(8,128)(2,1)S(1)} async-done(((bf16[4,256,128]{2,1,0:T(8,128)(2,1)}), bf16[4,256,128]{2,1,0:T(8,128)(2,1)S(1)}, u32[]{:S(2)}, u32[]{:S(2)}) %all-to-all-start.3) | async-done | bytes 262176 | tf_op jit(solution)/shard_map/all_to_all | solution.py:375
  171.6 0.8 copy.12
  172.4 0.8 copy.11
  (77 shorter events, 1.0 us)
Async XLA Ops:
  13.4 8.4 %collective-permute-start = (bf16[4,128,256]{2,1,0:T(8,128)(2,1)S(1)}, bf16[4,128,256]{2,1,0:T(8,128)(2,1)S(1)}, u32[]{:S(2)}, u32[]{:S(2)}) collective-permute-start(bf16[4,128,256]{2,1,0:T(8,128)(2,1)S(1)} %all_to_all.20), channel_id=1, source_target_pairs={{0,1},{1,2},{2,3},{3,0},{4,5},{5,6},{6,7},{7,4},{8,9},{9,10},{10,1... | collective-permute-start | bytes 786440 | tf_op jit(solution)/shard_map/ppermute | solution.py:333
  15.4 9.5 %collective-permute-start.2 = (bf16[4,128,256]{2,1,0:T(8,128)(2,1)S(1)}, bf16[4,128,256]{2,1,0:T(8,128)(2,1)S(1)}, u32[]{:S(2)}, u32[]{:S(2)}) collective-permute-start(bf16[4,128,256]{2,1,0:T(8,128)(2,1)S(1)} %all_to_all.20), channel_id=1, source_target_pairs={{0,3},{1,0},{2,1},{3,2},{4,7},{5,4},{6,5},{7,6},{8,11},{9,8},{10,9... | collective-permute-start | bytes 786440 | tf_op jit(solution)/shard_map/ppermute | solution.py:333
  17.5 8.6 %collective-permute-start.1 = (bf16[4,128,256]{2,1,0:T(8,128)(2,1)S(1)}, bf16[4,128,256]{2,1,0:T(8,128)(2,1)S(1)}, u32[]{:S(2)}, u32[]{:S(2)}) collective-permute-start(bf16[4,128,256]{2,1,0:T(8,128)(2,1)S(1)} %all_to_all.20), channel_id=1, source_target_pairs={{0,2},{1,3},{2,0},{3,1},{4,6},{5,7},{6,4},{7,5},{8,10},{9,11},{10,... | collective-permute-start | bytes 786440 | tf_op jit(solution)/shard_map/ppermute | solution.py:333
  21.8 19.1 %copy-start.10 = (bf16[1,128,1536]{2,1,0:T(8,128)(2,1)S(1)}, bf16[1,128,1536]{2,1,0:T(8,128)(2,1)}, u32[]{:S(2)}) copy-start(bf16[1,128,1536]{2,1,0:T(8,128)(2,1)} %param.7) | copy-start | bytes 1179652
  21.8 19.1 %copy-start.11 = (bf16[1,128,1536]{2,1,0:T(8,128)(2,1)S(1)}, bf16[1,128,1536]{2,1,0:T(8,128)(2,1)}, u32[]{:S(2)}) copy-start(bf16[1,128,1536]{2,1,0:T(8,128)(2,1)} %param.10) | copy-start | bytes 1179652
  21.9 19.1 %copy-start.5 = (bf16[2,4,128,256]{3,2,1,0:T(8,128)(2,1)}, bf16[2,4,128,256]{3,2,1,0:T(8,128)(2,1)S(1)}, u32[]{:S(2)}) copy-start(bf16[2,4,128,256]{3,2,1,0:T(8,128)(2,1)S(1)} %pad_maximum_fusion.2.refs_0_) | copy-start | bytes 1572868
  21.9 7.1 %collective-permute-start.9 = (bf16[2,4,128,256]{3,2,1,0:T(8,128)(2,1)S(1)}, bf16[2,4,128,256]{3,2,1,0:T(8,128)(2,1)S(1)}, u32[]{:S(2)}, u32[]{:S(2)}) collective-permute-start(bf16[2,4,128,256]{3,2,1,0:T(8,128)(2,1)S(1)} %pad_maximum_fusion.2.refs_0_), channel_id=1, source_target_pairs={{0,16},{16,0},{32,48},{48,32},{64,80},{80,64},{96,112},{112,96},{1... | collective-permute-start | bytes 1572872 | tf_op jit(solution)/shard_map/ppermute | solution.py:391
  22.0 9.5 %collective-permute-start.5 = (bf16[2,4,128,256]{3,2,1,0:T(8,128)(2,1)S(1)}, bf16[2,4,128,256]{3,2,1,0:T(8,128)(2,1)S(1)}, u32[]{:S(2)}, u32[]{:S(2)}) collective-permute-start(bf16[2,4,128,256]{3,2,1,0:T(8,128)(2,1)S(1)} %pad_maximum_fusion.2.refs_0_), channel_id=1, source_target_pairs={{0,12},{1,13},{2,14},{3,15},{4,0},{5,1},{6,2},{7,3},{8,4},{9,5},{1... | collective-permute-start | bytes 1572872 | tf_op jit(solution)/shard_map/ppermute | solution.py:333
  24.8 10.5 %collective-permute-start.3 = (bf16[2,4,128,256]{3,2,1,0:T(8,128)(2,1)S(1)}, bf16[2,4,128,256]{3,2,1,0:T(8,128)(2,1)}, u32[]{:S(2)}, u32[]{:S(2)}) collective-permute-start(bf16[2,4,128,256]{3,2,1,0:T(8,128)(2,1)S(1)} %pad_maximum_fusion.2.refs_0_), channel_id=1, source_target_pairs={{0,4},{1,5},{2,6},{3,7},{4,8},{5,9},{6,10},{7,11},{8,12},{9,13},{1... | collective-permute-start | bytes 1572872 | tf_op jit(solution)/shard_map/ppermute | solution.py:333
  26.1 15.7 %copy-start.6 = (bf16[2,4,128,256]{3,2,1,0:T(8,128)(2,1)}, bf16[2,4,128,256]{3,2,1,0:T(8,128)(2,1)S(1)}, u32[]{:S(2)}) copy-start(bf16[2,4,128,256]{3,2,1,0:T(8,128)(2,1)S(1)} %pad_maximum_fusion.3.refs_1_) | copy-start | bytes 1572868
  26.2 11.0 %collective-permute-start.6 = (bf16[2,4,128,256]{3,2,1,0:T(8,128)(2,1)S(1)}, bf16[2,4,128,256]{3,2,1,0:T(8,128)(2,1)}, u32[]{:S(2)}, u32[]{:S(2)}) collective-permute-start(bf16[2,4,128,256]{3,2,1,0:T(8,128)(2,1)S(1)} %pad_maximum_fusion.3.refs_1_), channel_id=1, source_target_pairs={{0,12},{1,13},{2,14},{3,15},{4,0},{5,1},{6,2},{7,3},{8,4},{9,5},{1... | collective-permute-start | bytes 1572872 | tf_op jit(solution)/shard_map/ppermute | solution.py:333
  29.0 17.5 %collective-permute-start.10 = (bf16[2,4,128,256]{3,2,1,0:T(8,128)(2,1)S(1)}, bf16[2,4,128,256]{3,2,1,0:T(8,128)(2,1)}, u32[]{:S(2)}, u32[]{:S(2)}) collective-permute-start(bf16[2,4,128,256]{3,2,1,0:T(8,128)(2,1)S(1)} %pad_maximum_fusion.3.refs_1_), channel_id=1, source_target_pairs={{0,16},{16,0},{32,48},{48,32},{64,80},{80,64},{96,112},{112,96},{1... | collective-permute-start | bytes 1572872 | tf_op jit(solution)/shard_map/ppermute | solution.py:391
  29.0 12.8 %copy-start.14 = (bf16[2,4,128,256]{3,2,1,0:T(8,128)(2,1)}, bf16[2,4,128,256]{3,2,1,0:T(8,128)(2,1)S(1)}, u32[]{:S(2)}) copy-start(bf16[2,4,128,256]{3,2,1,0:T(8,128)(2,1)S(1)} %collective-permute-done.9.refs_8_) | copy-start | bytes 1572868
  29.0 17.5 %collective-permute-start.4 = (bf16[2,4,128,256]{3,2,1,0:T(8,128)(2,1)S(1)}, bf16[2,4,128,256]{3,2,1,0:T(8,128)(2,1)}, u32[]{:S(2)}, u32[]{:S(2)}) collective-permute-start(bf16[2,4,128,256]{3,2,1,0:T(8,128)(2,1)S(1)} %pad_maximum_fusion.3.refs_1_), channel_id=1, source_target_pairs={{0,4},{1,5},{2,6},{3,7},{4,8},{5,9},{6,10},{7,11},{8,12},{9,13},{1... | collective-permute-start | bytes 1572872 | tf_op jit(solution)/shard_map/ppermute | solution.py:333
  31.5 10.3 %copy-start.15 = (bf16[2,4,128,256]{3,2,1,0:T(8,128)(2,1)}, bf16[2,4,128,256]{3,2,1,0:T(8,128)(2,1)S(1)}, u32[]{:S(2)}) copy-start(bf16[2,4,128,256]{3,2,1,0:T(8,128)(2,1)S(1)} %collective-permute-done.5.refs_4_) | copy-start | bytes 1572868
  31.5 15.5 %collective-permute-start.13 = (bf16[2,4,128,256]{3,2,1,0:T(8,128)(2,1)S(1)}, bf16[2,4,128,256]{3,2,1,0:T(8,128)(2,1)}, u32[]{:S(2)}, u32[]{:S(2)}) collective-permute-start(bf16[2,4,128,256]{3,2,1,0:T(8,128)(2,1)S(1)} %collective-permute-done.5.refs_4_), channel_id=1, source_target_pairs={{0,16},{16,0},{32,48},{48,32},{64,80},{80,64},{96,112},{112,96},{1... | collective-permute-start | bytes 1572872 | tf_op jit(solution)/shard_map/ppermute | solution.py:391
  35.3 11.8 %collective-permute-start.7 = (bf16[2,4,128,256]{3,2,1,0:T(8,128)(2,1)}, bf16[2,4,128,256]{3,2,1,0:T(8,128)(2,1)}, u32[]{:S(2)}, u32[]{:S(2)}) collective-permute-start(bf16[2,4,128,256]{3,2,1,0:T(8,128)(2,1)} %collective-permute-done.3.refs_2_), channel_id=1, source_target_pairs={{0,4},{1,5},{2,6},{3,7},{4,8},{5,9},{6,10},{7,11},{8,12},{9,13},{1... | collective-permute-start | bytes 1572872 | tf_op jit(solution)/shard_map/ppermute | solution.py:333
  37.1 10.8 %collective-permute-start.8 = (bf16[2,4,128,256]{3,2,1,0:T(8,128)(2,1)}, bf16[2,4,128,256]{3,2,1,0:T(8,128)(2,1)}, u32[]{:S(2)}, u32[]{:S(2)}) collective-permute-start(bf16[2,4,128,256]{3,2,1,0:T(8,128)(2,1)} %collective-permute-done.6.refs_5_), channel_id=1, source_target_pairs={{0,12},{1,13},{2,14},{3,15},{4,0},{5,1},{6,2},{7,3},{8,4},{9,5},{1... | collective-permute-start | bytes 1572872 | tf_op jit(solution)/shard_map/ppermute | solution.py:333
  42.9 15.8 %all-to-all-start = ((bf16[4,144,768]{2,1,0:T(8,128)(2,1)}), bf16[4,144,768]{2,1,0:T(8,128)(2,1)S(1)}, u32[]{:S(2)}, u32[]{:S(2)}) async-start(bf16[4,144,768]{2,1,0:T(8,128)(2,1)} %pad_maximum_fusion), calls=%async_computation | async-start | bytes 1769472 | tf_op jit(solution)/shard_map/all_to_all | solution.py:375
  46.4 12.3 %collective-permute-start.11 = (bf16[2,4,128,256]{3,2,1,0:T(8,128)(2,1)}, bf16[2,4,128,256]{3,2,1,0:T(8,128)(2,1)S(1)}, u32[]{:S(2)}, u32[]{:S(2)}) collective-permute-start(bf16[2,4,128,256]{3,2,1,0:T(8,128)(2,1)} %collective-permute-done.3.refs_2_), channel_id=1, source_target_pairs={{0,16},{16,0},{32,48},{48,32},{64,80},{80,64},{96,112},{112,96},{1... | collective-permute-start | bytes 1572872 | tf_op jit(solution)/shard_map/ppermute | solution.py:391
  46.5 12.2 %collective-permute-start.14 = (bf16[2,4,128,256]{3,2,1,0:T(8,128)(2,1)}, bf16[2,4,128,256]{3,2,1,0:T(8,128)(2,1)}, u32[]{:S(2)}, u32[]{:S(2)}) collective-permute-start(bf16[2,4,128,256]{3,2,1,0:T(8,128)(2,1)} %collective-permute-done.6.refs_5_), channel_id=1, source_target_pairs={{0,16},{16,0},{32,48},{48,32},{64,80},{80,64},{96,112},{112,96},{1... | collective-permute-start | bytes 1572872 | tf_op jit(solution)/shard_map/ppermute | solution.py:391
  47.0 11.7 %collective-permute-start.12 = (bf16[2,4,128,256]{3,2,1,0:T(8,128)(2,1)}, bf16[2,4,128,256]{3,2,1,0:T(8,128)(2,1)S(1)}, u32[]{:S(2)}, u32[]{:S(2)}) collective-permute-start(bf16[2,4,128,256]{3,2,1,0:T(8,128)(2,1)} %collective-permute-done.4.refs_3_), channel_id=1, source_target_pairs={{0,16},{16,0},{32,48},{48,32},{64,80},{80,64},{96,112},{112,96},{1... | collective-permute-start | bytes 1572872 | tf_op jit(solution)/shard_map/ppermute | solution.py:391
  47.1 11.6 %collective-permute-start.15 = (bf16[2,4,128,256]{3,2,1,0:T(8,128)(2,1)}, bf16[2,4,128,256]{3,2,1,0:T(8,128)(2,1)}, u32[]{:S(2)}, u32[]{:S(2)}) collective-permute-start(bf16[2,4,128,256]{3,2,1,0:T(8,128)(2,1)} %collective-permute-done.7.refs_6_), channel_id=1, source_target_pairs={{0,16},{16,0},{32,48},{48,32},{64,80},{80,64},{96,112},{112,96},{1... | collective-permute-start | bytes 1572872 | tf_op jit(solution)/shard_map/ppermute | solution.py:391
  47.9 10.8 %collective-permute-start.16 = (bf16[2,4,128,256]{3,2,1,0:T(8,128)(2,1)}, bf16[2,4,128,256]{3,2,1,0:T(8,128)(2,1)}, u32[]{:S(2)}, u32[]{:S(2)}) collective-permute-start(bf16[2,4,128,256]{3,2,1,0:T(8,128)(2,1)} %collective-permute-done.8.refs_7_), channel_id=1, source_target_pairs={{0,16},{16,0},{32,48},{48,32},{64,80},{80,64},{96,112},{112,96},{1... | collective-permute-start | bytes 1572872 | tf_op jit(solution)/shard_map/ppermute | solution.py:391
  58.7 1.0 copy-start
  58.7 1.2 copy-start.17
  58.8 1.4 copy-start.18
  96.5 8.3 %copy-start.16 = (bf16[2,4,256,128]{3,2,1,0:T(8,128)(2,1)S(1)}, bf16[2,4,256,128]{3,2,1,0:T(8,128)(2,1)}, u32[]{:S(2)}) copy-start(bf16[2,4,256,128]{3,2,1,0:T(8,128)(2,1)} %get-tuple-element.37) | copy-start | bytes 1572868
  96.6 8.5 %copy-start.4 = (bf16[2,4,256,128]{3,2,1,0:T(8,128)(2,1)S(1)}, bf16[2,4,256,128]{3,2,1,0:T(8,128)(2,1)}, u32[]{:S(2)}) copy-start(bf16[2,4,256,128]{3,2,1,0:T(8,128)(2,1)} %get-tuple-element.30) | copy-start | bytes 1572868
  96.6 6.7 %collective-permute-start.18 = (bf16[2,4,256,128]{3,2,1,0:T(8,128)(2,1)}, bf16[2,4,256,128]{3,2,1,0:T(8,128)(2,1)S(1)}, u32[]{:S(2)}, u32[]{:S(2)}) collective-permute-start(bf16[2,4,256,128]{3,2,1,0:T(8,128)(2,1)} %get-tuple-element.27), channel_id=1, source_target_pairs={{0,16},{16,0},{32,48},{48,32},{64,80},{80,64},{96,112},{112,96},{1... | collective-permute-start | bytes 1572872 | tf_op jit(solution)/shard_map/ppermute | solution.py:414
  101.5 3.3 %collective-permute-start.21 = (bf16[2,4,256,128]{3,2,1,0:T(8,128)(2,1)}, bf16[2,4,256,128]{3,2,1,0:T(8,128)(2,1)S(1)}, u32[]{:S(2)}, u32[]{:S(2)}) collective-permute-start(bf16[2,4,256,128]{3,2,1,0:T(8,128)(2,1)} %get-tuple-element.31), channel_id=1, source_target_pairs={{0,16},{16,0},{32,48},{48,32},{64,80},{80,64},{96,112},{112,96},{1... | collective-permute-start | bytes 1572872 | tf_op jit(solution)/shard_map/ppermute | solution.py:414
  101.6 34.2 %collective-permute-start.17 = (bf16[2,4,256,128]{3,2,1,0:T(8,128)(2,1)}, bf16[2,4,256,128]{3,2,1,0:T(8,128)(2,1)}, u32[]{:S(2)}, u32[]{:S(2)}) collective-permute-start(bf16[2,4,256,128]{3,2,1,0:T(8,128)(2,1)} %get-tuple-element.25), channel_id=1, source_target_pairs={{0,16},{16,0},{32,48},{48,32},{64,80},{80,64},{96,112},{112,96},{1... | collective-permute-start | bytes 1572872 | tf_op jit(solution)/shard_map/ppermute | solution.py:414
  102.0 19.8 %collective-permute-start.20 = (bf16[2,4,256,128]{3,2,1,0:T(8,128)(2,1)}, bf16[2,4,256,128]{3,2,1,0:T(8,128)(2,1)S(1)}, u32[]{:S(2)}, u32[]{:S(2)}) collective-permute-start(bf16[2,4,256,128]{3,2,1,0:T(8,128)(2,1)} %get-tuple-element.29), channel_id=1, source_target_pairs={{0,16},{16,0},{32,48},{48,32},{64,80},{80,64},{96,112},{112,96},{1... | collective-permute-start | bytes 1572872 | tf_op jit(solution)/shard_map/ppermute | solution.py:414
  102.1 19.5 %collective-permute-start.26 = (bf16[2,4,256,128]{3,2,1,0:T(8,128)(2,1)}, bf16[2,4,256,128]{3,2,1,0:T(8,128)(2,1)S(1)}, u32[]{:S(2)}, u32[]{:S(2)}) collective-permute-start(bf16[2,4,256,128]{3,2,1,0:T(8,128)(2,1)} %get-tuple-element.35), channel_id=1, source_target_pairs={{0,16},{16,0},{32,48},{48,32},{64,80},{80,64},{96,112},{112,96},{1... | collective-permute-start | bytes 1572872 | tf_op jit(solution)/shard_map/ppermute | solution.py:414
  103.2 3.7 %collective-permute-start.29 = (bf16[2,4,256,128]{3,2,1,0:T(8,128)(2,1)}, bf16[2,4,256,128]{3,2,1,0:T(8,128)(2,1)S(1)}, u32[]{:S(2)}, u32[]{:S(2)}) collective-permute-start(bf16[2,4,256,128]{3,2,1,0:T(8,128)(2,1)} %get-tuple-element.39), channel_id=1, source_target_pairs={{0,16},{16,0},{32,48},{48,32},{64,80},{80,64},{96,112},{112,96},{1... | collective-permute-start | bytes 1572872 | tf_op jit(solution)/shard_map/ppermute | solution.py:414
  104.8 16.6 %copy-start.3 = (bf16[2,4,256,128]{3,2,1,0:T(8,128)(2,1)S(1)}, bf16[2,4,256,128]{3,2,1,0:T(8,128)(2,1)}, u32[]{:S(2)}) copy-start(bf16[2,4,256,128]{3,2,1,0:T(8,128)(2,1)} %get-tuple-element.38) | copy-start | bytes 1572868
  104.8 24.3 %collective-permute-start.28 = (bf16[2,4,256,128]{3,2,1,0:T(8,128)(2,1)S(1)}, bf16[2,4,256,128]{3,2,1,0:T(8,128)(2,1)S(1)}, u32[]{:S(2)}, u32[]{:S(2)}) collective-permute-start(bf16[2,4,256,128]{3,2,1,0:T(8,128)(2,1)S(1)} %copy-done.16), channel_id=1, source_target_pairs={{0,16},{16,0},{32,48},{48,32},{64,80},{80,64},{96,112},{112,96},{1... | collective-permute-start | bytes 1572872 | tf_op jit(solution)/shard_map/ppermute | solution.py:414
  105.2 16.5 %copy-start.2 = (bf16[2,4,256,128]{3,2,1,0:T(8,128)(2,1)S(1)}, bf16[2,4,256,128]{3,2,1,0:T(8,128)(2,1)}, u32[]{:S(2)}) copy-start(bf16[2,4,256,128]{3,2,1,0:T(8,128)(2,1)} %get-tuple-element.34) | copy-start | bytes 1572868
  107.0 21.1 %collective-permute-start.22 = (bf16[2,4,256,128]{3,2,1,0:T(8,128)(2,1)S(1)}, bf16[2,4,256,128]{3,2,1,0:T(8,128)(2,1)S(1)}, u32[]{:S(2)}, u32[]{:S(2)}) collective-permute-start(bf16[2,4,256,128]{3,2,1,0:T(8,128)(2,1)S(1)} %add_convert_fusion.4), channel_id=1, source_target_pairs={{0,12},{1,13},{2,14},{3,15},{4,0},{5,1},{6,2},{7,3},{8,4},{9,5},{1... | collective-permute-start | bytes 1572872 | tf_op jit(solution)/shard_map/ppermute | solution.py:333
  121.5 6.6 %copy-start.9 = (bf16[2,4,256,128]{3,2,1,0:T(8,128)(2,1)S(1)}, bf16[2,4,256,128]{3,2,1,0:T(8,128)(2,1)}, u32[]{:S(2)}) copy-start(bf16[2,4,256,128]{3,2,1,0:T(8,128)(2,1)} %get-tuple-element.28) | copy-start | bytes 1572868
  121.5 11.3 %collective-permute-start.30 = (bf16[2,4,256,128]{3,2,1,0:T(8,128)(2,1)S(1)}, bf16[2,4,256,128]{3,2,1,0:T(8,128)(2,1)S(1)}, u32[]{:S(2)}, u32[]{:S(2)}) collective-permute-start(bf16[2,4,256,128]{3,2,1,0:T(8,128)(2,1)S(1)} %add_convert_fusion.1), channel_id=1, source_target_pairs={{0,4},{1,5},{2,6},{3,7},{4,8},{5,9},{6,10},{7,11},{8,12},{9,13},{1... | collective-permute-start | bytes 1572872 | tf_op jit(solution)/shard_map/ppermute | solution.py:333
  121.8 25.5 %collective-permute-start.25 = (bf16[2,4,256,128]{3,2,1,0:T(8,128)(2,1)}, bf16[2,4,256,128]{3,2,1,0:T(8,128)(2,1)S(1)}, u32[]{:S(2)}, u32[]{:S(2)}) collective-permute-start(bf16[2,4,256,128]{3,2,1,0:T(8,128)(2,1)} %get-tuple-element.33), channel_id=1, source_target_pairs={{0,16},{16,0},{32,48},{48,32},{64,80},{80,64},{96,112},{112,96},{1... | collective-permute-start | bytes 1572872 | tf_op jit(solution)/shard_map/ppermute | solution.py:414
  128.1 12.4 %collective-permute-start.19 = (bf16[2,4,256,128]{3,2,1,0:T(8,128)(2,1)S(1)}, bf16[2,4,256,128]{3,2,1,0:T(8,128)(2,1)}, u32[]{:S(2)}, u32[]{:S(2)}) collective-permute-start(bf16[2,4,256,128]{3,2,1,0:T(8,128)(2,1)S(1)} %add_convert_fusion.5), channel_id=1, source_target_pairs={{0,4},{1,5},{2,6},{3,7},{4,8},{5,9},{6,10},{7,11},{8,12},{9,13},{1... | collective-permute-start | bytes 1572872 | tf_op jit(solution)/shard_map/ppermute | solution.py:333
  128.1 6.7 %copy-start.8 = (bf16[2,4,256,128]{3,2,1,0:T(8,128)(2,1)S(1)}, bf16[2,4,256,128]{3,2,1,0:T(8,128)(2,1)}, u32[]{:S(2)}) copy-start(bf16[2,4,256,128]{3,2,1,0:T(8,128)(2,1)} %get-tuple-element.36) | copy-start | bytes 1572868
  129.1 18.2 %collective-permute-start.27 = (bf16[2,4,256,128]{3,2,1,0:T(8,128)(2,1)S(1)}, bf16[2,4,256,128]{3,2,1,0:T(8,128)(2,1)S(1)}, u32[]{:S(2)}, u32[]{:S(2)}) collective-permute-start(bf16[2,4,256,128]{3,2,1,0:T(8,128)(2,1)S(1)} %add_convert_fusion.2), channel_id=1, source_target_pairs={{0,12},{1,13},{2,14},{3,15},{4,0},{5,1},{6,2},{7,3},{8,4},{9,5},{1... | collective-permute-start | bytes 1572872 | tf_op jit(solution)/shard_map/ppermute | solution.py:333
  132.8 12.4 %collective-permute-start.23 = (bf16[2,4,256,128]{3,2,1,0:T(8,128)(2,1)}, bf16[2,4,256,128]{3,2,1,0:T(8,128)(2,1)}, u32[]{:S(2)}, u32[]{:S(2)}) collective-permute-start(bf16[2,4,256,128]{3,2,1,0:T(8,128)(2,1)} %add_convert_fusion.3), channel_id=1, source_target_pairs={{0,12},{1,13},{2,14},{3,15},{4,0},{5,1},{6,2},{7,3},{8,4},{9,5},{1... | collective-permute-start | bytes 1572872 | tf_op jit(solution)/shard_map/ppermute | solution.py:333
  134.8 1.0 copy-start.12
  134.8 1.1 copy-start.13
  135.8 11.5 %collective-permute-start.31 = (bf16[2,4,256,128]{3,2,1,0:T(8,128)(2,1)}, bf16[2,4,256,128]{3,2,1,0:T(8,128)(2,1)S(1)}, u32[]{:S(2)}, u32[]{:S(2)}) collective-permute-start(bf16[2,4,256,128]{3,2,1,0:T(8,128)(2,1)} %add_convert_fusion), channel_id=1, source_target_pairs={{0,4},{1,5},{2,6},{3,7},{4,8},{5,9},{6,10},{7,11},{8,12},{9,13},{1... | collective-permute-start | bytes 1572872 | tf_op jit(solution)/shard_map/ppermute | solution.py:333
  136.9 15.1 %all-to-all-start.2 = ((bf16[4,128,768]{2,1,0:T(8,128)(2,1)}), bf16[4,128,768]{2,1,0:T(8,128)(2,1)S(1)}, u32[]{:S(2)}, u32[]{:S(2)}) async-start(bf16[4,128,768]{2,1,0:T(8,128)(2,1)} %pad_maximum_fusion.1), calls=%async_computation.2 | async-start | bytes 1572864 | tf_op jit(solution)/shard_map/all_to_all | solution.py:375
  140.4 6.8 %copy-start.1 = (bf16[2,4,256,128]{3,2,1,0:T(8,128)(2,1)S(1)}, bf16[2,4,256,128]{3,2,1,0:T(8,128)(2,1)}, u32[]{:S(2)}) copy-start(bf16[2,4,256,128]{3,2,1,0:T(8,128)(2,1)} %get-tuple-element.32) | copy-start | bytes 1572868
  147.3 6.7 %collective-permute-start.24 = (bf16[4,256,128]{2,1,0:T(8,128)(2,1)}, bf16[4,256,128]{2,1,0:T(8,128)(2,1)}, u32[]{:S(2)}, u32[]{:S(2)}) collective-permute-start(bf16[4,256,128]{2,1,0:T(8,128)(2,1)} %fusion.5), channel_id=1, source_target_pairs={{0,3},{1,0},{2,1},{3,2},{4,7},{5,4},{6,5},{7,6},{8,11},{9,8},{10,9... | collective-permute-start | bytes 786440 | tf_op jit(solution)/shard_map/ppermute | solution.py:333
  148.3 7.8 %collective-permute-start.32 = (bf16[4,256,128]{2,1,0:T(8,128)(2,1)}, bf16[4,256,128]{2,1,0:T(8,128)(2,1)S(1)}, u32[]{:S(2)}, u32[]{:S(2)}) collective-permute-start(bf16[4,256,128]{2,1,0:T(8,128)(2,1)} %get-tuple-element.44), channel_id=1, source_target_pairs={{0,1},{1,2},{2,3},{3,0},{4,5},{5,6},{6,7},{7,4},{8,9},{9,10},{10,1... | collective-permute-start | bytes 786440 | tf_op jit(solution)/shard_map/ppermute | solution.py:333
  150.3 9.1 %copy-start.7 = (bf16[2,4,256,128]{3,2,1,0:T(8,128)(2,1)S(1)}, bf16[2,4,256,128]{3,2,1,0:T(8,128)(2,1)}, u32[]{:S(2)}) copy-start(bf16[2,4,256,128]{3,2,1,0:T(8,128)(2,1)} %get-tuple-element.24) | copy-start | bytes 1572868
  150.3 9.1 %collective-permute-start.33 = (bf16[4,256,128]{2,1,0:T(8,128)(2,1)S(1)}, bf16[4,256,128]{2,1,0:T(8,128)(2,1)S(1)}, u32[]{:S(2)}, u32[]{:S(2)}) collective-permute-start(bf16[4,256,128]{2,1,0:T(8,128)(2,1)S(1)} %get-tuple-element.45), channel_id=1, source_target_pairs={{0,2},{1,3},{2,0},{3,1},{4,6},{5,7},{6,4},{7,5},{8,10},{9,11},{10,... | collective-permute-start | bytes 786440 | tf_op jit(solution)/shard_map/ppermute | solution.py:333
  161.5 10.1 %all-to-all-start.3 = ((bf16[4,256,128]{2,1,0:T(8,128)(2,1)}), bf16[4,256,128]{2,1,0:T(8,128)(2,1)S(1)}, u32[]{:S(2)}, u32[]{:S(2)}) async-start(bf16[4,256,128]{2,1,0:T(8,128)(2,1)} %fusion.2), calls=%async_computation.3 | async-start | bytes 524288 | tf_op jit(solution)/shard_map/all_to_all | solution.py:375
